TPU v7x, 32 devices: a whole 2x2x4 slice. The times are simulated.
32 devices in a mesh: shard: 4 (over z), ctx: 2 (over core), tp: 4 (over y, x).
Axes of the slice: x: 2, y: 2, z: 4, core: 2. Of those that a mesh axis runs over, the one named last changes fastest.
Arguments:
- tokens: bfloat16 [16384, 896], P(('shard', 'ctx', 'tp')), may hold values from -6 to 6
- doc_ids: int32 [16, 1024], P(('shard', 'tp')), may hold values from -1 to 7, as said below
- w_query: bfloat16 [896, 896], P(('shard', 'ctx')), may hold values from -0.1875 to 0.1875
- b_query: bfloat16 [896], P(('shard', 'ctx')), may hold values from -3 to 3
- key_projection: bfloat16 [896, 128], P(('shard', 'ctx')), may hold values from -0.1875 to 0.1875
- key_bias_vector: bfloat16 [128], P(('shard', 'ctx')), may hold values from -3 to 3
- value_projection: bfloat16 [896, 128], P(('shard', 'ctx')), may hold values from -0.1875 to 0.1875
- value_bias_vector: bfloat16 [128], P(('shard', 'ctx')), may hold values from -3 to 3
- w_output: bfloat16 [896, 896], P(('shard', 'ctx')), may hold values from -1.5 to 1.5
- gain_attn: bfloat16 [896], P(('shard', 'ctx')), may hold values from 0.5 to 1.5
- gain_mlp: bfloat16 [896], P(('shard', 'ctx')), may hold values from 0.5 to 1.5
- w_gate: bfloat16 [896, 4864], P(('shard', 'ctx'), 'tp'), may hold values from -0.1875 to 0.1875
- w_up: bfloat16 [896, 4864], P(('shard', 'ctx'), 'tp'), may hold values from -0.1875 to 0.1875
- w_down: bfloat16 [4864, 896], P('tp', ('shard', 'ctx')), may hold values from -0.078125 to 0.078125
- cotangent: bfloat16 [16384, 896], P(('shard', 'ctx', 'tp')), may hold values from -6 to 6
Outputs:
- output: bfloat16 [16384, 896], P(('shard', 'ctx', 'tp'))
- grad_tokens: bfloat16 [16384, 896], P(('shard', 'ctx', 'tp'))
- grad_w_query: float32 [896, 896], P(('shard', 'ctx'))
- grad_b_query: float32 [896], P(('shard', 'ctx'))
- grad_w_key: float32 [896, 128], P(('shard', 'ctx'))
- grad_b_key: float32 [128], P(('shard', 'ctx'))
- grad_w_value: float32 [896, 128], P(('shard', 'ctx'))
- grad_b_value: float32 [128], P(('shard', 'ctx'))
- grad_w_output: float32 [896, 896], P(('shard', 'ctx'))
- grad_gain_attn: float32 [896], P(('shard', 'ctx'))
- grad_gain_mlp: float32 [896], P(('shard', 'ctx'))
- grad_w_gate: float32 [896, 4864], P(('shard', 'ctx'), 'tp')
- grad_w_up: float32 [896, 4864], P(('shard', 'ctx'), 'tp')
- grad_w_down: float32 [4864, 896], P('tp', ('shard', 'ctx'))
Inputs may be any that keep to these rules, and one draw needn't show every extreme that they name: `doc_ids`: documents begin at multiples of 128 within a buffer, are numbered 0, 1, 2 in order in each buffer, and only the rest of a document's last block of 128 slots is padding (-1).
All inputs are finite; a program needn't handle non-finite values.
Results may differ from a plain program's by a relative error of at most 0.02.
Values may be sent and summed in bfloat16 or wider, within the bound.
No kernel may reach another device: no remote copies, remote signals or barrier semaphores. Data moves between devices by JAX's collectives and lax.ppermute only.
A program may use at most 192 MiB of HBM per device.

v0:
```python
import jax
import jax.numpy as jnp
from jax import lax
from jax.sharding import PartitionSpec as P

QUERY_HEADS = 14
KEY_VALUE_HEADS = 2
HEAD_WIDTH = 64


EPSILON = 1e-06
THETA = 1000000.0
NEGATIVE = -1e30


def matmul(left_side, right_side):
    return jnp.dot(left_side, right_side, preferred_element_type=jnp.float32)


def times_transpose(left_side, right_side):
    return lax.dot_general(
        left_side, right_side, (((1,), (1,)), ((), ())), preferred_element_type=jnp.float32
    )


def transpose_times(left_side, right_side):
    return lax.dot_general(
        left_side, right_side, (((0,), (0,)), ((), ())), preferred_element_type=jnp.float32
    )


def rotation(positions, head_size):
    half_dim = head_size // 2
    frequency = THETA ** (-(jnp.arange(half_dim, dtype=jnp.float32) * 2.0) / head_size)
    angles = positions.astype(jnp.float32)[:, None] * frequency[None, :]
    return (jnp.cos(angles), jnp.sin(angles))


def apply_rotary(values, cosine_table, sine_table):
    half_dim = values.shape[-1] // 2
    first_half = values[..., :half_dim]
    second_half = values[..., half_dim:]
    cosine_table = cosine_table[:, None, :]
    sine_table = sine_table[:, None, :]
    return jnp.concatenate(
        [
            first_half * cosine_table - second_half * sine_table,
            second_half * cosine_table + first_half * sine_table,
        ],
        -1,
    )


def unrotate(values, cosine_table, sine_table):
    half_dim = values.shape[-1] // 2
    first_half = values[..., :half_dim]
    second_half = values[..., half_dim:]
    cosine_table = cosine_table[:, None, :]
    sine_table = sine_table[:, None, :]
    return jnp.concatenate(
        [
            first_half * cosine_table + second_half * sine_table,
            second_half * cosine_table - first_half * sine_table,
        ],
        -1,
    )


def attention_mask(doc_row):
    places = jnp.arange(doc_row.shape[0], dtype=jnp.int32)
    same_doc = (
        (doc_row[:, None] == doc_row[None, :])
        & (doc_row[:, None] >= 0)
        & (places[None, :] <= places[:, None])
    )
    return same_doc | (places[:, None] == places[None, :])


def scores_of(query_grouped, key_three, key_mask, score_scale):
    raw_scores = (
        jnp.einsum("qkgd,skd->kgqs", query_grouped, key_three, preferred_element_type=jnp.float32)
        * score_scale
    )
    return jnp.where(key_mask[None, None], raw_scores, NEGATIVE)


def per_device(
    tokens,
    doc_ids,
    w_query,
    b_query,
    key_projection,
    key_bias_vector,
    value_projection,
    value_bias_vector,
    w_output,
    gain_attn,
    gain_mlp,
    w_gate,
    w_up,
    w_down,
    cotangent,
):
    token_count_total = tokens.shape[0]
    context_splits_count = lax.axis_size("ctx")
    local_heads = QUERY_HEADS // context_splits_count
    local_key_value = KEY_VALUE_HEADS // context_splits_count
    queries_per_group = QUERY_HEADS // KEY_VALUE_HEADS
    score_scale = HEAD_WIDTH ** (-0.5)

    def attn_gather():
        return (
            lax.all_gather(w_query, ("shard", "ctx"), axis=0, tiled=True),
            lax.all_gather(b_query, ("shard", "ctx"), axis=0, tiled=True),
            lax.all_gather(key_projection, ("shard", "ctx"), axis=0, tiled=True),
            lax.all_gather(key_bias_vector, ("shard", "ctx"), axis=0, tiled=True),
            lax.all_gather(value_projection, ("shard", "ctx"), axis=0, tiled=True),
            lax.all_gather(value_bias_vector, ("shard", "ctx"), axis=0, tiled=True),
            lax.all_gather(w_output, ("shard", "ctx"), axis=0, tiled=True),
            lax.all_gather(gain_attn, ("shard", "ctx"), axis=0, tiled=True),
            lax.all_gather(gain_mlp, ("shard", "ctx"), axis=0, tiled=True),
        )

    def mlp_gather():
        return (
            lax.all_gather(w_gate, ("shard", "ctx"), axis=0, tiled=True),
            lax.all_gather(w_up, ("shard", "ctx"), axis=0, tiled=True),
            lax.all_gather(w_down, ("shard", "ctx"), axis=1, tiled=True),
        )

    (
        query_weight,
        query_bias,
        key_weight,
        key_bias,
        value_weight,
        value_bias,
        output_weight,
        first_gain,
        second_gain,
    ) = attn_gather()
    first_gain_f = first_gain.astype(jnp.float32)
    second_gain_f = second_gain.astype(jnp.float32)
    tok_float = tokens.astype(jnp.float32)
    first_inv = lax.rsqrt(jnp.mean(tok_float * tok_float, -1, keepdims=True) + EPSILON)
    normed_attn = (tok_float * first_inv * first_gain_f).astype(jnp.bfloat16)
    positions = lax.axis_index("ctx") * token_count_total + jnp.arange(
        token_count_total, dtype=jnp.int32
    )
    cosine_table, sine_table = rotation(positions, HEAD_WIDTH)
    query_pre = (matmul(normed_attn, query_weight) + query_bias.astype(jnp.float32)).reshape(
        token_count_total, QUERY_HEADS, HEAD_WIDTH
    )
    key_before_rotary = (matmul(normed_attn, key_weight) + key_bias.astype(jnp.float32)).reshape(
        token_count_total, KEY_VALUE_HEADS, HEAD_WIDTH
    )
    value_pre = matmul(normed_attn, value_weight) + value_bias.astype(jnp.float32)
    query_send = (
        apply_rotary(query_pre, cosine_table, sine_table)
        .reshape(token_count_total, QUERY_HEADS * HEAD_WIDTH)
        .astype(jnp.bfloat16)
    )
    key_send = (
        apply_rotary(key_before_rotary, cosine_table, sine_table)
        .reshape(token_count_total, KEY_VALUE_HEADS * HEAD_WIDTH)
        .astype(jnp.bfloat16)
    )
    value_send = value_pre.astype(jnp.bfloat16)
    query_heads, key_heads, value_heads = (
        lax.all_to_all(query_send, "ctx", split_axis=1, concat_axis=0, tiled=True),
        lax.all_to_all(key_send, "ctx", split_axis=1, concat_axis=0, tiled=True),
        lax.all_to_all(value_send, "ctx", split_axis=1, concat_axis=0, tiled=True),
    )
    pair_span = query_heads.shape[0]
    query_grouped = query_heads.reshape(pair_span, local_key_value, queries_per_group, HEAD_WIDTH)
    key_three = key_heads.reshape(pair_span, local_key_value, HEAD_WIDTH)
    value_three = value_heads.reshape(pair_span, local_key_value, HEAD_WIDTH)
    key_mask = attention_mask(doc_ids[0])
    scores = scores_of(query_grouped, key_three, key_mask, score_scale)
    row_max = jnp.max(scores, -1, keepdims=True)
    exponent = jnp.exp(scores - row_max)
    totals = jnp.sum(exponent, -1, keepdims=True)
    attn_probs = exponent / totals
    log_total = row_max + jnp.log(totals)
    mixed_heads = jnp.einsum(
        "kgqs,skd->qkgd",
        attn_probs.astype(jnp.bfloat16),
        value_three,
        preferred_element_type=jnp.float32,
    )
    mixed_heads = mixed_heads.reshape(pair_span, local_heads * HEAD_WIDTH).astype(jnp.bfloat16)
    mixed_rows = lax.all_to_all(mixed_heads, "ctx", split_axis=0, concat_axis=1, tiled=True)
    hidden = tok_float + matmul(mixed_rows, output_weight)
    second_inv = lax.rsqrt(jnp.mean(hidden * hidden, -1, keepdims=True) + EPSILON)
    normed_mlp = (hidden * second_inv * second_gain_f).astype(jnp.bfloat16)
    mlp_rows = lax.all_gather(normed_mlp, "tp", axis=0, tiled=True)
    gate_weight_full, up_weight_full, down_weight_full = mlp_gather()
    gate_pre = matmul(mlp_rows, gate_weight_full)
    up_pre = matmul(mlp_rows, up_weight_full)
    sigmoid_gate = jax.nn.sigmoid(gate_pre)
    silu_gate = gate_pre * sigmoid_gate
    activation = (silu_gate * up_pre).astype(jnp.bfloat16)
    down_rows = lax.psum_scatter(
        matmul(activation, down_weight_full).astype(jnp.bfloat16),
        "tp",
        scatter_dimension=0,
        tiled=True,
    ).astype(jnp.float32)
    result = hidden + down_rows
    grad_out = cotangent.astype(jnp.float32)
    grad_rows = lax.all_gather(cotangent, "tp", axis=0, tiled=True)
    gate_again, up_again, down_again = mlp_gather()
    grad_activ = times_transpose(grad_rows, down_again)
    grad_gate = (
        grad_activ * up_pre * sigmoid_gate * (1.0 + gate_pre * (1.0 - sigmoid_gate))
    ).astype(jnp.bfloat16)
    grad_up = (grad_activ * silu_gate).astype(jnp.bfloat16)
    grad_normed_mlp = lax.psum_scatter(
        times_transpose(grad_gate, gate_again) + times_transpose(grad_up, up_again),
        "tp",
        scatter_dimension=0,
        tiled=True,
    )
    grad_gate_weight = transpose_times(mlp_rows, grad_gate)
    grad_up_weight = transpose_times(mlp_rows, grad_up)
    grad_down_weight = transpose_times(activation, grad_rows)
    part_gate, part_up, part_down = (
        lax.psum_scatter(grad_gate_weight, ("shard", "ctx"), scatter_dimension=0, tiled=True),
        lax.psum_scatter(grad_up_weight, ("shard", "ctx"), scatter_dimension=0, tiled=True),
        lax.psum_scatter(grad_down_weight, ("shard", "ctx"), scatter_dimension=1, tiled=True),
    )
    scaled_two = grad_normed_mlp * second_gain_f
    grad_hidden = (
        grad_out
        + second_inv * scaled_two
        - hidden * second_inv**3 * jnp.mean(scaled_two * hidden, -1, keepdims=True)
    )
    grad_second_gain = jnp.sum(grad_normed_mlp * hidden * second_inv, 0)
    (
        query_weight,
        query_bias,
        key_weight,
        key_bias,
        value_weight,
        value_bias,
        output_weight,
        first_gain,
        second_gain,
    ) = attn_gather()
    grad_branch = grad_hidden.astype(jnp.bfloat16)
    grad_mixed = times_transpose(grad_branch, output_weight).astype(jnp.bfloat16)
    grad_output_weight = transpose_times(mixed_rows, grad_branch)
    grad_heads = lax.all_to_all(grad_mixed, "ctx", split_axis=1, concat_axis=0, tiled=True)
    grad_four = grad_heads.reshape(pair_span, local_key_value, queries_per_group, HEAD_WIDTH)
    scores_again = scores_of(query_grouped, key_three, key_mask, score_scale)
    probs_again = jnp.exp(scores_again - log_total)
    grad_probs = jnp.einsum(
        "qkgd,skd->kgqs", grad_four, value_three, preferred_element_type=jnp.float32
    )
    delta_rows = jnp.sum(probs_again * grad_probs, -1, keepdims=True)
    grad_scores = (probs_again * (grad_probs - delta_rows)).astype(jnp.bfloat16)
    grad_query = (
        jnp.einsum("kgqs,skd->qkgd", grad_scores, key_three, preferred_element_type=jnp.float32)
        * score_scale
    )
    grad_query = grad_query.reshape(pair_span, local_heads * HEAD_WIDTH).astype(jnp.bfloat16)
    grad_key = (
        jnp.einsum("kgqs,qkgd->skd", grad_scores, query_grouped, preferred_element_type=jnp.float32)
        * score_scale
    )
    grad_key = grad_key.reshape(pair_span, local_key_value * HEAD_WIDTH).astype(jnp.bfloat16)
    grad_value = jnp.einsum(
        "kgqs,qkgd->skd",
        probs_again.astype(jnp.bfloat16),
        grad_four,
        preferred_element_type=jnp.float32,
    )
    grad_value = grad_value.reshape(pair_span, local_key_value * HEAD_WIDTH).astype(jnp.bfloat16)
    query_back, key_gradient_rows, value_back = (
        lax.all_to_all(grad_query, "ctx", split_axis=0, concat_axis=1, tiled=True),
        lax.all_to_all(grad_key, "ctx", split_axis=0, concat_axis=1, tiled=True),
        lax.all_to_all(grad_value, "ctx", split_axis=0, concat_axis=1, tiled=True),
    )
    grad_query_pre = unrotate(
        query_back.astype(jnp.float32).reshape(token_count_total, QUERY_HEADS, HEAD_WIDTH),
        cosine_table,
        sine_table,
    ).reshape(token_count_total, QUERY_HEADS * HEAD_WIDTH)
    grad_key_pre = unrotate(
        key_gradient_rows.astype(jnp.float32).reshape(
            token_count_total, KEY_VALUE_HEADS, HEAD_WIDTH
        ),
        cosine_table,
        sine_table,
    ).reshape(token_count_total, KEY_VALUE_HEADS * HEAD_WIDTH)
    grad_query_bias = jnp.sum(grad_query_pre, 0)
    grad_key_bias = jnp.sum(grad_key_pre, 0)
    grad_value_bias = jnp.sum(value_back.astype(jnp.float32), 0)
    query_low = grad_query_pre.astype(jnp.bfloat16)
    key_low = grad_key_pre.astype(jnp.bfloat16)
    grad_normed_attn = (
        times_transpose(query_low, query_weight)
        + times_transpose(key_low, key_weight)
        + times_transpose(value_back, value_weight)
    )
    grad_query_weight = transpose_times(normed_attn, query_low)
    grad_key_weight = transpose_times(normed_attn, key_low)
    grad_value_weight = transpose_times(normed_attn, value_back)
    scaled_one = grad_normed_attn * first_gain_f
    grad_tokens = (
        grad_hidden
        + first_inv * scaled_one
        - tok_float * first_inv**3 * jnp.mean(scaled_one * tok_float, -1, keepdims=True)
    )
    grad_first_gain = jnp.sum(grad_normed_attn * tok_float * first_inv, 0)
    (
        shard_query_weight,
        shard_query_bias,
        shard_key_weight,
        shard_key_bias,
        shard_value_weight,
        shard_value_bias,
        shard_output_weight,
        shard_first_gain,
        shard_second_gain,
    ) = (
        lax.psum_scatter(grad_query_weight, ("shard", "ctx"), scatter_dimension=0, tiled=True),
        lax.psum_scatter(grad_query_bias, ("shard", "ctx"), scatter_dimension=0, tiled=True),
        lax.psum_scatter(grad_key_weight, ("shard", "ctx"), scatter_dimension=0, tiled=True),
        lax.psum_scatter(grad_key_bias, ("shard", "ctx"), scatter_dimension=0, tiled=True),
        lax.psum_scatter(grad_value_weight, ("shard", "ctx"), scatter_dimension=0, tiled=True),
        lax.psum_scatter(grad_value_bias, ("shard", "ctx"), scatter_dimension=0, tiled=True),
        lax.psum_scatter(grad_output_weight, ("shard", "ctx"), scatter_dimension=0, tiled=True),
        lax.psum_scatter(grad_first_gain, ("shard", "ctx"), scatter_dimension=0, tiled=True),
        lax.psum_scatter(grad_second_gain, ("shard", "ctx"), scatter_dimension=0, tiled=True),
    )
    (
        sum_query_weight,
        sum_query_bias,
        sum_key_weight,
        sum_key_bias,
        sum_value_weight,
        sum_value_bias,
        sum_output_weight,
        sum_first_gain,
        sum_second_gain,
    ) = lax.psum(
        (
            shard_query_weight,
            shard_query_bias,
            shard_key_weight,
            shard_key_bias,
            shard_value_weight,
            shard_value_bias,
            shard_output_weight,
            shard_first_gain,
            shard_second_gain,
        ),
        "tp",
    )
    return (
        result.astype(jnp.bfloat16),
        grad_tokens.astype(jnp.bfloat16),
        sum_query_weight,
        sum_query_bias,
        sum_key_weight,
        sum_key_bias,
        sum_value_weight,
        sum_value_bias,
        sum_output_weight,
        sum_first_gain,
        sum_second_gain,
        part_gate,
        part_up,
        part_down,
    )


def solution(mesh):
    in_specs = (
        P(("shard", "ctx", "tp"), None),
        P(("shard", "tp"), None),
        P(("shard", "ctx"), None),
        P(("shard", "ctx")),
        P(("shard", "ctx"), None),
        P(("shard", "ctx")),
        P(("shard", "ctx"), None),
        P(("shard", "ctx")),
        P(("shard", "ctx"), None),
        P(("shard", "ctx")),
        P(("shard", "ctx")),
        P(("shard", "ctx"), "tp"),
        P(("shard", "ctx"), "tp"),
        P("tp", ("shard", "ctx")),
        P(("shard", "ctx", "tp"), None),
    )
    out_specs = (
        P(("shard", "ctx", "tp"), None),
        P(("shard", "ctx", "tp"), None),
        P(("shard", "ctx"), None),
        P(("shard", "ctx")),
        P(("shard", "ctx"), None),
        P(("shard", "ctx")),
        P(("shard", "ctx"), None),
        P(("shard", "ctx")),
        P(("shard", "ctx"), None),
        P(("shard", "ctx")),
        P(("shard", "ctx")),
        P(("shard", "ctx"), "tp"),
        P(("shard", "ctx"), "tp"),
        P("tp", ("shard", "ctx")),
    )
    return jax.shard_map(
        per_device, mesh=mesh, in_specs=in_specs, out_specs=out_specs, check_vma=False
    )
```

profile of v0, /device:TPU:0, one launch (start us, length us, event | category | flops | bytes accessed | tf_op | source)
XLA Modules:
  0.0 968.9 jit_solution(9325236112312374507)
XLA Ops:
  15.6 19.6 %all-reduce.13 = (bf16[128]{0:T(256)(128)(2,1)S(1)}, bf16[896]{0:T(1024)(128)(2,1)S(1)}, bf16[128]{0:T(256)(128)(2,1)S(1)}, bf16[896]{0:T(1024)(128)(2,1)S(1)}, bf16[896]{0:T(1024)(128)(2,1)S(1)}) all-reduce(bf16[128]{0:T(256)(128)(2,1)S(1)} %dynamic-update-slice.1, ...), channel_id=1, replica_groups=mesh['shard'=4,'ctx'=2,'tp'=4] {'shard','ctx'}, use_global_device_ids=true, to_apply=%add.1 | all-reduce | flops 2944 | bytes 11776
  35.2 14.4 %all_gather.50 = bf16[896,128]{1,0:T(8,128)(2,1)S(1)} all-gather(bf16[112,128]{1,0:T(8,128)(2,1)} %param.21), channel_id=1, replica_groups=mesh['shard'=4,'ctx'=2,'tp'=4] {'shard','ctx'}, dimensions={0}, use_global_device_ids=true | all-gather | bytes 258048 | tf_op jit(solution)/shard_map/all_gather | solution.py:117
  49.6 1.5 fusion.15
  51.7 2.4 fusion.37
  54.1 3.4 all-to-all-start
  58.3 14.3 %all_gather.52 = bf16[896,128]{1,0:T(8,128)(2,1)S(1)} all-gather(bf16[112,128]{1,0:T(8,128)(2,1)S(1)} %copy-done.22), channel_id=1, replica_groups=mesh['shard'=4,'ctx'=2,'tp'=4] {'shard','ctx'}, dimensions={0}, use_global_device_ids=true | all-gather | bytes 258048 | tf_op jit(solution)/shard_map/all_gather | solution.py:115
  74.6 3.4 all-to-all-start.1
  79.7 2.9 fusion.14
  82.6 4.0 convolution_add_fusion.1
  86.6 1.8 copy.57
  88.8 5.0 all_to_all.110
  95.4 13.3 %fusion.61 = (f32[7,1024]{1,0:T(8,128)S(1)}, f32[1,7,1024,1024]{2,3,1,0:T(8,128)}) fusion(bf16[1024,64,1]{0,1,2:T(8,128)(2,1)S(1)} %reshape.386, bf16[1024,7,64]{0,2,1:T(8,128)(2,1)S(1)} %reshape.355, pred[1024,1024]{0,1:T(8,128)(4,1)} %fusion.14), kind=kOutput, calls=%fused_computation.103 | convolution fusion | flops 961537024 | bytes 31485952 | tf_op jit(solution)/shard_map/qkgd,skd->kgqs/dot_general | solution.py:81
  108.7 11.8 %fusion.3 = f32[7,1024]{1,0:T(8,128)S(1)} fusion(f32[1,7,1024,1024]{2,3,1,0:T(8,128)} %get-tuple-element.59, f32[7,1024]{1,0:T(8,128)S(1)} %get-tuple-element.58), kind=kLoop, calls=%fused_computation.9 | loop fusion | flops 14672896 | bytes 29417472 | tf_op jit(solution)/shard_map/reduce_sum | solution.py:182
  120.5 12.1 %fusion.30 = bf16[1024,1,7,64]{0,3,2,1:T(8,128)(2,1)S(1)} fusion(bf16[1024,64,1]{0,1,2:T(8,128)(2,1)S(1)} %reshape.387, f32[7,1024]{1,0:T(8,128)S(1)} %fusion.3, f32[1,7,1024,1024]{2,3,1,0:T(8,128)} %get-tuple-element.59, f32[7,1024]{1,0:T(8,128)S(1)} %get-tuple-element.58), kind=kOutput, calls=%fused_computation.58 | convolution fusion | flops 962002944 | bytes 30466048 | tf_op jit(solution)/shard_map/kgqs,skd->qkgd/dot_general | solution.py:185
  134.3 3.6 all-to-all-start.3
  138.0 1.9 all-to-all-done.3
  140.8 3.1 multiply_reduce_fusion.2
  147.5 44.4 %all-gather.12.cloned.1.call-done = bf16[2048,896]{1,0:T(8,128)(2,1)} async-done(((bf16[512,896]{1,0:T(8,128)(2,1)}), bf16[2048,896]{1,0:T(8,128)(2,1)}) %all-gather.12.cloned.1.call-update) | async-done | bytes 3670032 | tf_op jit(solution)/shard_map/all_gather | solution.py:196
  191.9 10.0 %fusion.63 = f32[2048,1216]{0,1:T(8,128)} fusion(bf16[2048,896]{1,0:T(8,128)(2,1)} %all-gather.12.cloned.1.call-done, bf16[896,1216]{1,0:T(8,128)(2,1)} %all-gather.16.cloned.1.call-done), kind=kOutput, calls=%fused_computation.105 | convolution fusion | flops 4462739456 | bytes 15810560 | tf_op jit(solution)/shard_map/dot_general | solution.py:17
  201.9 22.3 %all-gather.14.cloned.1.call-done = bf16[896,1216]{1,0:T(8,128)(2,1)} async-done(((bf16[112,1216]{1,0:T(8,128)(2,1)}), bf16[896,1216]{1,0:T(8,128)(2,1)}) %all-gather.14.cloned.1.call-update) | async-done | bytes 2179088 | tf_op jit(solution)/shard_map/all_gather | solution.py:126
  224.2 9.9 %fusion.62 = f32[2048,1216]{0,1:T(8,128)} fusion(bf16[2048,896]{1,0:T(8,128)(2,1)} %all-gather.12.cloned.1.call-done, bf16[896,1216]{1,0:T(8,128)(2,1)} %all-gather.14.cloned.1.call-done), kind=kOutput, calls=%fused_computation.104 | convolution fusion | flops 4462739456 | bytes 15810560 | tf_op jit(solution)/shard_map/dot_general | solution.py:17
  234.2 21.7 %all-gather.18.cloned.1.call-done = bf16[1216,896]{0,1:T(8,128)(2,1)} async-done(((bf16[1216,112]{0,1:T(8,128)(2,1)}), bf16[1216,896]{0,1:T(8,128)(2,1)}) %all-gather.18.cloned.1.call-update) | async-done | bytes 2179088 | tf_op jit(solution)/shard_map/all_gather | solution.py:128
  255.9 49.5 %all-gather.20.cloned.1.call-done = bf16[2048,896]{1,0:T(8,128)(2,1)} async-done(((bf16[512,896]{1,0:T(8,128)(2,1)}), bf16[2048,896]{1,0:T(8,128)(2,1)}) %all-gather.20.cloned.1.call-update) | async-done | bytes 3670032 | tf_op jit(solution)/shard_map/all_gather | solution.py:211
  305.4 19.3 %multiply_convert_fusion = (bf16[2048,1216]{0,1:T(8,128)(2,1)}, bf16[2048,1216]{0,1:T(8,128)(2,1)}, bf16[2048,1216]{0,1:T(8,128)(2,1)}) fusion(f32[2048,1216]{0,1:T(8,128)} %fusion.62, f32[2048,1216]{0,1:T(8,128)} %fusion.63, bf16[2048,896]{1,0:T(8,128)(2,1)} %all-gather.20.cloned.1.call-done, bf16[1216,896]{0,1:T(8,128)(2,1)} %all-gather.18.cloned.1.call-done), kind=kOutput, calls=%fused_computation.17 | convolution fusion | flops 4500094976 | bytes 40714240 | tf_op jit(solution)/shard_map/dot_general | solution.py:21
  324.7 8.7 fusion.64
  333.4 7.8 convolution_add_fusion
  341.2 9.6 convolution_convert_fusion
  350.9 69.2 %reduce-scatter.12.cloned.1.call-done = f32[512,896]{1,0:T(8,128)} async-done(((f32[2048,896]{1,0:T(8,128)}), f32[512,896]{1,0:T(8,128)}) %reduce-scatter.12.cloned.1.call-update) | async-done | bytes 1835024 | tf_op jit(solution)/shard_map/reduce_scatter | solution.py:218
  420.1 2.0 multiply_reduce_fusion
  422.1 49.3 %reduce-scatter.10.cloned.1.call-done = bf16[512,896]{1,0:T(8,128)(2,1)} async-done(((bf16[2048,896]{1,0:T(8,128)(2,1)}), bf16[512,896]{1,0:T(8,128)(2,1)}) %reduce-scatter.10.cloned.1.call-update) | async-done | bytes 917520 | tf_op jit(solution)/shard_map/reduce_scatter | solution.py:203
  471.4 4.2 multiply_subtract_fusion
  475.6 2.2 convolution_convert_fusion.1
  477.8 2.2 copy.61
  480.0 6.0 all_to_all.111
  486.0 1.9 copy.62
  487.9 3.5 reshape.357
  491.4 14.2 %fusion.42 = bf16[1024,1,64]{0,2,1:T(8,128)(2,1)S(1)} fusion(bf16[1024,7,64]{0,2,1:T(8,128)(2,1)} %reshape.357, f32[1,7,1024,1024]{2,3,1,0:T(8,128)} %get-tuple-element.59, f32[7,1024]{1,0:T(8,128)S(1)} %log_add_fusion), kind=kOutput, calls=%fused_computation.67 | convolution fusion | flops 954269696 | bytes 30437376 | tf_op jit(solution)/shard_map/kgqs,qkgd->skd/dot_general | solution.py:272
  505.6 18.5 %fusion = (f32[7,1024]{1,0:T(8,128)S(1)}, f32[1024,1024,7]{1,0,2:T(8,128)}) fusion(f32[1,7,1024,1024]{2,3,1,0:T(8,128)} %get-tuple-element.59, f32[7,1024]{1,0:T(8,128)S(1)} %log_add_fusion, bf16[1024,64,1]{0,1,2:T(8,128)(2,1)S(1)} %reshape.387, bf16[1024,7,64]{0,2,1:T(8,128)(2,1)} %reshape.357), kind=kOutput, calls=%fused_computation.3 | convolution fusion | flops 961537024 | bytes 59826176 | tf_op jit(solution)/shard_map/qkgd,skd->kgqs/dot_general | solution.py:257
  524.2 3.8 all_to_all.112
  529.5 25.3 %fusion.8 = bf16[7,1024,1024]{1,2,0:T(8,128)(2,1)} fusion(f32[1024,1024,7]{1,0,2:T(8,128)} %get-tuple-element.63, f32[1,7,1024,1024]{2,3,1,0:T(8,128)} %get-tuple-element.59, f32[7,1024]{1,0:T(8,128)S(1)} %get-tuple-element.62, f32[7,1024]{1,0:T(8,128)S(1)} %log_add_fusion), kind=kLoop, calls=%fused_computation.13 | loop fusion | flops 29360128 | bytes 73457664 | tf_op jit(solution)/shard_map/reshape.35
  554.8 10.1 %fusion.45 = bf16[1024,1,64]{0,2,1:T(8,128)(2,1)S(1)} fusion(bf16[1024,7,64]{0,2,1:T(8,128)(2,1)} %copy-done.2, bf16[7,1024,1024]{1,2,0:T(8,128)(2,1)} %fusion.8), kind=kOutput, calls=%fused_computation.68 | convolution fusion | flops 939655168 | bytes 15728640 | tf_op jit(solution)/shard_map/kgqs,qkgd->skd/dot_general | solution.py:268
  565.0 3.8 all_to_all.113
  570.3 3.9 fusion.46
  575.1 8.8 fusion.29
  584.0 3.5 convert_element_type.194
  588.8 4.5 all_to_all.114
  596.1 3.0 fusion.55
  599.3 10.7 %fusion.69 = f32[1216,896]{0,1:T(8,128)} fusion(bf16[2048,1216]{0,1:T(8,128)(2,1)} %get-tuple-element.39, bf16[2048,896]{1,0:T(8,128)(2,1)} %all-gather.20.cloned.1.call-done), kind=kOutput, calls=%fused_computation.111 | convolution fusion | flops 4462739456 | bytes 13008896 | tf_op jit(solution)/shard_map/dot_general | solution.py:27
  610.1 10.6 %fusion.68 = f32[896,1216]{1,0:T(8,128)} fusion(bf16[2048,896]{1,0:T(8,128)(2,1)} %all-gather.12.cloned.1.call-done, bf16[2048,1216]{0,1:T(8,128)(2,1)} %get-tuple-element.37), kind=kOutput, calls=%fused_computation.110 | convolution fusion | flops 4462739456 | bytes 13008896 | tf_op jit(solution)/shard_map/dot_general | solution.py:27
  621.0 10.8 %fusion.67 = f32[896,1216]{1,0:T(8,128)} fusion(bf16[2048,896]{1,0:T(8,128)(2,1)} %all-gather.12.cloned.1.call-done, bf16[2048,1216]{0,1:T(8,128)(2,1)} %get-tuple-element.38), kind=kOutput, calls=%fused_computation.109 | convolution fusion | flops 4462739456 | bytes 13008896 | tf_op jit(solution)/shard_map/dot_general | solution.py:27
  633.6 1.7 fusion.24
  635.8 3.0 fusion.65
  638.8 2.1 fusion.23
  640.9 29.8 %all-reduce.10 = (f32[896]{0:T(1024)S(1)}, f32[128]{0:T(128)S(1)}, f32[128]{0:T(128)S(1)}, f32[896]{0:T(1024)S(1)}, f32[896]{0:T(1024)S(1)}) all-reduce(f32[896]{0:T(1024)S(1)} %reduce_sum.112, f32[128]{0:T(128)S(1)} %reduce_sum.114, f32[128]{0:T(128)S(1)} %reduce_sum.116, ...), channel_id=5, replica_groups=mesh['shard'=4,'ctx'=2,'tp'=4] {'shard','ctx'}, use_global_device_ids=true, to_apply=%region_12.13.clone | all-reduce | flops 2944 | bytes 23552
  673.7 11.2 %reduce-scatter.14.cloned.1.call-done = f32[112,896]{1,0:T(8,128)} async-done(((f32[896,896]{1,0:T(8,128)}), f32[112,896]{1,0:T(8,128)}) %reduce-scatter.14.cloned.1.call-update) | async-done | bytes 401424 | tf_op jit(solution)/shard_map/reduce_scatter | solution.py:327
  684.9 2.9 fusion.20
  687.9 52.4 %reduce-scatter.26.cloned.1.call-done = f32[1216,112]{0,1:T(8,128)} async-done(((f32[1216,896]{0,1:T(8,128)}), f32[1216,112]{0,1:T(8,128)}) %reduce-scatter.26.cloned.1.call-update) | async-done | bytes 544784 | tf_op jit(solution)/shard_map/reduce_scatter | solution.py:230
  740.3 54.9 %reduce-scatter.24.cloned.1.call-done = f32[112,1216]{1,0:T(8,128)} async-done(((f32[896,1216]{1,0:T(8,128)}), f32[112,1216]{1,0:T(8,128)}) %reduce-scatter.24.cloned.1.call-update) | async-done | bytes 544784 | tf_op jit(solution)/shard_map/reduce_scatter | solution.py:229
  795.2 54.9 %reduce-scatter.22.cloned.1.call-done = f32[112,1216]{1,0:T(8,128)} async-done(((f32[896,1216]{1,0:T(8,128)}), f32[112,1216]{1,0:T(8,128)}) %reduce-scatter.22.cloned.1.call-update) | async-done | bytes 544784 | tf_op jit(solution)/shard_map/reduce_scatter | solution.py:228
  850.1 47.1 %all-reduce.17.cloned.1.call-done = (f32[112]{0:T(128)}, f32[112,128]{1,0:T(8,128)}, f32[16]{0:T(128)}, f32[112,128]{1,0:T(8,128)}, f32[16]{0:T(128)}, /*index=5*/f32[112]{0:T(128)}, f32[112]{0:T(128)}) async-done(((f32[112]{0:T(128)}, f32[112,128]{1,0:T(8,128)}, f32[16]{0:T(128)}, f32[112,128]{1,0:T(8,128)}, f32[16]{0:T(128)}, /*index=5*/f32[112]{0:T(128)}, f32[112]{0:T(128)}), (f32[112]{0:T(128)}, ...) | async-done | bytes 116176 | tf_op jit(solution)/shard_map/psum | solution.py:347
  897.2 52.1 %all-reduce.19.cloned.1.call-done = (f32[112,896]{1,0:T(8,128)}, f32[112,896]{1,0:T(8,128)}) async-done(((f32[112,896]{1,0:T(8,128)}, f32[112,896]{1,0:T(8,128)}), (f32[112,896]{1,0:T(8,128)}, f32[112,896]{1,0:T(8,128)})) %all-reduce.19.cloned.1.call-update) | async-done | bytes 802832 | tf_op jit(solution)/shard_map/psum | solution.py:347
  949.4 1.8 copy.87
  954.9 1.4 copy.91
  957.5 1.8 copy.93
  (167 shorter events, 40.1 us)
Async XLA Ops:
  7.2 66.2 %copy-start.1 = (bf16[512,896]{1,0:T(8,128)(2,1)S(1)}, bf16[512,896]{1,0:T(8,128)(2,1)}, u32[]{:S(2)}) copy-start(bf16[512,896]{1,0:T(8,128)(2,1)} %param.15) | copy-start | bytes 2752516
  7.2 51.0 %copy-start.19 = (s32[1,1024]{1,0:T(1,128)S(1)}, s32[1,1024]{1,0:T(1,128)}, u32[]{:S(2)}) copy-start(s32[1,1024]{1,0:T(1,128)} %param.16) | copy-start | bytes 12292
  7.2 51.1 %copy-start.22 = (bf16[112,128]{1,0:T(8,128)(2,1)S(1)}, bf16[112,128]{1,0:T(8,128)(2,1)}, u32[]{:S(2)}) copy-start(bf16[112,128]{1,0:T(8,128)(2,1)} %param.19) | copy-start | bytes 86020
  7.2 75.4 %all-gather.8.cloned.1.call-start = ((), (), s32[]{:S(2)}) async-start(), calls=%async_computation.17 | async-start | bytes 1806336 | tf_op jit(solution)/shard_map/all_gather | solution.py:113
  7.9 130.0 %all-gather.10.cloned.1.call-start = ((), (), s32[]{:S(2)}) async-start(), calls=%async_computation.18 | async-start | bytes 1806336 | tf_op jit(solution)/shard_map/all_gather | solution.py:119
  35.2 47.4 %copy-start.17 = (f32[896]{0:T(1024)}, f32[896]{0:T(1024)S(1)}, u32[]{:S(2)}) copy-start(f32[896]{0:T(1024)S(1)} %convert_element_type.166) | copy-start | bytes 10756
  49.6 2.1 copy-start.15
  51.7 30.9 %copy-start.20 = (f32[512]{0:T(512)}, f32[512]{0:T(512)S(1)}, u32[]{:S(2)}) copy-start(f32[512]{0:T(512)S(1)} %get-tuple-element.53) | copy-start | bytes 6148
  54.1 20.5 %all-to-all-start = ((bf16[512,2,64]{0,2,1:T(8,128)(2,1)}), bf16[512,2,64]{0,2,1:T(8,128)(2,1)S(1)}, u32[]{:S(2)}, u32[]{:S(2)}) async-start(bf16[512,2,64]{0,2,1:T(8,128)(2,1)} %bitcast.2), calls=%async_computation | async-start | bytes 262144 | tf_op jit(solution)/shard_map/all_to_all | solution.py:172
  57.5 90.0 %all-gather.16.cloned.1.call-start = ((), (), s32[]{:S(2)}) async-start(), calls=%async_computation.21 | async-start | bytes 2580480 | tf_op jit(solution)/shard_map/all_gather | solution.py:127
  72.7 0.7 copy-start.13
  73.3 15.0 %copy-start.7 = (f32[512,32]{0,1:T(8,128)}, f32[512,32]{0,1:T(8,128)S(1)}, u32[]{:S(2)}) copy-start(f32[512,32]{0,1:T(8,128)S(1)} %get-tuple-element.50) | copy-start | bytes 196612
  73.4 15.0 %copy-start.9 = (f32[512,32]{0,1:T(8,128)}, f32[512,32]{0,1:T(8,128)S(1)}, u32[]{:S(2)}) copy-start(f32[512,32]{0,1:T(8,128)S(1)} %get-tuple-element.51) | copy-start | bytes 196612
  74.6 4.8 all-to-all-start.1
  79.7 15.7 %copy-start.11 = (bf16[1024,64,1]{0,1,2:T(8,128)(2,1)}, bf16[1024,64,1]{0,1,2:T(8,128)(2,1)S(1)}, u32[]{:S(2)}) copy-start(bf16[1024,64,1]{0,1,2:T(8,128)(2,1)S(1)} %reshape.386) | copy-start | bytes 393220
  95.4 13.4 %copy-start.2 = (bf16[1024,7,64]{0,2,1:T(8,128)(2,1)}, bf16[1024,7,64]{0,2,1:T(8,128)(2,1)S(1)}, u32[]{:S(2)}) copy-start(bf16[1024,7,64]{0,2,1:T(8,128)(2,1)S(1)} %reshape.355) | copy-start | bytes 2752516
  134.3 5.6 all-to-all-start.3
  137.9 54.0 %all-gather.12.cloned.1.call-start = ((), (), s32[]{:S(2)}) async-start(), calls=%async_computation.19 | async-start | bytes 4587520 | tf_op jit(solution)/shard_map/all_gather | solution.py:196
  139.9 0.9 copy-start.5
  143.9 276.2 %copy-start = (f32[512,896]{1,0:T(8,128)}, f32[512,896]{1,0:T(8,128)S(1)}, u32[]{:S(2)}) copy-start(f32[512,896]{1,0:T(8,128)S(1)} %get-tuple-element.61) | copy-start | bytes 5505028
  145.3 78.9 %all-gather.14.cloned.1.call-start = ((), (), s32[]{:S(2)}) async-start(), calls=%async_computation.20 | async-start | bytes 2580480 | tf_op jit(solution)/shard_map/all_gather | solution.py:126
  145.9 110.0 %all-gather.18.cloned.1.call-start = ((), (), s32[]{:S(2)}) async-start(), calls=%async_computation.22 | async-start | bytes 2580480 | tf_op jit(solution)/shard_map/all_gather | solution.py:128
  146.5 158.9 %all-gather.20.cloned.1.call-start = ((), (), s32[]{:S(2)}) async-start(), calls=%async_computation.24 | async-start | bytes 4587520 | tf_op jit(solution)/shard_map/all_gather | solution.py:211
  147.3 272.8 %reduce-scatter.12.cloned.1.call-start = ((), (), s32[]{:S(2)}) async-start(), calls=%async_computation.25 | async-start | bytes 9175040 | tf_op jit(solution)/shard_map/reduce_scatter | solution.py:218
  324.7 8.7 copy-start.24
  324.7 8.7 copy-start.26
  341.2 130.2 %reduce-scatter.10.cloned.1.call-start = ((), (), s32[]{:S(2)}) async-start(), calls=%async_computation.23 | async-start | bytes 4587520 | tf_op jit(solution)/shard_map/reduce_scatter | solution.py:203
  350.8 322.8 %reduce-scatter.18.cloned.1.call-start = ((), (), s32[]{:S(2)}) async-start(), calls=%async_computation.28 | async-start | bytes 516096 | tf_op jit(solution)/shard_map/reduce_scatter | solution.py:331
  471.4 4.2 copy-start.25
  505.6 22.5 %copy-start.18 = (f32[896]{0:T(1024)S(1)}, f32[896]{0:T(1024)}, u32[]{:S(2)}) copy-start(f32[896]{0:T(1024)} %copy-done.17) | copy-start | bytes 10756
  505.6 22.5 %copy-start.21 = (f32[512]{0:T(512)S(1)}, f32[512]{0:T(512)}, u32[]{:S(2)}) copy-start(f32[512]{0:T(512)} %copy-done.20) | copy-start | bytes 6148
  529.4 144.2 %reduce-scatter.16.cloned.1.call-start = ((), (), s32[]{:S(2)}) async-start(), calls=%async_computation.27 | async-start | bytes 516096 | tf_op jit(solution)/shard_map/reduce_scatter | solution.py:329
  554.8 14.1 %copy-start.8 = (f32[512,32]{0,1:T(8,128)S(1)}, f32[512,32]{0,1:T(8,128)}, u32[]{:S(2)}) copy-start(f32[512,32]{0,1:T(8,128)} %copy-done.7) | copy-start | bytes 196612
  554.8 14.1 %copy-start.10 = (f32[512,32]{0,1:T(8,128)S(1)}, f32[512,32]{0,1:T(8,128)}, u32[]{:S(2)}) copy-start(f32[512,32]{0,1:T(8,128)} %copy-done.9) | copy-start | bytes 196612
  570.3 103.5 %reduce-scatter.20.cloned.1.call-start = ((), (), s32[]{:S(2)}) async-start(), calls=%async_computation.29 | async-start | bytes 3612672 | tf_op jit(solution)/shard_map/reduce_scatter | solution.py:333
  574.2 0.9 copy-start.12
  574.3 110.6 %reduce-scatter.14.cloned.1.call-start = ((), (), s32[]{:S(2)}) async-start(), calls=%async_computation.26 | async-start | bytes 3612672 | tf_op jit(solution)/shard_map/reduce_scatter | solution.py:327
  593.9 1.0 copy-start.3
  593.9 1.2 copy-start.4
  595.1 0.9 copy-start.6
  599.1 141.2 %reduce-scatter.26.cloned.1.call-start = ((), (), s32[]{:S(2)}) async-start(), calls=%async_computation.32 | async-start | bytes 5160960 | tf_op jit(solution)/shard_map/reduce_scatter | solution.py:230
  610.0 185.2 %reduce-scatter.24.cloned.1.call-start = ((), (), s32[]{:S(2)}) async-start(), calls=%async_computation.31 | async-start | bytes 5160960 | tf_op jit(solution)/shard_map/reduce_scatter | solution.py:229
  620.7 229.4 %reduce-scatter.22.cloned.1.call-start = ((), (), s32[]{:S(2)}) async-start(), calls=%async_computation.30 | async-start | bytes 5160960 | tf_op jit(solution)/shard_map/reduce_scatter | solution.py:228
  631.8 3.5 copy-start.14
  631.8 265.4 %all-reduce.17.cloned.1.call-start = ((), (), s32[]{:S(2)}) async-start(), calls=%async_computation.33 | async-start | bytes 234496 | tf_op jit(solution)/shard_map/psum | solution.py:347
  635.7 3.0 copy-start.16
  638.8 46.1 %copy-start.23 = (f32[512]{0:T(512)S(1)}, f32[512]{0:T(512)}, u32[]{:S(2)}) copy-start(f32[512]{0:T(512)} %get-tuple-element.52) | copy-start | bytes 6148
  673.7 275.7 %all-reduce.19.cloned.1.call-start = ((), (), s32[]{:S(2)}) async-start(), calls=%async_computation.34 | async-start | bytes 1605632 | tf_op jit(solution)/shard_map/psum | solution.py:347
Sparse Core Ops, SparseCore 0:
  9.7 28.7 all-gather.7
  40.1 24.9 all-gather.9
  66.8 30.2 all-gather.15
  145.5 46.4 all-gather.11
  193.4 30.7 all-gather.13
  225.7 30.1 all-gather.17
  257.8 47.5 all-gather.19
  341.3 78.7 reduce-scatter.11
  423.1 48.2 reduce-scatter.9
  529.6 31.1 reduce-scatter.17
  570.4 31.2 reduce-scatter.15
  603.9 38.7 reduce-scatter.19
  644.9 39.9 reduce-scatter.13
  687.6 52.6 reduce-scatter.25
  743.1 52.0 reduce-scatter.23
  798.0 52.0 reduce-scatter.21
  854.7 42.4 all-reduce.16
  900.2 49.0 all-reduce.18
where the time goes:
time: 976 us; the launch traced here: 969 us
  waiting for transfers between devices  536 us (55%)
  matrix products  202 us (21%)
  blocking collectives  101 us (10%)
  other arithmetic  56.7 us (6%)
  local copies, waits for them, and re-layouts  43.5 us (4%)
  between operations  18 us (2%)
  starting transfers between devices  11.7 us (1%)
    psum x2, waiting for transfers between devices, per_device(): lax.psum((shard_query_weight, shard_query_bias, shard_key_weight, shard_k...  99.3 us
    reduce_scatter x1, waiting for transfers between devices, per_device(): lax.psum_scatter(times_transpose(grad_gate, gate_again) + times_transpose...  69.2 us
    reduce_scatter x1, waiting for transfers between devices, per_device(): lax.psum_scatter(grad_gate_weight, ('shard', 'ctx'), scatter_dimension=0,...  54.9 us
    reduce_scatter x1, waiting for transfers between devices, per_device(): lax.psum_scatter(grad_up_weight, ('shard', 'ctx'), scatter_dimension=0, t...  54.9 us
    reduce_scatter x1, waiting for transfers between devices, per_device(): lax.psum_scatter(grad_down_weight, ('shard', 'ctx'), scatter_dimension=1,...  52.4 us
    all_gather x1, waiting for transfers between devices, per_device(): grad_rows = lax.all_gather(cotangent, 'tp', axis=0, tiled=True)  49.5 us
    unnamed x2, blocking collectives  49.4 us
    reduce_scatter x1, waiting for transfers between devices, per_device(): lax.psum_scatter(matmul(activation, down_weight_full).astype(jnp.bfloat16...  49.3 us
  transfers between devices with their start and end apart: 21, of which 14 were waited for; matrix products, arithmetic and copies ran while one was open for 21% of the time, Pallas kernels for 0%

commit v1 on v0

v1 whole, which is shorter than its diff:
```python
import functools

import jax
import jax.numpy as jnp
from jax import lax
from jax.experimental import pallas as pl
from jax.experimental.pallas import tpu as pltpu
from jax.sharding import PartitionSpec as P

QUERY_HEADS = 14
KEY_VALUE_HEADS = 2
HEAD_WIDTH = 64
GROUP = QUERY_HEADS // KEY_VALUE_HEADS

EPSILON = 1e-06
THETA = 1000000.0
NEGATIVE = -1e30
BF = jnp.bfloat16
F32 = jnp.float32


def dot(left, right, left_dim, right_dim, out=F32):
    return lax.dot_general(
        left, right, (((left_dim,), (right_dim,)), ((), ())), preferred_element_type=out
    )


def fill_bias(bias, doc_row, doc_col, row_start, row_count, span):
    keys = lax.broadcasted_iota(jnp.int32, (span, row_count), 0)
    queries = lax.broadcasted_iota(jnp.int32, (span, row_count), 1) + row_start
    key_doc = doc_col[0:span, :]
    query_doc = doc_row[:, row_start : row_start + row_count]
    same = (key_doc == query_doc) & (query_doc >= 0) & (keys <= queries)
    bias[0:span, :] = jnp.where(same | (keys == queries), 0.0, NEGATIVE)


def load_keys(half, own, other, keys_t, keys, values_t, values):
    width = KEY_VALUE_HEADS * HEAD_WIDTH
    parts = (own,) if half == 0 else (other, own)
    for place, part in enumerate(parts):
        count = part.shape[1]
        rows = slice(place * count, (place + 1) * count)
        key_t = part[0:width, :]
        value_t = part[width : 2 * width, :]
        keys_t[:, rows] = key_t
        values_t[:, rows] = value_t
        key = key_t.astype(F32).T.astype(BF)
        for head in range(KEY_VALUE_HEADS):
            lanes = slice(head * HEAD_WIDTH, (head + 1) * HEAD_WIDTH)
            keys[head, rows, :] = key[:, lanes]
        if values is not None:
            value = value_t.astype(F32).T.astype(BF)
            for head in range(KEY_VALUE_HEADS):
                lanes = slice(head * HEAD_WIDTH, (head + 1) * HEAD_WIDTH)
                values[head, rows, :] = value[:, lanes]


def attention_forward_body(
    half_ref, doc_row, doc_col, query_t, own, other, mixed_t, lse, keys_t, keys, values_t, bias
):
    token_count = query_t.shape[1]
    step = token_count // 2
    for half in (0, 1):

        @pl.when(half_ref[0] == half)
        def _():
            load_keys(half, own, other, keys_t, keys, values_t, None)
            for block in (0, 1):
                span = half * token_count + (block + 1) * step
                start = half * token_count + block * step
                cols = slice(block * step, (block + 1) * step)
                fill_bias(bias, doc_row, doc_col, start, step, span)
                for group in range(KEY_VALUE_HEADS):
                    head_rows = slice(group * HEAD_WIDTH, (group + 1) * HEAD_WIDTH)

                    def one(index, carry):
                        head = group * GROUP + index
                        place = pl.ds(pl.multiple_of(head * HEAD_WIDTH, HEAD_WIDTH), HEAD_WIDTH)
                        score = (
                            jnp.dot(
                                keys[group, 0:span, :],
                                query_t[place, cols],
                                preferred_element_type=F32,
                            )
                            + bias[0:span, :]
                        )
                        top = jnp.max(score, axis=0, keepdims=True)
                        weight = jnp.exp(score - top)
                        total = jnp.sum(weight, axis=0, keepdims=True)
                        out = jnp.dot(
                            values_t[head_rows, 0:span],
                            weight.astype(BF),
                            preferred_element_type=F32,
                        )
                        mixed_t[place, cols] = (out / total).astype(BF)
                        lse[head, :, cols] = jnp.broadcast_to(top + jnp.log(total), (8, step))
                        return carry

                    lax.fori_loop(0, GROUP, one, 0)


def attention_forward(half, doc_row, doc_col, query_t, own, other):
    width, token_count = query_t.shape
    kv = KEY_VALUE_HEADS * HEAD_WIDTH
    vmem = pl.BlockSpec(memory_space=pltpu.VMEM)
    return pl.pallas_call(
        attention_forward_body,
        out_shape=(
            jax.ShapeDtypeStruct((width, token_count), BF),
            jax.ShapeDtypeStruct((QUERY_HEADS, 8, token_count), F32),
        ),
        in_specs=[pl.BlockSpec(memory_space=pltpu.SMEM)] + [vmem] * 5,
        out_specs=(vmem, vmem),
        scratch_shapes=[
            pltpu.VMEM((kv, 2 * token_count), BF),
            pltpu.VMEM((KEY_VALUE_HEADS, 2 * token_count, HEAD_WIDTH), BF),
            pltpu.VMEM((kv, 2 * token_count), BF),
            pltpu.VMEM((2 * token_count, token_count // 2), F32),
        ],
        cost_estimate=pl.CostEstimate(
            flops=int(15e9), bytes_accessed=4 * width * token_count, transcendentals=0
        ),
        name="attention_forward",
    )(half, doc_row, doc_col, query_t, own, other)


def attention_backward_body(
    half_ref,
    doc_row,
    doc_col,
    query_t,
    own,
    other,
    mixed_t,
    grad_t,
    lse,
    grad_query_t,
    grad_key,
    grad_value,
    keys_t,
    keys,
    values_t,
    values,
    bias,
):
    token_count = query_t.shape[1]
    step = token_count // 2
    grad_key[...] = jnp.zeros_like(grad_key)
    grad_value[...] = jnp.zeros_like(grad_value)
    for half in (0, 1):

        @pl.when(half_ref[0] == half)
        def _():
            load_keys(half, own, other, keys_t, keys, values_t, values)
            for block in (0, 1):
                span = half * token_count + (block + 1) * step
                start = half * token_count + block * step
                cols = slice(block * step, (block + 1) * step)
                fill_bias(bias, doc_row, doc_col, start, step, span)
                for group in range(KEY_VALUE_HEADS):
                    head_rows = slice(group * HEAD_WIDTH, (group + 1) * HEAD_WIDTH)

                    def one(index, carry):
                        head = group * GROUP + index
                        place = pl.ds(pl.multiple_of(head * HEAD_WIDTH, HEAD_WIDTH), HEAD_WIDTH)
                        query = query_t[place, cols]
                        grad = grad_t[place, cols]
                        delta = jnp.sum(
                            grad.astype(F32) * mixed_t[place, cols].astype(F32),
                            axis=0,
                            keepdims=True,
                        )
                        score = (
                            jnp.dot(keys[group, 0:span, :], query, preferred_element_type=F32)
                            + bias[0:span, :]
                        )
                        prob = jnp.exp(score - lse[head, 0:1, cols])
                        grad_prob = jnp.dot(
                            values[group, 0:span, :], grad, preferred_element_type=F32
                        )
                        grad_score = (prob * (grad_prob - delta)).astype(BF)
                        grad_value[group, 0:span, :] += dot(prob.astype(BF), grad, 1, 1)
                        grad_key[group, 0:span, :] += dot(grad_score, query, 1, 1)
                        grad_query_t[place, cols] = jnp.dot(
                            keys_t[head_rows, 0:span], grad_score, preferred_element_type=F32
                        ) * (HEAD_WIDTH ** (-0.5))
                        return carry

                    lax.fori_loop(0, GROUP, one, 0)


def attention_backward(half, doc_row, doc_col, query_t, own, other, mixed_t, grad_t, lse):
    width, token_count = query_t.shape
    kv = KEY_VALUE_HEADS * HEAD_WIDTH
    vmem = pl.BlockSpec(memory_space=pltpu.VMEM)
    sums = jax.ShapeDtypeStruct((KEY_VALUE_HEADS, 2 * token_count, HEAD_WIDTH), F32)
    return pl.pallas_call(
        attention_backward_body,
        out_shape=(jax.ShapeDtypeStruct((width, token_count), F32), sums, sums),
        in_specs=[pl.BlockSpec(memory_space=pltpu.SMEM)] + [vmem] * 8,
        out_specs=(vmem, vmem, vmem),
        scratch_shapes=[
            pltpu.VMEM((kv, 2 * token_count), BF),
            pltpu.VMEM((KEY_VALUE_HEADS, 2 * token_count, HEAD_WIDTH), BF),
            pltpu.VMEM((kv, 2 * token_count), BF),
            pltpu.VMEM((KEY_VALUE_HEADS, 2 * token_count, HEAD_WIDTH), BF),
            pltpu.VMEM((2 * token_count, token_count // 2), F32),
        ],
        cost_estimate=pl.CostEstimate(
            flops=int(35e9), bytes_accessed=8 * width * token_count, transcendentals=0
        ),
        name="attention_backward",
    )(half, doc_row, doc_col, query_t, own, other, mixed_t, grad_t, lse)


def rope_tables(half, token_count):
    half_dim = HEAD_WIDTH // 2
    frequency = THETA ** (-(jnp.arange(half_dim, dtype=F32) * 2.0) / HEAD_WIDTH)
    positions = half * token_count + jnp.arange(token_count, dtype=jnp.int32)
    angles = frequency[:, None] * positions.astype(F32)[None, :]
    return jnp.cos(angles), jnp.sin(angles)


def rotate(values_t, cosine, sine):
    rows, count = values_t.shape
    split = values_t.reshape(rows // HEAD_WIDTH, 2, HEAD_WIDTH // 2, count)
    first, second = split[:, 0], split[:, 1]
    return jnp.stack(
        [first * cosine - second * sine, second * cosine + first * sine], 1
    ).reshape(rows, count)


class Mesh:
    def __init__(self):
        self.shards = lax.axis_size("shard")
        self.ctxs = lax.axis_size("ctx")
        self.tps = lax.axis_size("tp")
        self.fast = (self.shards, self.ctxs, self.tps) == (4, 2, 4)
        self.z = lax.axis_index("shard")
        self.c = lax.axis_index("ctx")
        self.t = lax.axis_index("tp")

    def across(self, value):
        pairs = [(i, self.ctxs - 1 - i) for i in range(self.ctxs)]
        return lax.ppermute(value, "ctx", pairs)

    def side(self, value, which):
        return lax.ppermute(value, "tp", [(i, i ^ which) for i in range(self.tps)])

    def gather_rows(self, block):
        if not self.fast:
            return lax.all_gather(block, ("shard", "ctx"), axis=0)
        last = self.shards - 1
        plus, minus = [], []
        right = left = block
        for step in range(1, self.shards):
            right = lax.ppermute(right, "shard", [(i, i + 1) for i in range(step - 1, last)])
            left = lax.ppermute(left, "shard", [(i + 1, i) for i in range(0, last - step + 1)])
            plus.append(right)
            minus.append(left)
        line = jnp.stack(plus[::-1] + [block] + minus)
        mine = lax.dynamic_slice_in_dim(line, last - self.z, self.shards, 0)
        theirs = self.across(mine)
        low = jnp.where(self.c == 0, mine, theirs)
        high = jnp.where(self.c == 0, theirs, mine)
        full = jnp.stack([low, high], 1)
        return full.reshape((self.shards * self.ctxs,) + block.shape)

    def reduce_rows(self, value):
        blocks, rows, cols = value.shape
        if not self.fast:
            part = lax.psum_scatter(
                value, ("shard", "ctx"), scatter_dimension=0, tiled=True
            )
            return lax.psum(part[0].astype(F32), "tp")
        value = value.reshape(self.shards, self.ctxs, rows, cols)
        send = lax.dynamic_index_in_dim(value, 1 - self.c, 1, False).astype(BF)
        keep = lax.dynamic_index_in_dim(value, self.c, 1, False)
        part = keep.astype(F32) + self.across(send).astype(F32)
        part = part.reshape(self.shards, self.tps, rows // self.tps, cols)

        def quarter(which):
            return lax.dynamic_index_in_dim(part, self.t ^ which, 1, False)

        mine = quarter(0)
        for which in (1, 2, 3):
            mine = mine + self.side(quarter(which).astype(BF), which).astype(F32)
        total = lax.dynamic_index_in_dim(mine, self.z, 0, False)
        for shift in (-3, 3, -2, 2, -1, 1):
            index = jnp.clip(self.z + shift, 0, self.shards - 1)
            piece = lax.dynamic_index_in_dim(mine, index, 0, False).astype(BF)
            pairs = [
                (i, i + shift) for i in range(self.shards) if 0 <= i + shift < self.shards
            ]
            total = total + lax.ppermute(piece, "shard", pairs).astype(F32)
        low = total.astype(BF)
        one, two, three = (self.side(low, which) for which in (1, 2, 3))
        odd = (self.t & 1) == 1
        a, b = jnp.where(odd, one, low), jnp.where(odd, low, one)
        c, d = jnp.where(odd, three, two), jnp.where(odd, two, three)
        far = self.t >= 2
        return jnp.concatenate(
            [
                jnp.where(far, c, a),
                jnp.where(far, d, b),
                jnp.where(far, a, c),
                jnp.where(far, b, d),
            ],
            0,
        ).astype(F32)

    def gather_tokens(self, rows):
        if not self.fast:
            every = lax.all_gather(rows, "tp", axis=0)
            return [
                lax.dynamic_index_in_dim(every, (self.t + i) % self.tps, 0, False)
                for i in range(self.tps)
            ]
        half = rows.shape[0] // 2
        one = self.side(rows, 1)
        two = self.side(rows, 2)
        top = self.side(one[:half], 2)
        bottom = self.side(two[half:], 1)
        return [rows, one, two, jnp.concatenate([top, bottom], 0)]

    def scatter_tokens(self, parts):
        if not self.fast:
            every = jnp.stack(parts)
            ordered = jnp.stack(
                [
                    lax.dynamic_index_in_dim(every, (i - self.t) % self.tps, 0, False)
                    for i in range(self.tps)
                ]
            )
            return lax.psum_scatter(ordered, "tp", scatter_dimension=0, tiled=False)
        own, one, two, three = parts
        half = own.shape[0] // 2
        top = self.side(three[:half], 1)
        bottom = self.side(three[half:], 2)
        two = jnp.concatenate([two[:half] + top, two[half:]], 0)
        one = jnp.concatenate([one[:half], one[half:] + bottom], 0)
        return (
            own.astype(F32)
            + self.side(one, 1).astype(F32)
            + self.side(two, 2).astype(F32)
        )


def per_device(
    tokens,
    doc_ids,
    w_query,
    b_query,
    key_projection,
    key_bias_vector,
    value_projection,
    value_bias_vector,
    w_output,
    gain_attn,
    gain_mlp,
    w_gate,
    w_up,
    w_down,
    cotangent,
):
    mesh = Mesh()
    token_count, width = tokens.shape
    rows = w_query.shape[0]
    padded = (rows // 16 + 1) * 16
    query_width = QUERY_HEADS * HEAD_WIDTH
    kv_width = KEY_VALUE_HEADS * HEAD_WIDTH
    kv_rows = key_bias_vector.shape[0]
    fused_width = query_width + 2 * kv_width
    blocks = mesh.shards * mesh.ctxs

    small = jnp.concatenate(
        [b_query, key_bias_vector, value_bias_vector, gain_attn, gain_mlp]
    )
    small_ends = [rows, rows + kv_rows, rows + 2 * kv_rows, 2 * rows + 2 * kv_rows]
    small = jnp.pad(small, (0, fused_width - small.shape[0]))
    packed = jnp.concatenate(
        [
            jnp.concatenate([w_query, key_projection, value_projection], 1),
            small[None],
            jnp.zeros((padded - rows - 1, fused_width), BF),
        ],
        0,
    )
    gathered = mesh.gather_rows(packed)
    fused_weight = gathered[:, :rows].reshape(width, fused_width)
    smalls = gathered[:, rows]
    pieces = jnp.split(smalls[:, : small_ends[-1] + rows], small_ends, 1)
    bias_q, bias_k, bias_v, first_gain, second_gain = (
        piece.reshape(-1).astype(F32) for piece in pieces
    )
    fused_bias = jnp.concatenate([bias_q, bias_k, bias_v])

    output_weight = mesh.gather_rows(w_output).reshape(width, width)
    gate_weight = lax.all_gather(w_gate, ("shard", "ctx"), axis=0, tiled=True)
    up_weight = lax.all_gather(w_up, ("shard", "ctx"), axis=0, tiled=True)
    down_weight_t = lax.all_gather(w_down.T, ("shard", "ctx"), axis=0, tiled=True)
    grad_parts = mesh.gather_tokens(cotangent)

    tok_float = tokens.astype(F32)
    first_inv = lax.rsqrt(jnp.mean(tok_float * tok_float, -1, keepdims=True) + EPSILON)
    normed_attn = (tok_float * first_inv * first_gain).astype(BF)
    cosine, sine = rope_tables(mesh.c, token_count)
    fused_t = dot(fused_weight, normed_attn, 0, 1) + fused_bias[:, None]
    query_t = rotate(fused_t[:query_width], cosine, sine).astype(BF) * (HEAD_WIDTH ** (-0.5))
    key_t = rotate(fused_t[query_width : query_width + kv_width], cosine, sine).astype(BF)
    value_t = fused_t[query_width + kv_width :].astype(BF)
    own = jnp.concatenate([key_t, value_t], 0)
    other = mesh.across(own)
    half = mesh.c.astype(jnp.int32).reshape(1)
    doc_col = doc_ids.reshape(-1, 1)
    mixed_t, lse = attention_forward(half, doc_ids, doc_col, query_t, own, other)

    hidden = tok_float + dot(mixed_t, output_weight, 0, 0)
    second_inv = lax.rsqrt(jnp.mean(hidden * hidden, -1, keepdims=True) + EPSILON)
    normed_mlp = (hidden * second_inv * second_gain).astype(BF)
    normed_parts = mesh.gather_tokens(normed_mlp)

    downs, backs, acts, gates, ups = [], [], [], [], []
    for x, g in zip(normed_parts, grad_parts):
        gate = dot(x, gate_weight, 1, 0)
        up = dot(x, up_weight, 1, 0)
        sig = jax.nn.sigmoid(gate)
        silu = gate * sig
        act = (silu * up).astype(BF)
        grad_act = dot(g, down_weight_t, 1, 0)
        grad_gate = (grad_act * up * sig * (1.0 + gate * (1.0 - sig))).astype(BF)
        grad_up = (grad_act * silu).astype(BF)
        backs.append(
            (dot(grad_gate, gate_weight, 1, 1) + dot(grad_up, up_weight, 1, 1)).astype(BF)
        )
        downs.append(dot(act, down_weight_t, 1, 1).astype(BF))
        acts.append(act)
        gates.append(grad_gate)
        ups.append(grad_up)
    grad_normed_mlp = mesh.scatter_tokens(backs).astype(F32)
    down_rows = mesh.scatter_tokens(downs).astype(F32)
    result = hidden + down_rows

    normed_all = jnp.concatenate(normed_parts, 0)
    grad_all = jnp.concatenate(grad_parts, 0)

    def scatter_grad(left, right):
        full = dot(left, jnp.concatenate(right, 0), 0, 0).astype(BF)
        return lax.psum_scatter(full, ("shard", "ctx"), scatter_dimension=0, tiled=True).astype(
            F32
        )

    part_gate = scatter_grad(normed_all, gates)
    part_up = scatter_grad(normed_all, ups)
    part_down = scatter_grad(grad_all, acts).T

    grad_out = cotangent.astype(F32)
    scaled_two = grad_normed_mlp * second_gain
    grad_hidden = (
        grad_out
        + second_inv * scaled_two
        - hidden * second_inv**3 * jnp.mean(scaled_two * hidden, -1, keepdims=True)
    )
    grad_second_gain = jnp.sum(grad_normed_mlp * hidden * second_inv, 0)
    grad_branch = grad_hidden.astype(BF)
    grad_mixed_t = dot(output_weight, grad_branch, 1, 1).astype(BF)
    grad_output_weight = dot(mixed_t, grad_branch, 1, 0)
    grad_query_rot, grad_key_sum, grad_value_sum = attention_backward(
        half, doc_ids, doc_col, query_t, own, other, mixed_t, grad_mixed_t, lse
    )
    sums = jnp.concatenate([grad_key_sum * (HEAD_WIDTH ** (-0.5) * 8.0), grad_value_sum], 0)
    first_half, second_half = sums[:, :token_count], sums[:, token_count:]
    to_other = jnp.where(mesh.c == 0, second_half, first_half).astype(BF)
    own_sums = jnp.where(mesh.c == 0, first_half, second_half)
    own_sums = (own_sums + mesh.across(to_other).astype(F32)).astype(BF).astype(F32)
    own_sums_t = own_sums.transpose(0, 2, 1).reshape(2 * kv_width, token_count)
    grad_query_pre = rotate(grad_query_rot.astype(BF).astype(F32), cosine, -sine)
    grad_key_pre = rotate(own_sums_t[:kv_width], cosine, -sine)
    fused_grad_t = jnp.concatenate([grad_query_pre, grad_key_pre, own_sums_t[kv_width:]], 0)
    grad_fused_bias = jnp.sum(fused_grad_t, 1)
    fused_low = fused_grad_t.astype(BF)
    grad_normed_attn = dot(fused_low, fused_weight, 0, 1)
    grad_fused_weight = dot(normed_attn, fused_low, 0, 1)
    scaled_one = grad_normed_attn * first_gain
    grad_tokens = (
        grad_hidden
        + first_inv * scaled_one
        - tok_float * first_inv**3 * jnp.mean(scaled_one * tok_float, -1, keepdims=True)
    )
    grad_first_gain = jnp.sum(grad_normed_attn * tok_float * first_inv, 0)

    grad_smalls = jnp.concatenate(
        [
            grad_fused_bias[:query_width].reshape(blocks, rows),
            grad_fused_bias[query_width : query_width + kv_width].reshape(blocks, kv_rows),
            grad_fused_bias[query_width + kv_width :].reshape(blocks, kv_rows),
            grad_first_gain.reshape(blocks, rows),
            grad_second_gain.reshape(blocks, rows),
        ],
        1,
    )
    grad_smalls = jnp.pad(grad_smalls, ((0, 0), (0, fused_width - grad_smalls.shape[1])))
    grad_packed = jnp.concatenate(
        [
            grad_fused_weight.reshape(blocks, rows, fused_width),
            grad_smalls[:, None],
            jnp.zeros((blocks, padded - rows - 1, fused_width), F32),
        ],
        1,
    )
    grad_out_padded = jnp.pad(
        grad_output_weight.reshape(blocks, rows, width), ((0, 0), (0, padded - rows), (0, 0))
    )
    sum_output_weight = mesh.reduce_rows(grad_out_padded)[:rows]
    summed = mesh.reduce_rows(grad_packed)
    sum_small = jnp.split(summed[rows, : small_ends[-1] + rows], small_ends)
    return (
        result.astype(BF),
        grad_tokens.astype(BF),
        summed[:rows, :query_width],
        sum_small[0],
        summed[:rows, query_width : query_width + kv_width],
        sum_small[1],
        summed[:rows, query_width + kv_width :],
        sum_small[2],
        sum_output_weight,
        sum_small[3],
        sum_small[4],
        part_gate,
        part_up,
        part_down,
    )


def solution(mesh):
    both = ("shard", "ctx")
    every = ("shard", "ctx", "tp")
    in_specs = (
        P(every, None),
        P(("shard", "tp"), None),
        P(both, None),
        P(both),
        P(both, None),
        P(both),
        P(both, None),
        P(both),
        P(both, None),
        P(both),
        P(both),
        P(both, "tp"),
        P(both, "tp"),
        P("tp", both),
        P(every, None),
    )
    out_specs = (
        P(every, None),
        P(every, None),
        P(both, None),
        P(both),
        P(both, None),
        P(both),
        P(both, None),
        P(both),
        P(both, None),
        P(both),
        P(both),
        P(both, "tp"),
        P(both, "tp"),
        P("tp", both),
    )
    return jax.shard_map(
        per_device, mesh=mesh, in_specs=in_specs, out_specs=out_specs, check_vma=False
    )
```

time: 976 us -> 497 us (0.51)
  waiting for transfers between devices: 536 us -> 141 us
  blocking collectives: 101 us -> 0 us
  starting transfers between devices: 11.7 us -> 102 us
  matrix products: 202 us -> 115 us
  Pallas kernels: 0 us -> 31.5 us
  other arithmetic: 56.7 us -> 39 us
    reduce_scatter x9 -> x3, waiting for transfers between devices: 292 us -> 0.01 us  [scatter_grad(): lax.psum_scatter(full, ('shard', 'ctx'), scatter_dimension=0, tiled=True)]
    ppermute x0 -> x58, waiting for transfers between devices: none -> 140 us  [the longest x28 67.7 us: side(): return lax.ppermute(value, 'tp', [(i, i ^ which) for i in range(self.tps)])]
    all_gather x7 -> x3, waiting for transfers between devices: 138 us -> 0.01 us  [the longest x1 0.01 us: per_device(): gate_weight = lax.all_gather(w_gate, ('shard', 'ctx'), axis=0, tiled=True)]
    ppermute x0 -> x58, starting transfers between devices: none -> 102 us  [the longest x12 34.4 us: reduce_rows(): total = total + lax.ppermute(piece, 'shard', pairs).astype(F32)]
    psum x2 -> x0, waiting for transfers between devices: 99.3 us -> none  [per_device(): lax.psum((shard_query_weight, shard_query_bias, shard_key_weight, shard_k...]
    dot_general x27 -> x33, matrix products: 202 us -> 115 us  [dot(): lax.dot_general(left, right, (((left_dim,), (right_dim,)), ((), ())), pre...]
    unnamed x2 -> x0, blocking collectives: 49.4 us -> none
    pallas_call x0 -> x2, Pallas kernels: none -> 31.5 us  [the longest x1 16.2 us: attention_backward(): pl.pallas_call(attention_backward_body, out_shape=(jax.ShapeDtypeStruct((...]
  transfers between devices with their start and end apart: 21 -> 64, of which waited for: 14 -> 23; matrix products, arithmetic and copies ran while one was open for 21% -> 35% of each run, Pallas kernels for 0% -> 6%
where the time goes in v1:
time: 497 us; the launch traced here: 487 us
  waiting for transfers between devices  141 us (28%)
  matrix products  115 us (23%)
  starting transfers between devices  102 us (21%)
  local copies, waits for them, and re-layouts  42 us (8%)
  other arithmetic  39 us (8%)
  Pallas kernels  31.5 us (6%)
  between operations  15.9 us (3%)
    dot_general x33, matrix products, dot(): lax.dot_general(left, right, (((left_dim,), (right_dim,)), ((), ())), pre...  115 us
    ppermute x28, waiting for transfers between devices, side(): return lax.ppermute(value, 'tp', [(i, i ^ which) for i in range(self.tps)])  67.7 us
    ppermute x6, waiting for transfers between devices, gather_rows(): lax.ppermute(left, 'shard', [(i + 1, i) for i in range(0, last - step + 1)])  52 us
    ppermute x12, starting transfers between devices, reduce_rows(): total = total + lax.ppermute(piece, 'shard', pairs).astype(F32)  34.4 us
    ppermute x28, starting transfers between devices, side(): return lax.ppermute(value, 'tp', [(i, i ^ which) for i in range(self.tps)])  32.1 us
    unnamed x174, local copies, waits for them, and re-layouts  21.8 us
    ppermute x6, starting transfers between devices, across(): return lax.ppermute(value, 'ctx', pairs)  16.2 us
    pallas_call x1, Pallas kernels, attention_backward(): pl.pallas_call(attention_backward_body, out_shape=(jax.ShapeDtypeStruct((...  16.2 us
  transfers between devices with their start and end apart: 64, of which 23 were waited for; matrix products, arithmetic and copies ran while one was open for 35% of the time, Pallas kernels for 6%

profile of v1, /device:TPU:0, one launch (start us, length us, event | category | flops | bytes accessed | tf_op | source)
XLA Modules:
  0.0 487.0 jit_solution(1972835925940107887)
XLA Ops:
  8.0 5.0 %collective-permute-start.8 = (bf16[112,896]{1,0:T(8,128)(2,1)}, bf16[112,896]{1,0:T(8,128)(2,1)S(1)}, u32[]{:S(2)}, u32[]{:S(2)}) collective-permute-start(bf16[112,896]{1,0:T(8,128)(2,1)} %param.23), channel_id=1, source_target_pairs={{0,8},{8,16},{16,24},{1,9},{9,17},{17,25},{2,10},{10,18},{18,26},{... | collective-permute-start | bytes 602120 | tf_op jit(solution)/shard_map/ppermute | solution.py:257
  13.0 3.4 concatenate.77
  17.6 3.5 collective-permute-start
  24.4 9.9 %collective-permute-done = bf16[128,1152]{1,0:T(8,128)(2,1)S(1)} collective-permute-done((bf16[128,1152]{1,0:T(8,128)(2,1)S(1)}, bf16[128,1152]{1,0:T(8,128)(2,1)S(1)}, u32[]{:S(2)}, u32[]{:S(2)}) %collective-permute-start) | collective-permute-done | bytes 294944 | tf_op jit(solution)/shard_map/ppermute | solution.py:257
  34.9 9.1 %collective-permute-done.3 = bf16[128,1152]{1,0:T(8,128)(2,1)S(1)} collective-permute-done((bf16[128,1152]{1,0:T(8,128)(2,1)S(1)}, bf16[128,1152]{1,0:T(8,128)(2,1)S(1)}, u32[]{:S(2)}, u32[]{:S(2)}) %collective-permute-start.3) | collective-permute-done | bytes 294944 | tf_op jit(solution)/shard_map/ppermute | solution.py:258
  45.3 6.5 %collective-permute-done.11 = bf16[112,896]{1,0:T(8,128)(2,1)S(1)} collective-permute-done((bf16[112,896]{1,0:T(8,128)(2,1)}, bf16[112,896]{1,0:T(8,128)(2,1)S(1)}, u32[]{:S(2)}, u32[]{:S(2)}) %collective-permute-start.11) | collective-permute-done | bytes 200736 | tf_op jit(solution)/shard_map/ppermute | solution.py:258
  53.8 8.5 %collective-permute-done.12 = bf16[112,896]{1,0:T(8,128)(2,1)S(1)} collective-permute-done((bf16[112,896]{1,0:T(8,128)(2,1)S(1)}, bf16[112,896]{1,0:T(8,128)(2,1)S(1)}, u32[]{:S(2)}, u32[]{:S(2)}) %collective-permute-start.12) | collective-permute-done | bytes 200736 | tf_op jit(solution)/shard_map/ppermute | solution.py:258
  65.8 18.7 %collective-permute-done.13 = bf16[112,896]{1,0:T(8,128)(2,1)S(1)} collective-permute-done((bf16[112,896]{1,0:T(8,128)(2,1)S(1)}, bf16[112,896]{1,0:T(8,128)(2,1)S(1)}, u32[]{:S(2)}, u32[]{:S(2)}) %collective-permute-start.13) | collective-permute-done | bytes 200736 | tf_op jit(solution)/shard_map/ppermute | solution.py:258
  86.0 9.3 %collective-permute-done.5 = bf16[128,1152]{1,0:T(8,128)(2,1)S(1)} collective-permute-done((bf16[128,1152]{1,0:T(8,128)(2,1)S(1)}, bf16[128,1152]{1,0:T(8,128)(2,1)S(1)}, u32[]{:S(2)}, u32[]{:S(2)}) %collective-permute-start.5) | collective-permute-done | bytes 294944 | tf_op jit(solution)/shard_map/ppermute | solution.py:258
  109.4 15.3 %attention_forward.1 = (bf16[896,512]{1,0:T(8,128)(2,1)}, f32[14,8,512]{2,1,0:T(8,128)}) custom-call(s32[1]{0:T(128)} %bitcast.half_ref, s32[1,1024]{1,0:T(1,128)} %doc_row.3, s32[1024,1]{1,0:T(8,128)} %copy.43.doc_col, bf16[896,512]{1,0:T(8,128)(2,1)} %bitcast.261, bf16[256,512]{1,0:T(8,128)(2,1)} %copy-done.28, bf16[256,512]{1,0:T(8,128)(2,1)} %copy-done.50), custom_call_target="tpu_custom_call" | custom-call | flops 15000000512 | bytes 1835008 | tf_op jit(solution)/shard_map/attention_forward/pallas_call | solution.py:106
  124.7 3.1 multiply_reduce_fusion.2
  133.7 13.9 %collective-permute-done.15 = bf16[512,896]{1,0:T(8,128)(2,1)} collective-permute-done((bf16[512,896]{1,0:T(8,128)(2,1)}, bf16[512,896]{1,0:T(8,128)(2,1)}, u32[]{:S(2)}, u32[]{:S(2)}) %collective-permute-start.15) | collective-permute-done | bytes 917536 | tf_op jit(solution)/shard_map/ppermute | solution.py:248
  150.2 1.6 collective-permute-start.18
  151.8 17.4 %collective-permute-done.25 = bf16[512,896]{1,0:T(8,128)(2,1)S(1)} collective-permute-done((bf16[512,896]{1,0:T(8,128)(2,1)S(1)}, bf16[512,896]{1,0:T(8,128)(2,1)S(1)}, u32[]{:S(2)}, u32[]{:S(2)}) %collective-permute-start.25) | collective-permute-done | bytes 917536 | tf_op jit(solution)/shard_map/ppermute | solution.py:248
  173.2 2.2 constant_dynamic-update-slice_fusion.7
  176.4 2.7 collective-permute-done.16
  181.1 5.0 %fusion.116 = f32[512,1216]{0,1:T(8,128)} fusion(bf16[512,896]{1,0:T(8,128)(2,1)} %copy-done.17, bf16[896,1216]{1,0:T(8,128)(2,1)} %all-gather.4.cloned.1.call-done), kind=kOutput, calls=%fused_computation.277 | convolution fusion | flops 1115684864 | bytes 5586944 | tf_op jit(solution)/shard_map/dot_general | solution.py:23
  186.1 4.1 fusion.112
  190.2 5.0 %fusion.117 = f32[512,1216]{0,1:T(8,128)} fusion(bf16[512,896]{1,0:T(8,128)(2,1)} %copy-done.17, bf16[896,1216]{1,0:T(8,128)(2,1)} %all-gather.6.cloned.1.call-done), kind=kOutput, calls=%fused_computation.278 | convolution fusion | flops 1115684864 | bytes 5586944 | tf_op jit(solution)/shard_map/dot_general | solution.py:23
  195.2 4.3 fusion.113
  199.6 4.2 fusion.110
  203.7 4.2 fusion.111
  207.9 7.9 %multiply_convert_fusion = (bf16[512,1216]{0,1:T(8,128)(2,1)}, bf16[512,1216]{0,1:T(8,128)(2,1)S(1)}, bf16[512,1216]{0,1:T(8,128)(2,1)}) fusion(f32[512,1216]{0,1:T(8,128)} %fusion.116, f32[512,1216]{0,1:T(8,128)} %fusion.117, bf16[512,896]{1,0:T(8,128)(2,1)} %copy-done.12, bf16[896,1216]{1,0:T(8,128)(2,1)} %all-gather.8.cloned.1.call-done), kind=kOutput, calls=%fused_computation.35 | convolution fusion | flops 1125023744 | bytes 11812864 | tf_op jit(solution)/shard_map/dot_general | solution.py:23
  215.9 4.0 multiply_convert_fusion.4
  219.9 4.1 multiply_convert_fusion.6
  224.0 3.2 fusion.114
  227.2 2.7 fusion.115
  229.9 5.0 %multiply_convert_fusion.2 = (bf16[512,1216]{0,1:T(8,128)(2,1)}, bf16[512,1216]{0,1:T(8,128)(2,1)S(1)}, bf16[512,1216]{0,1:T(8,128)(2,1)}) fusion(f32[512,1216]{0,1:T(8,128)S(1)} %fusion.114, f32[512,1216]{0,1:T(8,128)S(1)} %fusion.115, bf16[896,1216]{1,0:T(8,128)(2,1)S(1)} %copy-done.47, bf16[256,896]{1,0:T(8,128)(2,1)S(1)} %collective-permute-done.26, ...), kind=kOutput, calls=%fused_computation.37 | convolution fusion | flops 1126858752 | bytes 11812864 | tf_op jit(solution)/shard_map/dot_general | solution.py:23
  236.0 8.6 %fusion.30 = bf16[896,1216]{1,0:T(8,128)(2,1)} fusion(bf16[2048,896]{1,0:T(8,128)(2,1)} %get-tuple-element.78, bf16[512,1216]{0,1:T(8,128)(2,1)S(1)} %get-tuple-element.37, bf16[512,1216]{0,1:T(8,128)(2,1)S(1)} %get-tuple-element.40, bf16[512,1216]{0,1:T(8,128)(2,1)S(1)} %get-tuple-element.34, bf16[512,1216]{0,1:T(8,128)(2,1)S(1)} %get-tuple-element.31), kind=kOutput, calls=%fused_computation.33 | convolution fusion | flops 4483751936 | bytes 10829824 | tf_op jit(solution)/shard_map/dot_general | solution.py:23
  248.3 2.3 constant_dynamic-update-slice_fusion.10
  253.4 1.6 add_convert_fusion.1
  262.5 8.5 %fusion.27 = bf16[896,1216]{1,0:T(8,128)(2,1)} fusion(bf16[2048,896]{1,0:T(8,128)(2,1)} %get-tuple-element.78, bf16[512,1216]{0,1:T(8,128)(2,1)S(1)} %copy-done.68, bf16[512,1216]{0,1:T(8,128)(2,1)S(1)} %copy-done.64, bf16[512,1216]{0,1:T(8,128)(2,1)S(1)} %copy-done.66, bf16[512,1216]{0,1:T(8,128)(2,1)S(1)} %copy-done.51), kind=kOutput, calls=%fused_computation.32 | convolution fusion | flops 4483751936 | bytes 10829824 | tf_op jit(solution)/shard_map/dot_general | solution.py:23
  271.3 3.8 fusion.121
  278.7 1.6 add_convert_fusion
  280.3 1.6 add_convert_fusion.2
  293.0 1.6 collective-permute-start.20
  294.6 2.0 convolution_convert_fusion.4
  296.6 5.3 %collective-permute-done.30 = bf16[512,896]{1,0:T(8,128)(2,1)S(1)} collective-permute-done((bf16[512,896]{1,0:T(8,128)(2,1)S(1)}, bf16[512,896]{1,0:T(8,128)(2,1)S(1)}, u32[]{:S(2)}, u32[]{:S(2)}) %collective-permute-start.30) | collective-permute-done | bytes 917536 | tf_op jit(solution)/shard_map/ppermute | solution.py:248
  302.0 3.0 collective-permute-done.28
  305.0 2.2 multiply_reduce_fusion
  307.2 14.4 %collective-permute-done.22 = bf16[512,896]{1,0:T(8,128)(2,1)S(1)} collective-permute-done((bf16[512,896]{1,0:T(8,128)(2,1)S(1)}, bf16[512,896]{1,0:T(8,128)(2,1)S(1)}, u32[]{:S(2)}, u32[]{:S(2)}) %collective-permute-start.22) | collective-permute-done | bytes 917536 | tf_op jit(solution)/shard_map/ppermute | solution.py:248
  321.6 3.0 collective-permute-done.20
  324.7 2.1 multiply_subtract_fusion
  326.7 2.1 convolution_convert_fusion.grad_t
  329.9 16.2 %attention_backward.1 = (f32[896,512]{1,0:T(8,128)}, f32[2,1024,64]{2,1,0:T(8,128)}, f32[2,1024,64]{2,1,0:T(8,128)}) custom-call(s32[1]{0:T(128)} %bitcast.half_ref, s32[1,1024]{1,0:T(1,128)} %doc_row.3, s32[1024,1]{1,0:T(8,128)} %copy.43.doc_col, bf16[896,512]{1,0:T(8,128)(2,1)} %bitcast.262, bf16[256,512]{1,0:T(8,128)(2,1)} %copy-done.28, ...), custom_call_target="tpu_custom_call" | custom-call | flops 35000000512 | bytes 3670016 | tf_op jit(solution)/shard_map/attention_backward/pallas_call | solution.py:197
  349.9 15.6 %collective-permute-start.31 = (bf16[4,512,64]{2,1,0:T(8,128)(2,1)}, bf16[4,512,64]{2,1,0:T(8,128)(2,1)}, u32[]{:S(2)}, u32[]{:S(2)}) collective-permute-start(bf16[4,512,64]{2,1,0:T(8,128)(2,1)} %select_convert_fusion), channel_id=1, source_target_pairs={{0,4},{4,0},{1,5},{5,1},{2,6},{6,2},{3,7},{7,3},{8,12},{12,8},{9,1... | collective-permute-start | bytes 786440 | tf_op jit(solution)/shard_map/ppermute | solution.py:245
  368.5 1.8 copy-done.9
  376.2 4.5 fusion.45
  381.0 1.6 fusion.64
  384.2 2.0 copy-done.4
  386.3 2.1 bitcast_add_fusion.1
  392.8 8.4 %fusion.24 = bf16[896,1216]{1,0:T(8,128)(2,1)} fusion(bf16[2048,896]{1,0:T(8,128)(2,1)} %constant_dynamic-update-slice_fusion.9, bf16[512,1216]{0,1:T(8,128)(2,1)S(1)} %copy-done.76, bf16[512,1216]{0,1:T(8,128)(2,1)S(1)} %copy-done.70, bf16[512,1216]{0,1:T(8,128)(2,1)S(1)} %copy-done.72, bf16[512,1216]{0,1:T(8,128)(2,1)S(1)} %copy-done.74), kind=kOutput, calls=%fused_computation.31 | convolution fusion | flops 4483751936 | bytes 10829824 | tf_op jit(solution)/shard_map/dot_general | solution.py:23
  406.2 4.0 collective-permute-start.52
  411.5 4.8 collective-permute-start.50
  416.3 2.3 bitcast_add_fusion
  423.9 4.1 collective-permute-done.49
  428.0 1.6 collective-permute-start.55
  432.4 3.2 collective-permute-done.34
  441.0 7.9 %collective-permute-start.39 = (bf16[32,1152]{1,0:T(8,128)(2,1)S(1)}, bf16[32,1152]{1,0:T(8,128)(2,1)S(1)}, u32[]{:S(2)}, u32[]{:S(2)}) collective-permute-start(bf16[32,1152]{1,0:T(8,128)(2,1)S(1)} %get-tuple-element.75), channel_id=1, source_target_pairs={{0,16},{8,24},{1,17},{9,25},{2,18},{10,26},{3,19},{11,27},{4,20},{... | collective-permute-start | bytes 221192 | tf_op jit(solution)/shard_map/ppermute | solution.py:295
  450.2 6.9 %collective-permute-start.37 = (bf16[32,1152]{1,0:T(8,128)(2,1)S(1)}, bf16[32,1152]{1,0:T(8,128)(2,1)S(1)}, u32[]{:S(2)}, u32[]{:S(2)}) collective-permute-start(bf16[32,1152]{1,0:T(8,128)(2,1)S(1)} %get-tuple-element.77), channel_id=1, source_target_pairs={{0,24},{1,25},{2,26},{3,27},{4,28},{5,29},{6,30},{7,31}} | collective-permute-start | bytes 221192 | tf_op jit(solution)/shard_map/ppermute | solution.py:295
  459.0 6.1 %collective-permute-done.36 = bf16[32,1152]{1,0:T(8,128)(2,1)S(1)} collective-permute-done((bf16[32,1152]{1,0:T(8,128)(2,1)S(1)}, bf16[32,1152]{1,0:T(8,128)(2,1)S(1)}, u32[]{:S(2)}, u32[]{:S(2)}) %collective-permute-start.36) | collective-permute-done | bytes 73760 | tf_op jit(solution)/shard_map/ppermute | solution.py:295
  474.5 1.8 convert_element_type.489
  476.3 1.8 convert_element_type.491
  478.1 1.8 convert_bitcast_fusion.1
  (391 shorter events, 125.4 us)
Async XLA Ops:
  7.2 173.9 %all-gather.4.cloned.1.call-start = ((), (), s32[]{:S(2)}) async-start(), calls=%async_computation.3 | async-start | bytes 2580480 | tf_op jit(solution)/shard_map/all_gather | solution.py:399
  7.9 182.3 %all-gather.6.cloned.1.call-start = ((), (), s32[]{:S(2)}) async-start(), calls=%async_computation.4 | async-start | bytes 2580480 | tf_op jit(solution)/shard_map/all_gather | solution.py:400
  8.0 15.7 %collective-permute-start.8 = (bf16[112,896]{1,0:T(8,128)(2,1)}, bf16[112,896]{1,0:T(8,128)(2,1)S(1)}, u32[]{:S(2)}, u32[]{:S(2)}) collective-permute-start(bf16[112,896]{1,0:T(8,128)(2,1)} %param.23), channel_id=1, source_target_pairs={{0,8},{8,16},{16,24},{1,9},{9,17},{17,25},{2,10},{10,18},{18,26},{... | collective-permute-start | bytes 602120 | tf_op jit(solution)/shard_map/ppermute | solution.py:257
  17.6 16.7 %collective-permute-start = (bf16[128,1152]{1,0:T(8,128)(2,1)S(1)}, bf16[128,1152]{1,0:T(8,128)(2,1)S(1)}, u32[]{:S(2)}, u32[]{:S(2)}) collective-permute-start(bf16[128,1152]{1,0:T(8,128)(2,1)S(1)} %maximum_maximum_fusion.1), channel_id=1, source_target_pairs={{0,8},{8,16},{16,24},{1,9},{9,17},{17,25},{2,10},{10,18},{18,26},{... | collective-permute-start | bytes 884744 | tf_op jit(solution)/shard_map/ppermute | solution.py:257
  21.1 22.9 %collective-permute-start.3 = (bf16[128,1152]{1,0:T(8,128)(2,1)S(1)}, bf16[128,1152]{1,0:T(8,128)(2,1)S(1)}, u32[]{:S(2)}, u32[]{:S(2)}) collective-permute-start(bf16[128,1152]{1,0:T(8,128)(2,1)S(1)} %maximum_maximum_fusion.1), channel_id=1, source_target_pairs={{8,0},{16,8},{24,16},{9,1},{17,9},{25,17},{10,2},{18,10},{26,18},{... | collective-permute-start | bytes 884744 | tf_op jit(solution)/shard_map/ppermute | solution.py:258
  22.4 29.4 %collective-permute-start.11 = (bf16[112,896]{1,0:T(8,128)(2,1)}, bf16[112,896]{1,0:T(8,128)(2,1)S(1)}, u32[]{:S(2)}, u32[]{:S(2)}) collective-permute-start(bf16[112,896]{1,0:T(8,128)(2,1)} %param.23), channel_id=1, source_target_pairs={{8,0},{16,8},{24,16},{9,1},{17,9},{25,17},{10,2},{18,10},{26,18},{... | collective-permute-start | bytes 602120 | tf_op jit(solution)/shard_map/ppermute | solution.py:258
  23.7 29.3 %collective-permute-start.9 = (bf16[112,896]{1,0:T(8,128)(2,1)S(1)}, bf16[112,896]{1,0:T(8,128)(2,1)S(1)}, u32[]{:S(2)}, u32[]{:S(2)}) collective-permute-start(bf16[112,896]{1,0:T(8,128)(2,1)S(1)} %collective-permute-done.8), channel_id=1, source_target_pairs={{8,16},{16,24},{9,17},{17,25},{10,18},{18,26},{11,19},{19,27},{12,... | collective-permute-start | bytes 602120 | tf_op jit(solution)/shard_map/ppermute | solution.py:257
  34.2 29.3 %collective-permute-start.1 = (bf16[128,1152]{1,0:T(8,128)(2,1)S(1)}, bf16[128,1152]{1,0:T(8,128)(2,1)S(1)}, u32[]{:S(2)}, u32[]{:S(2)}) collective-permute-start(bf16[128,1152]{1,0:T(8,128)(2,1)S(1)} %collective-permute-done), channel_id=1, source_target_pairs={{8,16},{16,24},{9,17},{17,25},{10,18},{18,26},{11,19},{19,27},{12,... | collective-permute-start | bytes 884744 | tf_op jit(solution)/shard_map/ppermute | solution.py:257
  44.0 20.3 %collective-permute-start.4 = (bf16[128,1152]{1,0:T(8,128)(2,1)S(1)}, bf16[128,1152]{1,0:T(8,128)(2,1)S(1)}, u32[]{:S(2)}, u32[]{:S(2)}) collective-permute-start(bf16[128,1152]{1,0:T(8,128)(2,1)S(1)} %collective-permute-done.3), channel_id=1, source_target_pairs={{8,0},{16,8},{9,1},{17,9},{10,2},{18,10},{11,3},{19,11},{12,4},{20... | collective-permute-start | bytes 884744 | tf_op jit(solution)/shard_map/ppermute | solution.py:258
  51.7 10.6 %collective-permute-start.12 = (bf16[112,896]{1,0:T(8,128)(2,1)S(1)}, bf16[112,896]{1,0:T(8,128)(2,1)S(1)}, u32[]{:S(2)}, u32[]{:S(2)}) collective-permute-start(bf16[112,896]{1,0:T(8,128)(2,1)S(1)} %collective-permute-done.11), channel_id=1, source_target_pairs={{8,0},{16,8},{9,1},{17,9},{10,2},{18,10},{11,3},{19,11},{12,4},{20... | collective-permute-start | bytes 602120 | tf_op jit(solution)/shard_map/ppermute | solution.py:258
  53.0 12.6 %collective-permute-start.10 = (bf16[112,896]{1,0:T(8,128)(2,1)S(1)}, bf16[112,896]{1,0:T(8,128)(2,1)S(1)}, u32[]{:S(2)}, u32[]{:S(2)}) collective-permute-start(bf16[112,896]{1,0:T(8,128)(2,1)S(1)} %collective-permute-done.9), channel_id=1, source_target_pairs={{16,24},{17,25},{18,26},{19,27},{20,28},{21,29},{22,30},{23,31}} | collective-permute-start | bytes 602120 | tf_op jit(solution)/shard_map/ppermute | solution.py:257
  53.7 154.2 %all-gather.8.cloned.1.call-start = ((), (), s32[]{:S(2)}) async-start(), calls=%async_computation.5 | async-start | bytes 2580480 | tf_op jit(solution)/shard_map/all_gather | solution.py:401
  62.3 22.2 %collective-permute-start.13 = (bf16[112,896]{1,0:T(8,128)(2,1)S(1)}, bf16[112,896]{1,0:T(8,128)(2,1)S(1)}, u32[]{:S(2)}, u32[]{:S(2)}) collective-permute-start(bf16[112,896]{1,0:T(8,128)(2,1)S(1)} %collective-permute-done.12), channel_id=1, source_target_pairs={{8,0},{9,1},{10,2},{11,3},{12,4},{13,5},{14,6},{15,7}} | collective-permute-start | bytes 602120 | tf_op jit(solution)/shard_map/ppermute | solution.py:258
  63.6 22.0 %collective-permute-start.2 = (bf16[128,1152]{1,0:T(8,128)(2,1)S(1)}, bf16[128,1152]{1,0:T(8,128)(2,1)S(1)}, u32[]{:S(2)}, u32[]{:S(2)}) collective-permute-start(bf16[128,1152]{1,0:T(8,128)(2,1)S(1)} %collective-permute-done.1), channel_id=1, source_target_pairs={{16,24},{17,25},{18,26},{19,27},{20,28},{21,29},{22,30},{23,31}} | collective-permute-start | bytes 884744 | tf_op jit(solution)/shard_map/ppermute | solution.py:257
  64.3 31.0 %collective-permute-start.5 = (bf16[128,1152]{1,0:T(8,128)(2,1)S(1)}, bf16[128,1152]{1,0:T(8,128)(2,1)S(1)}, u32[]{:S(2)}, u32[]{:S(2)}) collective-permute-start(bf16[128,1152]{1,0:T(8,128)(2,1)S(1)} %collective-permute-done.4), channel_id=1, source_target_pairs={{8,0},{9,1},{10,2},{11,3},{12,4},{13,5},{14,6},{15,7}} | collective-permute-start | bytes 884744 | tf_op jit(solution)/shard_map/ppermute | solution.py:258
  85.6 13.7 %collective-permute-start.14 = (bf16[4,112,896]{2,1,0:T(8,128)(2,1)}, bf16[4,112,896]{2,1,0:T(8,128)(2,1)}, u32[]{:S(2)}, u32[]{:S(2)}) collective-permute-start(bf16[4,112,896]{2,1,0:T(8,128)(2,1)} %constant_dynamic-slice_fusion), channel_id=1, source_target_pairs={{0,4},{4,0},{1,5},{5,1},{2,6},{6,2},{3,7},{7,3},{8,12},{12,8},{9,1... | collective-permute-start | bytes 2408456 | tf_op jit(solution)/shard_map/ppermute | solution.py:245
  96.5 5.8 %collective-permute-start.6 = (bf16[4,128,1152]{2,1,0:T(8,128)(2,1)}, bf16[4,128,1152]{2,1,0:T(8,128)(2,1)}, u32[]{:S(2)}, u32[]{:S(2)}) collective-permute-start(bf16[4,128,1152]{2,1,0:T(8,128)(2,1)} %constant_dynamic-slice_fusion.1), channel_id=1, source_target_pairs={{0,4},{4,0},{1,5},{5,1},{2,6},{6,2},{3,7},{7,3},{8,12},{12,8},{9,1... | collective-permute-start | bytes 3538952 | tf_op jit(solution)/shard_map/ppermute | solution.py:245
  106.6 2.0 collective-permute-start.7
  129.3 18.3 %collective-permute-start.15 = (bf16[512,896]{1,0:T(8,128)(2,1)}, bf16[512,896]{1,0:T(8,128)(2,1)}, u32[]{:S(2)}, u32[]{:S(2)}) collective-permute-start(bf16[512,896]{1,0:T(8,128)(2,1)} %get-tuple-element.29), channel_id=1, source_target_pairs={{0,1},{1,0},{2,3},{3,2},{4,5},{5,4},{6,7},{7,6},{8,9},{9,8},{10,11... | collective-permute-start | bytes 2752520 | tf_op jit(solution)/shard_map/ppermute | solution.py:248
  130.8 343.7 %reduce-scatter.4.cloned.1.call-start = ((), (), s32[]{:S(2)}) async-start(), calls=%async_computation.6 | async-start | bytes 2580480 | tf_op jit(solution)/shard_map/reduce_scatter | solution.py:449
  131.0 19.2 %collective-permute-start.17 = (bf16[512,896]{1,0:T(8,128)(2,1)}, bf16[512,896]{1,0:T(8,128)(2,1)S(1)}, u32[]{:S(2)}, u32[]{:S(2)}) collective-permute-start(bf16[512,896]{1,0:T(8,128)(2,1)} %get-tuple-element.29), channel_id=1, source_target_pairs={{0,2},{1,3},{2,0},{3,1},{4,6},{5,7},{6,4},{7,5},{8,10},{9,11},{10,... | collective-permute-start | bytes 2752520 | tf_op jit(solution)/shard_map/ppermute | solution.py:248
  132.6 36.7 %collective-permute-start.25 = (bf16[512,896]{1,0:T(8,128)(2,1)S(1)}, bf16[512,896]{1,0:T(8,128)(2,1)S(1)}, u32[]{:S(2)}, u32[]{:S(2)}) collective-permute-start(bf16[512,896]{1,0:T(8,128)(2,1)S(1)} %copy-done.10), channel_id=1, source_target_pairs={{0,2},{1,3},{2,0},{3,1},{4,6},{5,7},{6,4},{7,5},{8,10},{9,11},{10,... | collective-permute-start | bytes 2752520 | tf_op jit(solution)/shard_map/ppermute | solution.py:248
  133.1 37.5 %collective-permute-start.23 = (bf16[512,896]{1,0:T(8,128)(2,1)S(1)}, bf16[512,896]{1,0:T(8,128)(2,1)S(1)}, u32[]{:S(2)}, u32[]{:S(2)}) collective-permute-start(bf16[512,896]{1,0:T(8,128)(2,1)S(1)} %copy-done.10), channel_id=1, source_target_pairs={{0,1},{1,0},{2,3},{3,2},{4,5},{5,4},{6,7},{7,6},{8,9},{9,8},{10,11... | collective-permute-start | bytes 2752520 | tf_op jit(solution)/shard_map/ppermute | solution.py:248
  148.7 30.4 %collective-permute-start.16 = (bf16[256,896]{1,0:T(8,128)(2,1)S(1)}, bf16[256,896]{1,0:T(8,128)(2,1)S(1)}, u32[]{:S(2)}, u32[]{:S(2)}) collective-permute-start(bf16[256,896]{1,0:T(8,128)(2,1)S(1)} %slice.214), channel_id=1, source_target_pairs={{0,2},{1,3},{2,0},{3,1},{4,6},{5,7},{6,4},{7,5},{8,10},{9,11},{10,... | collective-permute-start | bytes 1376264 | tf_op jit(solution)/shard_map/ppermute | solution.py:248
  150.2 29.8 %collective-permute-start.18 = (bf16[256,896]{1,0:T(8,128)(2,1)S(1)}, bf16[256,896]{1,0:T(8,128)(2,1)S(1)}, u32[]{:S(2)}, u32[]{:S(2)}) collective-permute-start(bf16[256,896]{1,0:T(8,128)(2,1)S(1)} %slice.215), channel_id=1, source_target_pairs={{0,1},{1,0},{2,3},{3,2},{4,5},{5,4},{6,7},{7,6},{8,9},{9,8},{10,11... | collective-permute-start | bytes 1376264 | tf_op jit(solution)/shard_map/ppermute | solution.py:248
  170.1 59.8 %collective-permute-start.26 = (bf16[256,896]{1,0:T(8,128)(2,1)}, bf16[256,896]{1,0:T(8,128)(2,1)S(1)}, u32[]{:S(2)}, u32[]{:S(2)}) collective-permute-start(bf16[256,896]{1,0:T(8,128)(2,1)} %slice.223), channel_id=1, source_target_pairs={{0,1},{1,0},{2,3},{3,2},{4,5},{5,4},{6,7},{7,6},{8,9},{9,8},{10,11... | collective-permute-start | bytes 1376264 | tf_op jit(solution)/shard_map/ppermute | solution.py:248
  171.7 58.2 %collective-permute-start.24 = (bf16[256,896]{1,0:T(8,128)(2,1)}, bf16[256,896]{1,0:T(8,128)(2,1)}, u32[]{:S(2)}, u32[]{:S(2)}) collective-permute-start(bf16[256,896]{1,0:T(8,128)(2,1)} %slice.222), channel_id=1, source_target_pairs={{0,2},{1,3},{2,0},{3,1},{4,6},{5,7},{6,4},{7,5},{8,10},{9,11},{10,... | collective-permute-start | bytes 1376264 | tf_op jit(solution)/shard_map/ppermute | solution.py:248
  244.6 231.7 %reduce-scatter.6.cloned.1.call-start = ((), (), s32[]{:S(2)}) async-start(), calls=%async_computation.7 | async-start | bytes 2580480 | tf_op jit(solution)/shard_map/reduce_scatter | solution.py:449
  256.0 29.5 %collective-permute-start.29 = (bf16[256,896]{1,0:T(8,128)(2,1)}, bf16[256,896]{1,0:T(8,128)(2,1)}, u32[]{:S(2)}, u32[]{:S(2)}) collective-permute-start(bf16[256,896]{1,0:T(8,128)(2,1)} %get-tuple-element.63), channel_id=1, source_target_pairs={{0,1},{1,0},{2,3},{3,2},{4,5},{5,4},{6,7},{7,6},{8,9},{9,8},{10,11... | collective-permute-start | bytes 1376264 | tf_op jit(solution)/shard_map/ppermute | solution.py:248
  256.5 31.7 %collective-permute-start.27 = (bf16[256,896]{1,0:T(8,128)(2,1)}, bf16[256,896]{1,0:T(8,128)(2,1)}, u32[]{:S(2)}, u32[]{:S(2)}) collective-permute-start(bf16[256,896]{1,0:T(8,128)(2,1)} %get-tuple-element.62), channel_id=1, source_target_pairs={{0,2},{1,3},{2,0},{3,1},{4,6},{5,7},{6,4},{7,5},{8,10},{9,11},{10,... | collective-permute-start | bytes 1376264 | tf_op jit(solution)/shard_map/ppermute | solution.py:248
  260.4 29.6 %collective-permute-start.21 = (bf16[256,896]{1,0:T(8,128)(2,1)}, bf16[256,896]{1,0:T(8,128)(2,1)}, u32[]{:S(2)}, u32[]{:S(2)}) collective-permute-start(bf16[256,896]{1,0:T(8,128)(2,1)} %get-tuple-element.69), channel_id=1, source_target_pairs={{0,1},{1,0},{2,3},{3,2},{4,5},{5,4},{6,7},{7,6},{8,9},{9,8},{10,11... | collective-permute-start | bytes 1376264 | tf_op jit(solution)/shard_map/ppermute | solution.py:248
  261.9 29.9 %collective-permute-start.19 = (bf16[256,896]{1,0:T(8,128)(2,1)S(1)}, bf16[256,896]{1,0:T(8,128)(2,1)}, u32[]{:S(2)}, u32[]{:S(2)}) collective-permute-start(bf16[256,896]{1,0:T(8,128)(2,1)S(1)} %get-tuple-element.68), channel_id=1, source_target_pairs={{0,2},{1,3},{2,0},{3,1},{4,6},{5,7},{6,4},{7,5},{8,10},{9,11},{10,... | collective-permute-start | bytes 1376264 | tf_op jit(solution)/shard_map/ppermute | solution.py:248
  271.0 207.1 %reduce-scatter.8.cloned.1.call-start = ((), (), s32[]{:S(2)}) async-start(), calls=%async_computation.8 | async-start | bytes 2580480 | tf_op jit(solution)/shard_map/reduce_scatter | solution.py:449
  286.7 15.3 %collective-permute-start.30 = (bf16[512,896]{1,0:T(8,128)(2,1)S(1)}, bf16[512,896]{1,0:T(8,128)(2,1)S(1)}, u32[]{:S(2)}, u32[]{:S(2)}) collective-permute-start(bf16[512,896]{1,0:T(8,128)(2,1)S(1)} %pad_maximum_fusion.7), channel_id=1, source_target_pairs={{0,2},{1,3},{2,0},{3,1},{4,6},{5,7},{6,4},{7,5},{8,10},{9,11},{10,... | collective-permute-start | bytes 2752520 | tf_op jit(solution)/shard_map/ppermute | solution.py:248
  289.5 15.5 %collective-permute-start.28 = (bf16[512,896]{1,0:T(8,128)(2,1)S(1)}, bf16[512,896]{1,0:T(8,128)(2,1)S(1)}, u32[]{:S(2)}, u32[]{:S(2)}) collective-permute-start(bf16[512,896]{1,0:T(8,128)(2,1)S(1)} %pad_maximum_fusion.6), channel_id=1, source_target_pairs={{0,1},{1,0},{2,3},{3,2},{4,5},{5,4},{6,7},{7,6},{8,9},{9,8},{10,11... | collective-permute-start | bytes 2752520 | tf_op jit(solution)/shard_map/ppermute | solution.py:248
  291.2 30.4 %collective-permute-start.22 = (bf16[512,896]{1,0:T(8,128)(2,1)S(1)}, bf16[512,896]{1,0:T(8,128)(2,1)S(1)}, u32[]{:S(2)}, u32[]{:S(2)}) collective-permute-start(bf16[512,896]{1,0:T(8,128)(2,1)S(1)} %pad_maximum_fusion.5), channel_id=1, source_target_pairs={{0,2},{1,3},{2,0},{3,1},{4,6},{5,7},{6,4},{7,5},{8,10},{9,11},{10,... | collective-permute-start | bytes 2752520 | tf_op jit(solution)/shard_map/ppermute | solution.py:248
  293.0 31.6 %collective-permute-start.20 = (bf16[512,896]{1,0:T(8,128)(2,1)S(1)}, bf16[512,896]{1,0:T(8,128)(2,1)S(1)}, u32[]{:S(2)}, u32[]{:S(2)}) collective-permute-start(bf16[512,896]{1,0:T(8,128)(2,1)S(1)} %pad_maximum_fusion.4), channel_id=1, source_target_pairs={{0,1},{1,0},{2,3},{3,2},{4,5},{5,4},{6,7},{7,6},{8,9},{9,8},{10,11... | collective-permute-start | bytes 2752520 | tf_op jit(solution)/shard_map/ppermute | solution.py:248
  349.9 21.0 %collective-permute-start.31 = (bf16[4,512,64]{2,1,0:T(8,128)(2,1)}, bf16[4,512,64]{2,1,0:T(8,128)(2,1)}, u32[]{:S(2)}, u32[]{:S(2)}) collective-permute-start(bf16[4,512,64]{2,1,0:T(8,128)(2,1)} %select_convert_fusion), channel_id=1, source_target_pairs={{0,4},{4,0},{1,5},{5,1},{2,6},{6,2},{3,7},{7,3},{8,12},{12,8},{9,1... | collective-permute-start | bytes 786440 | tf_op jit(solution)/shard_map/ppermute | solution.py:245
  368.5 15.7 %collective-permute-start.45 = (bf16[4,128,896]{2,1,0:T(8,128)(2,1)}, bf16[4,128,896]{2,1,0:T(8,128)(2,1)}, u32[]{:S(2)}, u32[]{:S(2)}) collective-permute-start(bf16[4,128,896]{2,1,0:T(8,128)(2,1)} %fusion.49), channel_id=1, source_target_pairs={{0,4},{4,0},{1,5},{5,1},{2,6},{6,2},{3,7},{7,3},{8,12},{12,8},{9,1... | collective-permute-start | bytes 2752520 | tf_op jit(solution)/shard_map/ppermute | solution.py:245
  384.1 27.4 %collective-permute-start.32 = (bf16[4,128,1152]{2,1,0:T(8,128)(2,1)}, bf16[4,128,1152]{2,1,0:T(8,128)(2,1)}, u32[]{:S(2)}, u32[]{:S(2)}) collective-permute-start(bf16[4,128,1152]{2,1,0:T(8,128)(2,1)} %fusion.48), channel_id=1, source_target_pairs={{0,4},{4,0},{1,5},{5,1},{2,6},{6,2},{3,7},{7,3},{8,12},{12,8},{9,1... | collective-permute-start | bytes 3538952 | tf_op jit(solution)/shard_map/ppermute | solution.py:245
  389.3 12.0 %collective-permute-start.48 = (bf16[4,32,896]{2,1,0:T(8,128)(2,1)}, bf16[4,32,896]{2,1,0:T(8,128)(2,1)S(1)}, u32[]{:S(2)}, u32[]{:S(2)}) collective-permute-start(bf16[4,32,896]{2,1,0:T(8,128)(2,1)} %get-tuple-element.52), channel_id=1, source_target_pairs={{0,3},{1,2},{2,1},{3,0},{4,7},{5,6},{6,5},{7,4},{8,11},{9,10},{10,... | collective-permute-start | bytes 688136 | tf_op jit(solution)/shard_map/ppermute | solution.py:248
  389.7 12.4 %collective-permute-start.47 = (bf16[4,32,896]{2,1,0:T(8,128)(2,1)}, bf16[4,32,896]{2,1,0:T(8,128)(2,1)S(1)}, u32[]{:S(2)}, u32[]{:S(2)}) collective-permute-start(bf16[4,32,896]{2,1,0:T(8,128)(2,1)} %get-tuple-element.53), channel_id=1, source_target_pairs={{0,2},{1,3},{2,0},{3,1},{4,6},{5,7},{6,4},{7,5},{8,10},{9,11},{10,... | collective-permute-start | bytes 688136 | tf_op jit(solution)/shard_map/ppermute | solution.py:248
  391.2 10.9 %collective-permute-start.46 = (bf16[4,32,896]{2,1,0:T(8,128)(2,1)S(1)}, bf16[4,32,896]{2,1,0:T(8,128)(2,1)}, u32[]{:S(2)}, u32[]{:S(2)}) collective-permute-start(bf16[4,32,896]{2,1,0:T(8,128)(2,1)S(1)} %get-tuple-element.51), channel_id=1, source_target_pairs={{0,1},{1,0},{2,3},{3,2},{4,5},{5,4},{6,7},{7,6},{8,9},{9,8},{10,11... | collective-permute-start | bytes 688136 | tf_op jit(solution)/shard_map/ppermute | solution.py:248
  403.4 15.4 %collective-permute-start.54 = (bf16[32,896]{1,0:T(8,128)(2,1)S(1)}, bf16[32,896]{1,0:T(8,128)(2,1)S(1)}, u32[]{:S(2)}, u32[]{:S(2)}) collective-permute-start(bf16[32,896]{1,0:T(8,128)(2,1)S(1)} %get-tuple-element.83), channel_id=1, source_target_pairs={{0,8},{8,16},{16,24},{1,9},{9,17},{17,25},{2,10},{10,18},{18,26},{... | collective-permute-start | bytes 172040 | tf_op jit(solution)/shard_map/ppermute | solution.py:295
  404.9 15.4 %collective-permute-start.53 = (bf16[32,896]{1,0:T(8,128)(2,1)S(1)}, bf16[32,896]{1,0:T(8,128)(2,1)S(1)}, u32[]{:S(2)}, u32[]{:S(2)}) collective-permute-start(bf16[32,896]{1,0:T(8,128)(2,1)S(1)} %get-tuple-element.84), channel_id=1, source_target_pairs={{8,0},{16,8},{24,16},{9,1},{17,9},{25,17},{10,2},{18,10},{26,18},{... | collective-permute-start | bytes 172040 | tf_op jit(solution)/shard_map/ppermute | solution.py:295
  406.2 15.5 %collective-permute-start.52 = (bf16[32,896]{1,0:T(8,128)(2,1)S(1)}, bf16[32,896]{1,0:T(8,128)(2,1)S(1)}, u32[]{:S(2)}, u32[]{:S(2)}) collective-permute-start(bf16[32,896]{1,0:T(8,128)(2,1)S(1)} %get-tuple-element.85), channel_id=1, source_target_pairs={{0,16},{8,24},{1,17},{9,25},{2,18},{10,26},{3,19},{11,27},{4,20},{... | collective-permute-start | bytes 172040 | tf_op jit(solution)/shard_map/ppermute | solution.py:295
  410.2 12.9 %collective-permute-start.51 = (bf16[32,896]{1,0:T(8,128)(2,1)S(1)}, bf16[32,896]{1,0:T(8,128)(2,1)S(1)}, u32[]{:S(2)}, u32[]{:S(2)}) collective-permute-start(bf16[32,896]{1,0:T(8,128)(2,1)S(1)} %get-tuple-element.86), channel_id=1, source_target_pairs={{16,0},{24,8},{17,1},{25,9},{18,2},{26,10},{19,3},{27,11},{20,4},{... | collective-permute-start | bytes 172040 | tf_op jit(solution)/shard_map/ppermute | solution.py:295
  411.5 12.4 %collective-permute-start.50 = (bf16[32,896]{1,0:T(8,128)(2,1)S(1)}, bf16[32,896]{1,0:T(8,128)(2,1)S(1)}, u32[]{:S(2)}, u32[]{:S(2)}) collective-permute-start(bf16[32,896]{1,0:T(8,128)(2,1)S(1)} %get-tuple-element.87), channel_id=1, source_target_pairs={{0,24},{1,25},{2,26},{3,27},{4,28},{5,29},{6,30},{7,31}} | collective-permute-start | bytes 172040 | tf_op jit(solution)/shard_map/ppermute | solution.py:295
  418.8 9.2 %collective-permute-start.49 = (bf16[32,896]{1,0:T(8,128)(2,1)S(1)}, bf16[32,896]{1,0:T(8,128)(2,1)S(1)}, u32[]{:S(2)}, u32[]{:S(2)}) collective-permute-start(bf16[32,896]{1,0:T(8,128)(2,1)S(1)} %get-tuple-element.82), channel_id=1, source_target_pairs={{24,0},{25,1},{26,2},{27,3},{28,4},{29,5},{30,6},{31,7}} | collective-permute-start | bytes 172040 | tf_op jit(solution)/shard_map/ppermute | solution.py:295
  420.3 10.9 %collective-permute-start.35 = (bf16[4,32,1152]{2,1,0:T(8,128)(2,1)S(1)}, bf16[4,32,1152]{2,1,0:T(8,128)(2,1)S(1)}, u32[]{:S(2)}, u32[]{:S(2)}) collective-permute-start(bf16[4,32,1152]{2,1,0:T(8,128)(2,1)S(1)} %get-tuple-element.43), channel_id=1, source_target_pairs={{0,3},{1,2},{2,1},{3,0},{4,7},{5,6},{6,5},{7,4},{8,11},{9,10},{10,... | collective-permute-start | bytes 884744 | tf_op jit(solution)/shard_map/ppermute | solution.py:248
  421.7 13.9 %collective-permute-start.34 = (bf16[4,32,1152]{2,1,0:T(8,128)(2,1)S(1)}, bf16[4,32,1152]{2,1,0:T(8,128)(2,1)S(1)}, u32[]{:S(2)}, u32[]{:S(2)}) collective-permute-start(bf16[4,32,1152]{2,1,0:T(8,128)(2,1)S(1)} %get-tuple-element.44), channel_id=1, source_target_pairs={{0,2},{1,3},{2,0},{3,1},{4,6},{5,7},{6,4},{7,5},{8,10},{9,11},{10,... | collective-permute-start | bytes 884744 | tf_op jit(solution)/shard_map/ppermute | solution.py:248
  423.1 13.6 %collective-permute-start.33 = (bf16[4,32,1152]{2,1,0:T(8,128)(2,1)S(1)}, bf16[4,32,1152]{2,1,0:T(8,128)(2,1)S(1)}, u32[]{:S(2)}, u32[]{:S(2)}) collective-permute-start(bf16[4,32,1152]{2,1,0:T(8,128)(2,1)S(1)} %get-tuple-element.42), channel_id=1, source_target_pairs={{0,1},{1,0},{2,3},{3,2},{4,5},{5,4},{6,7},{7,6},{8,9},{9,8},{10,11... | collective-permute-start | bytes 884744 | tf_op jit(solution)/shard_map/ppermute | solution.py:248
  428.0 12.9 %collective-permute-start.55 = (bf16[32,896]{1,0:T(8,128)(2,1)S(1)}, bf16[32,896]{1,0:T(8,128)(2,1)S(1)}, u32[]{:S(2)}, u32[]{:S(2)}) collective-permute-start(bf16[32,896]{1,0:T(8,128)(2,1)S(1)} %fusion.82), channel_id=1, source_target_pairs={{0,3},{1,2},{2,1},{3,0},{4,7},{5,6},{6,5},{7,4},{8,11},{9,10},{10,... | collective-permute-start | bytes 172040 | tf_op jit(solution)/shard_map/ppermute | solution.py:248
  429.7 19.2 %collective-permute-start.56 = (bf16[32,896]{1,0:T(8,128)(2,1)S(1)}, bf16[32,896]{1,0:T(8,128)(2,1)S(1)}, u32[]{:S(2)}, u32[]{:S(2)}) collective-permute-start(bf16[32,896]{1,0:T(8,128)(2,1)S(1)} %fusion.82), channel_id=1, source_target_pairs={{0,2},{1,3},{2,0},{3,1},{4,6},{5,7},{6,4},{7,5},{8,10},{9,11},{10,... | collective-permute-start | bytes 172040 | tf_op jit(solution)/shard_map/ppermute | solution.py:248
  431.2 19.0 %collective-permute-start.57 = (bf16[32,896]{1,0:T(8,128)(2,1)S(1)}, bf16[32,896]{1,0:T(8,128)(2,1)S(1)}, u32[]{:S(2)}, u32[]{:S(2)}) collective-permute-start(bf16[32,896]{1,0:T(8,128)(2,1)S(1)} %fusion.82), channel_id=1, source_target_pairs={{0,1},{1,0},{2,3},{3,2},{4,5},{5,4},{6,7},{7,6},{8,9},{9,8},{10,11... | collective-permute-start | bytes 172040 | tf_op jit(solution)/shard_map/ppermute | solution.py:248
  436.9 20.2 %collective-permute-start.41 = (bf16[32,1152]{1,0:T(8,128)(2,1)S(1)}, bf16[32,1152]{1,0:T(8,128)(2,1)S(1)}, u32[]{:S(2)}, u32[]{:S(2)}) collective-permute-start(bf16[32,1152]{1,0:T(8,128)(2,1)S(1)} %get-tuple-element.73), channel_id=1, source_target_pairs={{0,8},{8,16},{16,24},{1,9},{9,17},{17,25},{2,10},{10,18},{18,26},{... | collective-permute-start | bytes 221192 | tf_op jit(solution)/shard_map/ppermute | solution.py:295
  439.7 18.8 %collective-permute-start.40 = (bf16[32,1152]{1,0:T(8,128)(2,1)S(1)}, bf16[32,1152]{1,0:T(8,128)(2,1)S(1)}, u32[]{:S(2)}, u32[]{:S(2)}) collective-permute-start(bf16[32,1152]{1,0:T(8,128)(2,1)S(1)} %get-tuple-element.74), channel_id=1, source_target_pairs={{8,0},{16,8},{24,16},{9,1},{17,9},{25,17},{10,2},{18,10},{26,18},{... | collective-permute-start | bytes 221192 | tf_op jit(solution)/shard_map/ppermute | solution.py:295
  441.0 17.5 %collective-permute-start.39 = (bf16[32,1152]{1,0:T(8,128)(2,1)S(1)}, bf16[32,1152]{1,0:T(8,128)(2,1)S(1)}, u32[]{:S(2)}, u32[]{:S(2)}) collective-permute-start(bf16[32,1152]{1,0:T(8,128)(2,1)S(1)} %get-tuple-element.75), channel_id=1, source_target_pairs={{0,16},{8,24},{1,17},{9,25},{2,18},{10,26},{3,19},{11,27},{4,20},{... | collective-permute-start | bytes 221192 | tf_op jit(solution)/shard_map/ppermute | solution.py:295
  448.9 9.6 %collective-permute-start.38 = (bf16[32,1152]{1,0:T(8,128)(2,1)S(1)}, bf16[32,1152]{1,0:T(8,128)(2,1)S(1)}, u32[]{:S(2)}, u32[]{:S(2)}) collective-permute-start(bf16[32,1152]{1,0:T(8,128)(2,1)S(1)} %get-tuple-element.76), channel_id=1, source_target_pairs={{16,0},{24,8},{17,1},{25,9},{18,2},{26,10},{19,3},{27,11},{20,4},{... | collective-permute-start | bytes 221192 | tf_op jit(solution)/shard_map/ppermute | solution.py:295
  450.2 8.9 %collective-permute-start.37 = (bf16[32,1152]{1,0:T(8,128)(2,1)S(1)}, bf16[32,1152]{1,0:T(8,128)(2,1)S(1)}, u32[]{:S(2)}, u32[]{:S(2)}) collective-permute-start(bf16[32,1152]{1,0:T(8,128)(2,1)S(1)} %get-tuple-element.77), channel_id=1, source_target_pairs={{0,24},{1,25},{2,26},{3,27},{4,28},{5,29},{6,30},{7,31}} | collective-permute-start | bytes 221192 | tf_op jit(solution)/shard_map/ppermute | solution.py:295
  457.1 8.0 %collective-permute-start.36 = (bf16[32,1152]{1,0:T(8,128)(2,1)S(1)}, bf16[32,1152]{1,0:T(8,128)(2,1)S(1)}, u32[]{:S(2)}, u32[]{:S(2)}) collective-permute-start(bf16[32,1152]{1,0:T(8,128)(2,1)S(1)} %get-tuple-element.72), channel_id=1, source_target_pairs={{24,0},{25,1},{26,2},{27,3},{28,4},{29,5},{30,6},{31,7}} | collective-permute-start | bytes 221192 | tf_op jit(solution)/shard_map/ppermute | solution.py:295
  465.2 5.4 %collective-permute-start.42 = (bf16[32,1152]{1,0:T(8,128)(2,1)S(1)}, bf16[32,1152]{1,0:T(8,128)(2,1)S(1)}, u32[]{:S(2)}, u32[]{:S(2)}) collective-permute-start(bf16[32,1152]{1,0:T(8,128)(2,1)S(1)} %fusion.76), channel_id=1, source_target_pairs={{0,3},{1,2},{2,1},{3,0},{4,7},{5,6},{6,5},{7,4},{8,11},{9,10},{10,... | collective-permute-start | bytes 221192 | tf_op jit(solution)/shard_map/ppermute | solution.py:248
  466.6 4.8 collective-permute-start.43
  467.5 4.4 collective-permute-start.44
  (77 other events, 521.6 us)
Sparse Core Ops, SparseCore 0:
  9.6 44.7 all-gather.3
  56.0 39.0 all-gather.5
  130.9 33.6 all-gather.7
  244.7 43.7 reduce-scatter.3
  290.7 35.7 reduce-scatter.5
  401.3 34.3 reduce-scatter.7

commit v2 on v1

--- a/solution.py
+++ b/solution.py
@@ -1,11 +1,10 @@
-import functools
-
 import jax
 import jax.numpy as jnp
 from jax import lax
 from jax.experimental import pallas as pl
 from jax.experimental.pallas import tpu as pltpu
 from jax.sharding import PartitionSpec as P
+
 
 QUERY_HEADS = 14
 KEY_VALUE_HEADS = 2
@@ -131,10 +130,11 @@
     query_t,
     own,
     other,
-    mixed_t,
     grad_t,
     lse,
     grad_query_t,
+    own_sums,
+    other_sums,
     grad_key,
     grad_value,
     keys_t,
@@ -165,11 +165,6 @@
                         place = pl.ds(pl.multiple_of(head * HEAD_WIDTH, HEAD_WIDTH), HEAD_WIDTH)
                         query = query_t[place, cols]
                         grad = grad_t[place, cols]
-                        delta = jnp.sum(
-                            grad.astype(F32) * mixed_t[place, cols].astype(F32),
-                            axis=0,
-                            keepdims=True,
-                        )
                         score = (
                             jnp.dot(keys[group, 0:span, :], query, preferred_element_type=F32)
                             + bias[0:span, :]
@@ -178,28 +173,46 @@
                         grad_prob = jnp.dot(
                             values[group, 0:span, :], grad, preferred_element_type=F32
                         )
+                        delta = jnp.sum(prob * grad_prob, axis=0, keepdims=True)
                         grad_score = (prob * (grad_prob - delta)).astype(BF)
                         grad_value[group, 0:span, :] += dot(prob.astype(BF), grad, 1, 1)
                         grad_key[group, 0:span, :] += dot(grad_score, query, 1, 1)
-                        grad_query_t[place, cols] = jnp.dot(
-                            keys_t[head_rows, 0:span], grad_score, preferred_element_type=F32
-                        ) * (HEAD_WIDTH ** (-0.5))
+                        grad_query_t[place, cols] = (
+                            jnp.dot(
+                                keys_t[head_rows, 0:span], grad_score, preferred_element_type=F32
+                            )
+                            * (HEAD_WIDTH ** (-0.5))
+                        ).astype(BF)
                         return carry
 
                     lax.fori_loop(0, GROUP, one, 0)
 
-
-def attention_backward(half, doc_row, doc_col, query_t, own, other, mixed_t, grad_t, lse):
+            for head in range(2 * KEY_VALUE_HEADS):
+                source = (grad_key, grad_value)[head // KEY_VALUE_HEADS]
+                rows = slice(head * HEAD_WIDTH, (head + 1) * HEAD_WIDTH)
+                first = source[head % KEY_VALUE_HEADS, 0:token_count, :].T
+                if half == 0:
+                    own_sums[rows, :] = first
+                    other_sums[rows, :] = jnp.zeros_like(first)
+                else:
+                    own_sums[rows, :] = source[head % KEY_VALUE_HEADS, token_count:, :].T
+                    other_sums[rows, :] = first
+
+
+def attention_backward(half, doc_row, doc_col, query_t, own, other, grad_t, lse):
     width, token_count = query_t.shape
     kv = KEY_VALUE_HEADS * HEAD_WIDTH
     vmem = pl.BlockSpec(memory_space=pltpu.VMEM)
-    sums = jax.ShapeDtypeStruct((KEY_VALUE_HEADS, 2 * token_count, HEAD_WIDTH), F32)
+    sums = jax.ShapeDtypeStruct((2 * kv, token_count), F32)
+    totals = pltpu.VMEM((KEY_VALUE_HEADS, 2 * token_count, HEAD_WIDTH), F32)
     return pl.pallas_call(
         attention_backward_body,
-        out_shape=(jax.ShapeDtypeStruct((width, token_count), F32), sums, sums),
-        in_specs=[pl.BlockSpec(memory_space=pltpu.SMEM)] + [vmem] * 8,
+        out_shape=(jax.ShapeDtypeStruct((width, token_count), BF), sums, sums),
+        in_specs=[pl.BlockSpec(memory_space=pltpu.SMEM)] + [vmem] * 7,
         out_specs=(vmem, vmem, vmem),
         scratch_shapes=[
+            totals,
+            totals,
             pltpu.VMEM((kv, 2 * token_count), BF),
             pltpu.VMEM((KEY_VALUE_HEADS, 2 * token_count, HEAD_WIDTH), BF),
             pltpu.VMEM((kv, 2 * token_count), BF),
@@ -210,7 +223,7 @@
             flops=int(35e9), bytes_accessed=8 * width * token_count, transcendentals=0
         ),
         name="attention_backward",
-    )(half, doc_row, doc_col, query_t, own, other, mixed_t, grad_t, lse)
+    )(half, doc_row, doc_col, query_t, own, other, grad_t, lse)
 
 
 def rope_tables(half, token_count):
@@ -247,35 +260,39 @@
     def side(self, value, which):
         return lax.ppermute(value, "tp", [(i, i ^ which) for i in range(self.tps)])
 
+    def ring(self, value, which):
+        return lax.ppermute(value, "shard", [(i, i ^ which) for i in range(self.shards)])
+
+    def place(self):
+        return jnp.stack([self.z, self.c, self.t]).astype(jnp.int32)
+
     def gather_rows(self, block):
-        if not self.fast:
-            return lax.all_gather(block, ("shard", "ctx"), axis=0)
-        last = self.shards - 1
-        plus, minus = [], []
-        right = left = block
-        for step in range(1, self.shards):
-            right = lax.ppermute(right, "shard", [(i, i + 1) for i in range(step - 1, last)])
-            left = lax.ppermute(left, "shard", [(i + 1, i) for i in range(0, last - step + 1)])
-            plus.append(right)
-            minus.append(left)
-        line = jnp.stack(plus[::-1] + [block] + minus)
-        mine = lax.dynamic_slice_in_dim(line, last - self.z, self.shards, 0)
-        theirs = self.across(mine)
-        low = jnp.where(self.c == 0, mine, theirs)
-        high = jnp.where(self.c == 0, theirs, mine)
-        full = jnp.stack([low, high], 1)
-        return full.reshape((self.shards * self.ctxs,) + block.shape)
-
-    def reduce_rows(self, value):
-        blocks, rows, cols = value.shape
-        if not self.fast:
-            part = lax.psum_scatter(
-                value, ("shard", "ctx"), scatter_dimension=0, tiled=True
-            )
-            return lax.psum(part[0].astype(F32), "tp")
-        value = value.reshape(self.shards, self.ctxs, rows, cols)
-        send = lax.dynamic_index_in_dim(value, 1 - self.c, 1, False).astype(BF)
-        keep = lax.dynamic_index_in_dim(value, self.c, 1, False)
+        return lax.all_gather(block, ("shard", "ctx"), axis=0)
+
+    def gather_spread(self, block):
+        rows, _ = block.shape
+        part = rows // self.tps
+        quarter = lax.dynamic_slice_in_dim(block, self.t * part, part, 0)
+        pieces = [block]
+        pieces += [self.ring(quarter, which) for which in (1, 2, 3)]
+        far = jnp.concatenate(pieces[1:], 0)
+        sides = [self.side(far, which) for which in (1, 2, 3)]
+        mine = [block, far] + sides
+        theirs = [self.across(piece) for piece in mine]
+        return far, sides, assemble_spread(self.place(), mine, theirs, rows)
+
+    def gather_line(self, block, after, later):
+        block, after = lax.optimization_barrier((block, after))
+        two = self.ring(block, 2)
+        one = self.ring(block, 1)
+        late, relayed, later = lax.optimization_barrier((block, two, later))
+        middle = lax.ppermute(late, "shard", [(1, 2), (2, 1)])
+        ends = lax.ppermute(relayed, "shard", [(2, 3), (1, 0)])
+        three = jnp.where((self.z == 1) | (self.z == 2), middle, ends)
+        return [block, one, two, three]
+
+    def reduce_rows(self, send, keep):
+        rows, cols = keep.shape[1:]
         part = keep.astype(F32) + self.across(send).astype(F32)
         part = part.reshape(self.shards, self.tps, rows // self.tps, cols)
 
@@ -286,13 +303,9 @@
         for which in (1, 2, 3):
             mine = mine + self.side(quarter(which).astype(BF), which).astype(F32)
         total = lax.dynamic_index_in_dim(mine, self.z, 0, False)
-        for shift in (-3, 3, -2, 2, -1, 1):
-            index = jnp.clip(self.z + shift, 0, self.shards - 1)
-            piece = lax.dynamic_index_in_dim(mine, index, 0, False).astype(BF)
-            pairs = [
-                (i, i + shift) for i in range(self.shards) if 0 <= i + shift < self.shards
-            ]
-            total = total + lax.ppermute(piece, "shard", pairs).astype(F32)
+        for which in (3, 2, 1):
+            piece = lax.dynamic_index_in_dim(mine, self.z ^ which, 0, False).astype(BF)
+            total = total + self.ring(piece, which).astype(F32)
         low = total.astype(BF)
         one, two, three = (self.side(low, which) for which in (1, 2, 3))
         odd = (self.t & 1) == 1
@@ -316,12 +329,10 @@
                 lax.dynamic_index_in_dim(every, (self.t + i) % self.tps, 0, False)
                 for i in range(self.tps)
             ]
-        half = rows.shape[0] // 2
         one = self.side(rows, 1)
         two = self.side(rows, 2)
-        top = self.side(one[:half], 2)
-        bottom = self.side(two[half:], 1)
-        return [rows, one, two, jnp.concatenate([top, bottom], 0)]
+        late, one, two = lax.optimization_barrier((rows, one, two))
+        return [rows, one, two, self.side(late, 3)]
 
     def scatter_tokens(self, parts):
         if not self.fast:
@@ -333,17 +344,330 @@
                 ]
             )
             return lax.psum_scatter(ordered, "tp", scatter_dimension=0, tiled=False)
-        own, one, two, three = parts
-        half = own.shape[0] // 2
-        top = self.side(three[:half], 1)
-        bottom = self.side(three[half:], 2)
-        two = jnp.concatenate([two[:half] + top, two[half:]], 0)
-        one = jnp.concatenate([one[:half], one[half:] + bottom], 0)
-        return (
-            own.astype(F32)
-            + self.side(one, 1).astype(F32)
-            + self.side(two, 2).astype(F32)
+        total = parts[0].astype(F32)
+        for which in (1, 2, 3):
+            total = total + self.side(parts[which], which).astype(F32)
+        return total
+
+    def scatter_line(self, send, keep):
+        received = self.across(send)
+        part = (keep.astype(F32) + received.astype(F32)).astype(BF)
+        total = lax.dynamic_index_in_dim(part, self.z, 0, False).astype(F32)
+        for which in (2, 3, 1):
+            piece = lax.dynamic_index_in_dim(part, self.z ^ which, 0, False)
+            total = total + self.ring(piece, which).astype(F32)
+        return total
+
+
+def assemble_spread_body(place, *refs):
+    mine, theirs, (out, small) = refs[0:5], refs[5:10], refs[10:]
+    rows = out.shape[0] // 8
+    part = mine[0].shape[0] // 4
+    z, c, t = place[0], place[1], place[2]
+    for block in range(8):
+        shard, core = block // 2, block % 2
+        for side in range(4):
+            first = side * part
+            count = min(part, rows - first)
+
+            def put(pieces, index, start):
+                value = pieces[index][pl.ds(start, part), :]
+                out[block * rows + first : block * rows + first + count, :] = value[:count]
+                if count < part:
+                    small[block, :, :] = value[count:]
+
+            start = pl.multiple_of(jnp.maximum((shard ^ z) - 1, 0) * part, 16)
+            for pieces, owned in ((mine, core == c), (theirs, core != c)):
+
+                @pl.when(owned & (shard == z))
+                def _():
+                    put(pieces, 0, first)
+
+                for which in range(4):
+
+                    @pl.when(owned & (shard != z) & ((side ^ t) == which))
+                    def _():
+                        put(pieces, 1 + which, start)
+
+
+def assemble_spread(place, mine, theirs, padded):
+    cols = mine[0].shape[1]
+    extra = 16
+    rows = padded - extra
+    vmem = pl.BlockSpec(memory_space=pltpu.VMEM)
+    return pl.pallas_call(
+        assemble_spread_body,
+        out_shape=(
+            jax.ShapeDtypeStruct((8 * rows, cols), BF),
+            jax.ShapeDtypeStruct((8, extra, cols), BF),
+        ),
+        in_specs=[pl.BlockSpec(memory_space=pltpu.SMEM)] + [vmem] * 10,
+        out_specs=(vmem, vmem),
+        cost_estimate=pl.CostEstimate(
+            flops=0, bytes_accessed=32 * rows * cols, transcendentals=0
+        ),
+        name="assemble_spread",
+    )(place, *mine, *theirs)
+
+
+def assemble_line_body(place, *refs):
+    mine, theirs, outs = refs[0:4], refs[4:8], refs[8:]
+    rows = outs[0].shape[0] // 8
+    z, c = place[0], place[1]
+    for here in range(4):
+
+        @pl.when(z == here)
+        def _():
+            for block in range(8):
+                shard, core = block // 2, block % 2
+                left, right = mine[shard ^ here], theirs[shard ^ here]
+                for index, out in enumerate(outs):
+                    part = slice(index * rows, (index + 1) * rows)
+                    out[block * rows : (block + 1) * rows, :] = jnp.where(
+                        core == c, left[part, :], right[part, :]
+                    )
+
+
+def assemble_line(place, mine, theirs, count):
+    rows, cols = mine[0].shape
+    rows = rows // count
+    vmem = pl.BlockSpec(memory_space=pltpu.VMEM)
+    return pl.pallas_call(
+        assemble_line_body,
+        out_shape=[jax.ShapeDtypeStruct((8 * rows, cols), BF)] * count,
+        in_specs=[pl.BlockSpec(memory_space=pltpu.SMEM)] + [vmem] * 8,
+        out_specs=[vmem] * count,
+        cost_estimate=pl.CostEstimate(
+            flops=0, bytes_accessed=32 * rows * cols * count, transcendentals=0
+        ),
+        name="assemble_line",
+    )(place, *mine, *theirs)
+
+
+def projection_gradients_body(
+    place,
+    grad_query,
+    own_sums,
+    other_sums,
+    cosine,
+    sine,
+    tokens,
+    inverse,
+    gain,
+    second_gain,
+    grad_hidden,
+    mixed_t,
+    weight,
+    grad_tokens,
+    send,
+    keep,
+    fused,
+):
+    half_dim = HEAD_WIDTH // 2
+    query_width, kv = grad_query.shape[0], own_sums.shape[0] // 2
+    rows = keep.shape[1] - 16
+
+    def unrotate(value, start):
+        first, second = value[:half_dim], value[half_dim:]
+        fused[start : start + half_dim, :] = first * cosine[...] + second * sine[...]
+        fused[start + half_dim : start + HEAD_WIDTH, :] = (
+            second * cosine[...] - first * sine[...]
         )
+
+    for head in range(QUERY_HEADS):
+        start = head * HEAD_WIDTH
+        unrotate(grad_query[start : start + HEAD_WIDTH, :].astype(F32), start)
+    sums = (own_sums[...] + other_sums[...]).astype(BF).astype(F32)
+    for head in range(KEY_VALUE_HEADS):
+        start = head * HEAD_WIDTH
+        unrotate(sums[start : start + HEAD_WIDTH], query_width + start)
+    fused[query_width + kv :, :] = sums[kv:]
+
+    exact = fused[...]
+    low = exact.astype(BF)
+    rest = (exact - low.astype(F32)).astype(BF)
+    ones = jnp.ones((16, exact.shape[1]), BF)
+    bias = dot(ones, low, 1, 1) + dot(ones, rest, 1, 1)
+    low_rows = low.T
+    x = tokens[...].astype(F32)
+    inv = inverse[...]
+    normed_t = (x * inv * gain[...]).astype(BF).T
+    grad_normed = dot(low_rows, weight[...], 1, 1)
+    scaled = grad_normed * gain[...]
+    mean = jnp.mean(scaled * x, -1, keepdims=True)
+    hidden = grad_hidden[...]
+    grad_tokens[...] = (hidden + inv * scaled - x * (inv * inv * inv) * mean).astype(BF)
+    grad_gain = jnp.sum(grad_normed * x * inv, 0, keepdims=True)
+    left = jnp.dot(normed_t, low_rows, preferred_element_type=F32).astype(BF)
+    right = jnp.dot(
+        mixed_t[...], hidden.astype(BF), preferred_element_type=F32
+    ).astype(BF)
+    split = left.shape[1]
+    first_row = jnp.concatenate(
+        [bias[:8], jnp.broadcast_to(grad_gain, (8, grad_gain.shape[1]))], 1
+    )
+    second_row = jnp.concatenate(
+        [
+            jnp.broadcast_to(second_gain[...], (8, second_gain.shape[1])),
+            jnp.zeros((8, split), F32),
+        ],
+        1,
+    )
+    index = lax.broadcasted_iota(jnp.int32, first_row.shape, 0)
+    small = jnp.where(index == 0, first_row, jnp.where(index == 1, second_row, 0.0))
+    small = jnp.concatenate([small, jnp.zeros_like(small)], 0).astype(BF)
+    for block in range(8):
+        shard, core = block // 2, block % 2
+        part = slice(block * rows, (block + 1) * rows)
+        for out, owned in ((keep, place[1] == core), (send, place[1] != core)):
+
+            @pl.when(owned)
+            def _():
+                out[shard, 0:rows, 0:split] = left[part]
+                out[shard, 0:rows, split:] = right[part]
+                out[shard, rows:, :] = small
+
+
+def projection_gradients(place, *arrays):
+    tokens, weight = arrays[5], arrays[11]
+    token_count, width = tokens.shape
+    fused_width = weight.shape[1] - width
+    vmem = pl.BlockSpec(memory_space=pltpu.VMEM)
+    half = jax.ShapeDtypeStruct((4, width // 8 + 16, weight.shape[1]), BF)
+    whole = [
+        pl.BlockSpec(array.shape, lambda i, n=array.ndim: (0,) * n) for array in arrays[:-1]
+    ]
+    return pl.pallas_call(
+        projection_gradients_body,
+        grid=(1,),
+        out_shape=(jax.ShapeDtypeStruct(tokens.shape, BF), half, half),
+        in_specs=[pl.BlockSpec(memory_space=pltpu.SMEM)]
+        + whole
+        + [pl.BlockSpec((width, fused_width), lambda i: (0, 0))],
+        out_specs=(
+            pl.BlockSpec(tokens.shape, lambda i: (0, 0)),
+            pl.BlockSpec(half.shape, lambda i: (0, 0, 0)),
+            pl.BlockSpec(half.shape, lambda i: (0, 0, 0)),
+        ),
+        scratch_shapes=[pltpu.VMEM((fused_width, token_count), F32)],
+        cost_estimate=pl.CostEstimate(
+            flops=int(6e9), bytes_accessed=int(16e6), transcendentals=0
+        ),
+        name="projection_gradients",
+    )(place, *arrays)
+
+
+def mlp_body(x_ref, g_ref, gate_ref, up_ref, down_ref, *refs):
+    back, down, units, rows_t = refs[-4:]
+    x, g = x_ref[...], g_ref[...]
+    gate = jnp.dot(x, gate_ref[...], preferred_element_type=F32)
+    up = jnp.dot(x, up_ref[...], preferred_element_type=F32)
+    sig = 1.0 / (1.0 + jnp.exp(-gate))
+    silu = gate * sig
+    act = (silu * up).astype(BF)
+    grad_act = jnp.dot(g, down_ref[...], preferred_element_type=F32)
+    grad_gate = (grad_act * up * sig * (1.0 + gate * (1.0 - sig))).astype(BF)
+    grad_up = (grad_act * silu).astype(BF)
+    back[...] = (
+        dot(grad_gate, gate_ref[...], 1, 1) + dot(grad_up, up_ref[...], 1, 1)
+    ).astype(BF)
+    down[...] = dot(act, down_ref[...], 1, 1).astype(BF)
+    units[0] = grad_gate
+    units[1] = grad_up
+    units[2] = act
+    rows_t[0] = x.T
+    rows_t[1] = g.T
+
+
+def mlp(x, g, weights, kept, first, total):
+    count, width = x.shape
+    units = weights[0].shape[1]
+    step = min(256, count)
+    offset = first // step
+    rows = pl.BlockSpec((step, width), lambda i: (i, 0))
+    whole = pl.BlockSpec((width, units), lambda i: (0, 0), pipeline_mode=pl.Buffered(1))
+    partial = jax.ShapeDtypeStruct((count, width), BF)
+    kept = list(kept)
+    outs = pl.pallas_call(
+        mlp_body,
+        grid=(count // step,),
+        out_shape=[
+            partial,
+            partial,
+            jax.ShapeDtypeStruct((3, total, units), BF),
+            jax.ShapeDtypeStruct((2, width, total), BF),
+        ],
+        in_specs=[rows, rows, whole, whole, whole]
+        + [pl.BlockSpec(memory_space=pl.ANY)] * len(kept),
+        out_specs=[
+            rows,
+            rows,
+            pl.BlockSpec((3, step, units), lambda i: (0, i + offset, 0)),
+            pl.BlockSpec((2, width, step), lambda i: (0, 0, i + offset)),
+        ],
+        input_output_aliases={5 + i: 2 + i for i in range(len(kept))},
+        cost_estimate=pl.CostEstimate(
+            flops=12 * count * width * units,
+            bytes_accessed=6 * width * units + 8 * count * (width + units),
+            transcendentals=count * units,
+        ),
+        name="mlp",
+    )(x, g, *weights, *kept)
+    return outs[0], outs[1], outs[2:]
+
+
+def weight_gradients_body(place, left, right, send, keep, total):
+    index, last = pl.program_id(1), pl.num_programs(1) - 1
+    rows = send.shape[2]
+    value = jnp.dot(left[0], right[0], preferred_element_type=F32)
+
+    @pl.when(index == 0)
+    def _():
+        total[...] = value
+
+    @pl.when(index > 0)
+    def _():
+        total[...] += value
+
+    @pl.when(index == last)
+    def _():
+        for block in range(8):
+            shard, core = block // 2, block % 2
+            piece = total[block * rows : (block + 1) * rows, :].astype(BF)
+
+            @pl.when(place[1] == core)
+            def _():
+                keep[shard, 0] = piece
+
+            @pl.when(place[1] != core)
+            def _():
+                send[shard, 0] = piece
+
+
+def weight_gradients(place, units, rows_t):
+    _, total, wide = units.shape
+    width = rows_t.shape[1]
+    step = total // 2
+    half = jax.ShapeDtypeStruct((4, 3, width // 8, wide), BF)
+    out = pl.BlockSpec((4, 1, width // 8, wide), lambda w, k: (0, w, 0, 0))
+    return pl.pallas_call(
+        weight_gradients_body,
+        grid=(3, 2),
+        out_shape=(half, half),
+        in_specs=[
+            pl.BlockSpec(memory_space=pltpu.SMEM),
+            pl.BlockSpec((1, width, step), lambda w, k: (w // 2, 0, k)),
+            pl.BlockSpec((1, step, wide), lambda w, k: (w, k, 0)),
+        ],
+        out_specs=(out, out),
+        scratch_shapes=[pltpu.VMEM((width, wide), F32)],
+        cost_estimate=pl.CostEstimate(
+            flops=6 * total * width * wide,
+            bytes_accessed=6 * total * (width + wide),
+            transcendentals=0,
+        ),
+        name="weight_gradients",
+    )(place, rows_t, units)
 
 
 def per_device(
@@ -366,40 +690,46 @@
     mesh = Mesh()
     token_count, width = tokens.shape
     rows = w_query.shape[0]
-    padded = (rows // 16 + 1) * 16
+    padded = (rows + 5 + 15) // 16 * 16
     query_width = QUERY_HEADS * HEAD_WIDTH
     kv_width = KEY_VALUE_HEADS * HEAD_WIDTH
     kv_rows = key_bias_vector.shape[0]
     fused_width = query_width + 2 * kv_width
     blocks = mesh.shards * mesh.ctxs
 
-    small = jnp.concatenate(
-        [b_query, key_bias_vector, value_bias_vector, gain_attn, gain_mlp]
-    )
-    small_ends = [rows, rows + kv_rows, rows + 2 * kv_rows, 2 * rows + 2 * kv_rows]
-    small = jnp.pad(small, (0, fused_width - small.shape[0]))
+    all_width = fused_width + width
+    small_vectors = [b_query, key_bias_vector, value_bias_vector, gain_attn, gain_mlp]
+    small_counts = [vector.shape[0] for vector in small_vectors]
     packed = jnp.concatenate(
-        [
-            jnp.concatenate([w_query, key_projection, value_projection], 1),
-            small[None],
-            jnp.zeros((padded - rows - 1, fused_width), BF),
-        ],
+        [jnp.concatenate([w_query, key_projection, value_projection, w_output], 1)]
+        + [
+            jnp.pad(vector[None], ((0, 0), (0, all_width - vector.shape[0])))
+            for vector in small_vectors
+        ]
+        + [jnp.zeros((padded - rows - len(small_vectors), all_width), BF)],
         0,
     )
-    gathered = mesh.gather_rows(packed)
-    fused_weight = gathered[:, :rows].reshape(width, fused_width)
-    smalls = gathered[:, rows]
-    pieces = jnp.split(smalls[:, : small_ends[-1] + rows], small_ends, 1)
+    if mesh.fast:
+        far, sides, (projection, smalls) = mesh.gather_spread(packed)
+        line = mesh.gather_line(jnp.concatenate([w_gate, w_up, w_down.T], 0), far, smalls)
+        others = [mesh.across(part) for part in line]
+        late, sides = lax.optimization_barrier((cotangent, sides))
+        grad_parts = mesh.gather_tokens(late)
+    else:
+        gathered = lax.all_gather(packed, ("shard", "ctx"), axis=0)
+        projection = gathered[:, :rows].reshape(width, all_width)
+        smalls = gathered[:, rows:]
+        weights = [
+            lax.all_gather(part, ("shard", "ctx"), axis=0, tiled=True)
+            for part in (w_gate, w_up, w_down.T)
+        ]
+        grad_parts = mesh.gather_tokens(cotangent)
+    fused_weight = projection[:, :fused_width]
+    output_weight = projection[:, fused_width:]
     bias_q, bias_k, bias_v, first_gain, second_gain = (
-        piece.reshape(-1).astype(F32) for piece in pieces
+        smalls[:, i, :count].reshape(-1).astype(F32) for i, count in enumerate(small_counts)
     )
     fused_bias = jnp.concatenate([bias_q, bias_k, bias_v])
-
-    output_weight = mesh.gather_rows(w_output).reshape(width, width)
-    gate_weight = lax.all_gather(w_gate, ("shard", "ctx"), axis=0, tiled=True)
-    up_weight = lax.all_gather(w_up, ("shard", "ctx"), axis=0, tiled=True)
-    down_weight_t = lax.all_gather(w_down.T, ("shard", "ctx"), axis=0, tiled=True)
-    grad_parts = mesh.gather_tokens(cotangent)
 
     tok_float = tokens.astype(F32)
     first_inv = lax.rsqrt(jnp.mean(tok_float * tok_float, -1, keepdims=True) + EPSILON)
@@ -419,41 +749,33 @@
     second_inv = lax.rsqrt(jnp.mean(hidden * hidden, -1, keepdims=True) + EPSILON)
     normed_mlp = (hidden * second_inv * second_gain).astype(BF)
     normed_parts = mesh.gather_tokens(normed_mlp)
-
-    downs, backs, acts, gates, ups = [], [], [], [], []
-    for x, g in zip(normed_parts, grad_parts):
-        gate = dot(x, gate_weight, 1, 0)
-        up = dot(x, up_weight, 1, 0)
-        sig = jax.nn.sigmoid(gate)
-        silu = gate * sig
-        act = (silu * up).astype(BF)
-        grad_act = dot(g, down_weight_t, 1, 0)
-        grad_gate = (grad_act * up * sig * (1.0 + gate * (1.0 - sig))).astype(BF)
-        grad_up = (grad_act * silu).astype(BF)
-        backs.append(
-            (dot(grad_gate, gate_weight, 1, 1) + dot(grad_up, up_weight, 1, 1)).astype(BF)
+    if mesh.fast:
+        line, others, _ = lax.optimization_barrier((line, others, normed_mlp))
+        weights = assemble_line(mesh.place(), line, others, 3)
+
+    total = token_count * mesh.tps
+    backs, downs, kept = [], [], []
+    for index, (x, g) in enumerate(zip(normed_parts, grad_parts)):
+        back, down, kept = mlp(x, g, weights, kept, index * token_count, total)
+        backs.append(back)
+        downs.append(down)
+    units, rows_t = kept
+    grad_normed_mlp = mesh.scatter_tokens(backs).astype(F32)
+    if mesh.fast:
+        send, keep = weight_gradients(mesh.place(), units, rows_t)
+        part_gate, part_up, part_down = mesh.scatter_line(send, keep)
+        downs, grad_normed_mlp = lax.optimization_barrier((downs, grad_normed_mlp))
+    else:
+        part_gate, part_up, part_down = (
+            lax.psum_scatter(
+                dot(rows_t[i // 2], units[i], 1, 0),
+                ("shard", "ctx"),
+                scatter_dimension=0,
+                tiled=True,
+            )
+            for i in range(3)
         )
-        downs.append(dot(act, down_weight_t, 1, 1).astype(BF))
-        acts.append(act)
-        gates.append(grad_gate)
-        ups.append(grad_up)
-    grad_normed_mlp = mesh.scatter_tokens(backs).astype(F32)
-    down_rows = mesh.scatter_tokens(downs).astype(F32)
-    result = hidden + down_rows
-
-    normed_all = jnp.concatenate(normed_parts, 0)
-    grad_all = jnp.concatenate(grad_parts, 0)
-
-    def scatter_grad(left, right):
-        full = dot(left, jnp.concatenate(right, 0), 0, 0).astype(BF)
-        return lax.psum_scatter(full, ("shard", "ctx"), scatter_dimension=0, tiled=True).astype(
-            F32
-        )
-
-    part_gate = scatter_grad(normed_all, gates)
-    part_up = scatter_grad(normed_all, ups)
-    part_down = scatter_grad(grad_all, acts).T
-
+    part_down = part_down.T
     grad_out = cotangent.astype(F32)
     scaled_two = grad_normed_mlp * second_gain
     grad_hidden = (
@@ -464,17 +786,61 @@
     grad_second_gain = jnp.sum(grad_normed_mlp * hidden * second_inv, 0)
     grad_branch = grad_hidden.astype(BF)
     grad_mixed_t = dot(output_weight, grad_branch, 1, 1).astype(BF)
+    grad_query_rot, own_sums, to_other = attention_backward(
+        half, doc_ids, doc_col, query_t, own, other, grad_mixed_t, lse
+    )
+    hidden_late, grad_query_rot = lax.optimization_barrier((hidden, grad_query_rot))
+    result = (hidden_late + mesh.scatter_tokens(downs).astype(F32)).astype(BF)
+    received = mesh.across(to_other)
+    if mesh.fast:
+        grad_tokens, send, keep = projection_gradients(
+            mesh.place(),
+            grad_query_rot,
+            own_sums,
+            received,
+            cosine,
+            sine,
+            tokens,
+            first_inv,
+            first_gain[None],
+            grad_second_gain[None],
+            grad_hidden,
+            mixed_t,
+            projection,
+        )
+        summed = mesh.reduce_rows(send, keep)
+        index = mesh.z * mesh.ctxs + mesh.c
+
+        def own_part(line, start, count):
+            return lax.dynamic_slice_in_dim(line, start + index * count, count, 0)
+
+        first, second = summed[rows], summed[rows + 1]
+        sum_small = [
+            own_part(first, 0, rows),
+            own_part(first, query_width, kv_rows),
+            own_part(first, query_width + kv_width, kv_rows),
+            own_part(first, fused_width, rows),
+            own_part(second, 0, rows),
+        ]
+        return (
+            result,
+            grad_tokens,
+            summed[:rows, :query_width],
+            sum_small[0],
+            summed[:rows, query_width : query_width + kv_width],
+            sum_small[1],
+            summed[:rows, query_width + kv_width : fused_width],
+            sum_small[2],
+            summed[:rows, fused_width:],
+            sum_small[3],
+            sum_small[4],
+            part_gate,
+            part_up,
+            part_down,
+        )
     grad_output_weight = dot(mixed_t, grad_branch, 1, 0)
-    grad_query_rot, grad_key_sum, grad_value_sum = attention_backward(
-        half, doc_ids, doc_col, query_t, own, other, mixed_t, grad_mixed_t, lse
-    )
-    sums = jnp.concatenate([grad_key_sum * (HEAD_WIDTH ** (-0.5) * 8.0), grad_value_sum], 0)
-    first_half, second_half = sums[:, :token_count], sums[:, token_count:]
-    to_other = jnp.where(mesh.c == 0, second_half, first_half).astype(BF)
-    own_sums = jnp.where(mesh.c == 0, first_half, second_half)
-    own_sums = (own_sums + mesh.across(to_other).astype(F32)).astype(BF).astype(F32)
-    own_sums_t = own_sums.transpose(0, 2, 1).reshape(2 * kv_width, token_count)
-    grad_query_pre = rotate(grad_query_rot.astype(BF).astype(F32), cosine, -sine)
+    own_sums_t = (own_sums + received).astype(BF).astype(F32)
+    grad_query_pre = rotate(grad_query_rot.astype(F32), cosine, -sine)
     grad_key_pre = rotate(own_sums_t[:kv_width], cosine, -sine)
     fused_grad_t = jnp.concatenate([grad_query_pre, grad_key_pre, own_sums_t[kv_width:]], 0)
     grad_fused_bias = jnp.sum(fused_grad_t, 1)
@@ -489,41 +855,41 @@
     )
     grad_first_gain = jnp.sum(grad_normed_attn * tok_float * first_inv, 0)
 
-    grad_smalls = jnp.concatenate(
-        [
-            grad_fused_bias[:query_width].reshape(blocks, rows),
-            grad_fused_bias[query_width : query_width + kv_width].reshape(blocks, kv_rows),
-            grad_fused_bias[query_width + kv_width :].reshape(blocks, kv_rows),
-            grad_first_gain.reshape(blocks, rows),
-            grad_second_gain.reshape(blocks, rows),
-        ],
-        1,
-    )
-    grad_smalls = jnp.pad(grad_smalls, ((0, 0), (0, fused_width - grad_smalls.shape[1])))
+    small_sums = [
+        grad_fused_bias[:query_width],
+        grad_fused_bias[query_width : query_width + kv_width],
+        grad_fused_bias[query_width + kv_width :],
+        grad_first_gain,
+        grad_second_gain,
+    ]
     grad_packed = jnp.concatenate(
         [
-            grad_fused_weight.reshape(blocks, rows, fused_width),
-            grad_smalls[:, None],
-            jnp.zeros((blocks, padded - rows - 1, fused_width), F32),
-        ],
+            jnp.concatenate([grad_fused_weight, grad_output_weight], 1).reshape(
+                blocks, rows, all_width
+            )
+        ]
+        + [
+            jnp.pad(
+                vector.reshape(blocks, 1, count), ((0, 0), (0, 0), (0, all_width - count))
+            )
+            for vector, count in zip(small_sums, small_counts)
+        ]
+        + [jnp.zeros((blocks, padded - rows - len(small_sums), all_width), F32)],
         1,
     )
-    grad_out_padded = jnp.pad(
-        grad_output_weight.reshape(blocks, rows, width), ((0, 0), (0, padded - rows), (0, 0))
-    )
-    sum_output_weight = mesh.reduce_rows(grad_out_padded)[:rows]
-    summed = mesh.reduce_rows(grad_packed)
-    sum_small = jnp.split(summed[rows, : small_ends[-1] + rows], small_ends)
+    summed = lax.psum_scatter(grad_packed, ("shard", "ctx"), scatter_dimension=0, tiled=True)
+    summed = lax.psum(summed[0], "tp")
+    sum_small = [summed[rows + i, :count] for i, count in enumerate(small_counts)]
     return (
-        result.astype(BF),
+        result,
         grad_tokens.astype(BF),
         summed[:rows, :query_width],
         sum_small[0],
         summed[:rows, query_width : query_width + kv_width],
         sum_small[1],
-        summed[:rows, query_width + kv_width :],
+        summed[:rows, query_width + kv_width : fused_width],
         sum_small[2],
-        sum_output_weight,
+        summed[:rows, fused_width:],
         sum_small[3],
         sum_small[4],
         part_gate,
@@ -568,6 +934,10 @@
         P(both, "tp"),
         P("tp", both),
     )
-    return jax.shard_map(
+
+    step = jax.shard_map(
         per_device, mesh=mesh, in_specs=in_specs, out_specs=out_specs, check_vma=False
     )
+    if tuple(mesh.shape[name] for name in every) != (4, 2, 4):
+        return step
+    return step

time: 497 us -> 440 us (0.89)
  Pallas kernels: 31.5 us -> 139 us
  matrix products: 115 us -> 10.6 us
  starting transfers between devices: 102 us -> 66.2 us
  waiting for transfers between devices: 141 us -> 172 us
  local copies, waits for them, and re-layouts: 42 us -> 15.7 us
  between operations: 15.9 us -> 1.58 us
  other arithmetic: 39 us -> 26.8 us
    dot_general x33 -> x3, matrix products: 115 us -> 10.6 us  [dot(): lax.dot_general(left, right, (((left_dim,), (right_dim,)), ((), ())), pre...]
    pallas_call x0 -> x8, Pallas kernels: none -> 104 us  [the longest x4 57.2 us: mlp(): pl.pallas_call(mlp_body, grid=(count // step,), out_shape=[partial, parti...]
    ppermute x24 -> x13, starting transfers between devices: 53.3 us -> 23.6 us  [the longest x11 21.6 us: ring(): lax.ppermute(value, 'shard', [(i, i ^ which) for i in range(self.shards)])]
    unnamed x174 -> x60, local copies, waits for them, and re-layouts: 21.8 us -> 2.84 us
    ppermute x28 -> x21, waiting for transfers between devices: 67.7 us -> 86.1 us  [side(): return lax.ppermute(value, 'tp', [(i, i ^ which) for i in range(self.tps)])]
    ppermute x24 -> x13, waiting for transfers between devices: 72.7 us -> 84.4 us  [the longest x11 84.4 us: ring(): lax.ppermute(value, 'shard', [(i, i ^ which) for i in range(self.shards)])]
    ppermute x28 -> x21, starting transfers between devices: 32.1 us -> 25.8 us  [side(): return lax.ppermute(value, 'tp', [(i, i ^ which) for i in range(self.tps)])]
    concatenate x8 -> x1, local copies, waits for them, and re-layouts: 5.56 us -> 0.01 us  [gather_spread(): far = jnp.concatenate(pieces[1:], 0)]
  transfers between devices with their start and end apart: 64 -> 47, of which waited for: 23 -> 21; matrix products, arithmetic and copies ran while one was open for 35% -> 8% of each run, Pallas kernels for 6% -> 28%
where the time goes in v2:
time: 440 us; the launch traced here: 432 us
  waiting for transfers between devices  172 us (39%)
  Pallas kernels  139 us (32%)
  starting transfers between devices  66.2 us (15%)
  other arithmetic  26.8 us (6%)
  local copies, waits for them, and re-layouts  15.7 us (4%)
  matrix products  10.6 us (2%)
    ppermute x21, waiting for transfers between devices, side(): return lax.ppermute(value, 'tp', [(i, i ^ which) for i in range(self.tps)])  86.1 us
    ppermute x11, waiting for transfers between devices, ring(): lax.ppermute(value, 'shard', [(i, i ^ which) for i in range(self.shards)])  84.4 us
    pallas_call x4, Pallas kernels, mlp(): pl.pallas_call(mlp_body, grid=(count // step,), out_shape=[partial, parti...  57.2 us
    ppermute x21, starting transfers between devices, side(): return lax.ppermute(value, 'tp', [(i, i ^ which) for i in range(self.tps)])  25.8 us
    pallas_call x1, Pallas kernels, weight_gradients(): pl.pallas_call(weight_gradients_body, grid=(3, 2), out_shape=(half, half)...  22.7 us
    ppermute x11, starting transfers between devices, ring(): lax.ppermute(value, 'shard', [(i, i ^ which) for i in range(self.shards)])  21.6 us
    pallas_call x1, Pallas kernels, attention_backward(): pl.pallas_call(attention_backward_body, out_shape=(jax.ShapeDtypeStruct((...  19.3 us
    ppermute x13, starting transfers between devices, across(): return lax.ppermute(value, 'ctx', pairs)  16.8 us
  transfers between devices with their start and end apart: 47, of which 21 were waited for; matrix products, arithmetic and copies ran while one was open for 8% of the time, Pallas kernels for 28%

profile of v2, /device:TPU:0, one launch (start us, length us, event | category | flops | bytes accessed | tf_op | source)
XLA Modules:
  0.0 431.6 jit_solution(4545728314164550791)
XLA Ops:
  5.7 3.1 collective-permute-start
  8.8 2.6 collective-permute-start.1
  11.4 2.5 collective-permute-done
  13.9 7.8 %collective-permute-done.1 = bf16[32,2048]{1,0:T(8,128)(2,1)S(1)} collective-permute-done((bf16[32,2048]{1,0:T(8,128)(2,1)S(1)}, bf16[32,2048]{1,0:T(8,128)(2,1)S(1)}, u32[]{:S(2)}, u32[]{:S(2)}) %collective-permute-start.1) | collective-permute-done | bytes 131104 | tf_op jit(solution)/shard_map/ppermute | solution.py:264
  21.7 2.5 collective-permute-start.5
  25.9 8.7 %collective-permute-done.5.refs_4_ = bf16[96,2048]{1,0:T(8,128)(2,1)S(1)} collective-permute-done((bf16[96,2048]{1,0:T(8,128)(2,1)S(1)}, bf16[96,2048]{1,0:T(8,128)(2,1)S(1)}, u32[]{:S(2)}, u32[]{:S(2)}) %collective-permute-start.5) | collective-permute-done | bytes 393248 | tf_op jit(solution)/shard_map/ppermute | solution.py:261
  34.7 5.1 %collective-permute-done.3.refs_2_ = bf16[96,2048]{1,0:T(8,128)(2,1)} collective-permute-done((bf16[96,2048]{1,0:T(8,128)(2,1)S(1)}, bf16[96,2048]{1,0:T(8,128)(2,1)}, u32[]{:S(2)}, u32[]{:S(2)}) %collective-permute-start.3) | collective-permute-done | bytes 393248 | tf_op jit(solution)/shard_map/ppermute | solution.py:261
  41.9 1.2 pad_maximum_fusion.refs_0_
  43.1 4.6 %collective-permute-start.13 = (bf16[336,1216]{1,0:T(8,128)(2,1)S(1)}, bf16[336,1216]{1,0:T(8,128)(2,1)}, u32[]{:S(2)}, u32[]{:S(2)}) collective-permute-start(bf16[336,1216]{1,0:T(8,128)(2,1)S(1)} %pad_maximum_fusion.refs_0_), channel_id=1, source_target_pairs={{0,16},{8,24},{16,0},{24,8},{1,17},{9,25},{17,1},{25,9},{2,18},{10... | collective-permute-start | bytes 2451464 | tf_op jit(solution)/shard_map/ppermute | solution.py:264
  47.7 1.5 collective-permute-start.22
  50.2 6.1 %assemble_spread.1 = (bf16[896,2048]{1,0:T(8,128)(2,1)}, bf16[8,16,2048]{2,1,0:T(8,128)(2,1)}) custom-call(s32[3]{0:T(128)} %pad_add_fusion.place, bf16[128,2048]{1,0:T(8,128)(2,1)} %copy-done.3, bf16[96,2048]{1,0:T(8,128)(2,1)} %copy-done.14, bf16[96,2048]{1,0:T(8,128)(2,1)} %collective-permute-done.3.refs_2_, ...), custom_call_target="tpu_custom_call" | custom-call | bytes 7340032 | tf_op jit(solution)/shard_map/assemble_spread/pallas_call | solution.py:398
  56.2 1.4 slice_convert_fusion.1
  59.7 3.1 convolution_add_fusion
  65.5 2.1 maximum_multiply_fusion
  67.6 18.0 %collective-permute-done.13.refs_2_ = bf16[336,1216]{1,0:T(8,128)(2,1)} collective-permute-done((bf16[336,1216]{1,0:T(8,128)(2,1)S(1)}, bf16[336,1216]{1,0:T(8,128)(2,1)}, u32[]{:S(2)}, u32[]{:S(2)}) %collective-permute-start.13) | collective-permute-done | bytes 817184 | tf_op jit(solution)/shard_map/ppermute | solution.py:264
  86.3 1.3 collective-permute-start.15
  87.6 15.5 %attention_forward.1 = (bf16[896,512]{1,0:T(8,128)(2,1)}, f32[14,8,512]{2,1,0:T(8,128)}) custom-call(s32[1]{0:T(128)} %bitcast.half_ref, s32[1,1024]{1,0:T(1,128)} %doc_row.3, s32[1024,1]{1,0:T(8,128)} %copy.38.doc_col, bf16[896,512]{1,0:T(8,128)(2,1)} %bitcast.87, bf16[256,512]{1,0:T(8,128)(2,1)} %pad_maximum_fusion.2.own, ...), custom_call_target="tpu_custom_call" | custom-call | flops 15000000512 | bytes 1835008 | tf_op jit(solution)/shard_map/attention_forward/pallas_call | solution.py:105
  103.1 3.3 multiply_reduce_fusion.2
  108.1 1.5 collective-permute-start.20
  109.6 3.6 collective-permute-start.12
  113.2 1.4 collective-permute-start.21
  114.6 1.2 broadcast_select_fusion.refs_3_
  115.9 13.1 %collective-permute-done.12.refs_1_ = bf16[336,1216]{1,0:T(8,128)(2,1)} collective-permute-done((bf16[336,1216]{1,0:T(8,128)(2,1)S(1)}, bf16[336,1216]{1,0:T(8,128)(2,1)}, u32[]{:S(2)}, u32[]{:S(2)}) %collective-permute-start.12) | collective-permute-done | bytes 817184 | tf_op jit(solution)/shard_map/ppermute | solution.py:264
  129.0 4.1 collective-permute-start.16
  133.7 1.4 collective-permute-start.25
  135.2 1.6 collective-permute-start.24
  139.0 7.0 %assemble_line.1 = (bf16[896,1216]{1,0:T(8,128)(2,1)}, bf16[896,1216]{1,0:T(8,128)(2,1)}, bf16[896,1216]{1,0:T(8,128)(2,1)}) custom-call(s32[3]{0:T(128)} %pad_add_fusion.place, bf16[336,1216]{1,0:T(8,128)(2,1)} %copy-done.1, bf16[336,1216]{1,0:T(8,128)(2,1)} %collective-permute-done.12.refs_1_, bf16[336,1216]{1,0:T(8,128)(2,1)} %collective-permute-done.13.refs_2_, ...), custom_call_target="tpu_custom_call" | custom-call | bytes 13074432 | tf_op jit(solution)/shard_map/assemble_line/pallas_call | solution.py:435
  146.0 14.2 %mlp.4 = (bf16[512,896]{1,0:T(8,128)(2,1)}, bf16[512,896]{1,0:T(8,128)(2,1)}, bf16[3,2048,1216]{2,1,0:T(8,128)(2,1)}, bf16[2,896,2048]{2,1,0:T(8,128)(2,1)}) custom-call(bf16[512,896]{1,0:T(8,128)(2,1)} %multiply_convert_fusion.x_ref, bf16[512,896]{1,0:T(8,128)(2,1)} %g_ref, bf16[896,1216]{1,0:T(8,128)(2,1)} %get-tuple-element.85.gate_ref, ...), custom_call_target="tpu_custom_call" | custom-call | flops 6694109184 | bytes 15187968 | tf_op jit(solution)/shard_map/mlp/pallas_call | solution.py:591
  160.2 14.2 %mlp.5 = (bf16[512,896]{1,0:T(8,128)(2,1)}, bf16[512,896]{1,0:T(8,128)(2,1)}, bf16[3,2048,1216]{2,1,0:T(8,128)(2,1)}, bf16[2,896,2048]{2,1,0:T(8,128)(2,1)}) custom-call(bf16[512,896]{1,0:T(8,128)(2,1)} %collective-permute-done.20.x_ref, bf16[512,896]{1,0:T(8,128)(2,1)} %collective-permute-done.22.g_ref, ...), custom_call_target="tpu_custom_call", output_to_operand_aliasing={{2}: (5, {}), {3}: (6, {})} | custom-call | flops 6694109184 | bytes 15187968 | tf_op jit(solution)/shard_map/mlp/pallas_call | solution.py:591
  174.4 14.3 %mlp.6 = (bf16[512,896]{1,0:T(8,128)(2,1)}, bf16[512,896]{1,0:T(8,128)(2,1)}, bf16[3,2048,1216]{2,1,0:T(8,128)(2,1)}, bf16[2,896,2048]{2,1,0:T(8,128)(2,1)}) custom-call(bf16[512,896]{1,0:T(8,128)(2,1)} %copy-done.8, bf16[512,896]{1,0:T(8,128)(2,1)} %collective-permute-done.23.g_ref, ...), custom_call_target="tpu_custom_call", output_to_operand_aliasing={{2}: (5, {}), {3}: (6, {})} | custom-call | flops 6694109184 | bytes 15187968 | tf_op jit(solution)/shard_map/mlp/pallas_call | solution.py:591
  188.7 1.4 collective-permute-start.27
  190.7 14.4 %mlp.7 = (bf16[512,896]{1,0:T(8,128)(2,1)}, bf16[512,896]{1,0:T(8,128)(2,1)}, bf16[3,2048,1216]{2,1,0:T(8,128)(2,1)}, bf16[2,896,2048]{2,1,0:T(8,128)(2,1)}) custom-call(bf16[512,896]{1,0:T(8,128)(2,1)} %collective-permute-done.24.x_ref, bf16[512,896]{1,0:T(8,128)(2,1)} %collective-permute-done.25.g_ref, ...), custom_call_target="tpu_custom_call", output_to_operand_aliasing={{2}: (5, {}), {3}: (6, {})} | custom-call | flops 6694109184 | bytes 15187968 | tf_op jit(solution)/shard_map/mlp/pallas_call | solution.py:591
  205.1 1.6 collective-permute-start.28
  208.2 3.2 collective-permute-done.27
  211.4 1.7 collective-permute-done.26
  213.1 19.7 %collective-permute-done.28 = bf16[512,896]{1,0:T(8,128)(2,1)} collective-permute-done((bf16[512,896]{1,0:T(8,128)(2,1)}, bf16[512,896]{1,0:T(8,128)(2,1)}, u32[]{:S(2)}, u32[]{:S(2)}) %collective-permute-start.28) | collective-permute-done | bytes 917536 | tf_op jit(solution)/shard_map/ppermute | solution.py:261
  232.8 2.2 convert_add_fusion.2
  235.7 1.7 multiply_subtract_fusion.grad_hidden
  237.4 4.1 convolution_convert_fusion.grad_t
  241.6 19.3 %attention_backward.1 = (bf16[896,512]{1,0:T(8,128)(2,1)}, f32[256,512]{1,0:T(8,128)}, f32[256,512]{1,0:T(8,128)}) custom-call(s32[1]{0:T(128)} %bitcast.half_ref, s32[1,1024]{1,0:T(1,128)} %doc_row.3, s32[1024,1]{1,0:T(8,128)} %copy.38.doc_col, bf16[896,512]{1,0:T(8,128)(2,1)} %bitcast.88, bf16[256,512]{1,0:T(8,128)(2,1)} %pad_maximum_fusion.2.own, ...), custom_call_target="tpu_custom_call" | custom-call | flops 35000000512 | bytes 3670016 | tf_op jit(solution)/shard_map/attention_backward/pallas_call | solution.py:208
  260.9 11.0 %collective-permute-start.32 = (f32[256,512]{1,0:T(8,128)}, f32[256,512]{1,0:T(8,128)S(1)}, u32[]{:S(2)}, u32[]{:S(2)}) collective-permute-start(f32[256,512]{1,0:T(8,128)} %get-tuple-element.118), channel_id=1, source_target_pairs={{0,4},{4,0},{1,5},{5,1},{2,6},{6,2},{3,7},{7,3},{8,12},{12,8},{9,1... | collective-permute-start | bytes 1572872 | tf_op jit(solution)/shard_map/ppermute | solution.py:258
  271.9 22.7 %weight_gradients.1 = (bf16[4,3,112,1216]{3,2,1,0:T(8,128)(2,1)}, bf16[4,3,112,1216]{3,2,1,0:T(8,128)(2,1)}) custom-call(s32[3]{0:T(128)} %pad_add_fusion.place, bf16[2,896,2048]{2,1,0:T(8,128)(2,1)} %get-tuple-element.122.left, bf16[3,2048,1216]{2,1,0:T(8,128)(2,1)} %get-tuple-element.123.right), custom_call_target="tpu_custom_call" | custom-call | flops 13388218368 | bytes 25952256 | tf_op jit(solution)/shard_map/weight_gradients/pallas_call | solution.py:653
  296.0 11.6 %projection_gradients.1 = (bf16[512,896]{1,0:T(8,128)(2,1)}, bf16[4,128,2048]{2,1,0:T(8,128)(2,1)}, bf16[4,128,2048]{2,1,0:T(8,128)(2,1)}) custom-call(s32[3]{0:T(128)} %pad_add_fusion.place, bf16[896,512]{1,0:T(8,128)(2,1)} %get-tuple-element.116.grad_query, f32[256,512]{1,0:T(8,128)} %get-tuple-element.117.own_sums, f32[256,512]{1,0:T(8,128)} %copy-done.28, ...), custom_call_target="tpu_custom_call" | custom-call | flops 6000000000 | bytes 16000000 | tf_op jit(solution)/shard_map/projection_gradients/pallas_call | solution.py:540
  310.0 1.6 collective-permute-start.31
  312.1 3.2 convert_add_fusion
  316.6 2.9 add_convert_fusion
  320.6 10.8 %collective-permute-done.29 = bf16[512,896]{1,0:T(8,128)(2,1)S(1)} collective-permute-done((bf16[512,896]{1,0:T(8,128)(2,1)}, bf16[512,896]{1,0:T(8,128)(2,1)S(1)}, u32[]{:S(2)}, u32[]{:S(2)}) %collective-permute-start.29) | collective-permute-done | bytes 917536 | tf_op jit(solution)/shard_map/ppermute | solution.py:261
  331.5 1.4 collective-permute-start.36
  333.1 18.6 %collective-permute-done.30 = bf16[512,896]{1,0:T(8,128)(2,1)S(1)} collective-permute-done((bf16[512,896]{1,0:T(8,128)(2,1)S(1)}, bf16[512,896]{1,0:T(8,128)(2,1)S(1)}, u32[]{:S(2)}, u32[]{:S(2)}) %collective-permute-start.30) | collective-permute-done | bytes 917536 | tf_op jit(solution)/shard_map/ppermute | solution.py:261
  351.6 1.3 collective-permute-start.44
  353.0 2.7 collective-permute-start.45
  355.6 6.8 %collective-permute-done.34 = bf16[4,32,2048]{2,1,0:T(8,128)(2,1)S(1)} collective-permute-done((bf16[4,32,2048]{2,1,0:T(8,128)(2,1)S(1)}, bf16[4,32,2048]{2,1,0:T(8,128)(2,1)S(1)}, u32[]{:S(2)}, u32[]{:S(2)}) %collective-permute-start.34) | collective-permute-done | bytes 524320 | tf_op jit(solution)/shard_map/ppermute | solution.py:261
  363.5 1.5 add_convert_fusion.1
  365.0 8.6 %collective-permute-done.36 = bf16[4,32,2048]{2,1,0:T(8,128)(2,1)S(1)} collective-permute-done((bf16[4,32,2048]{2,1,0:T(8,128)(2,1)S(1)}, bf16[4,32,2048]{2,1,0:T(8,128)(2,1)S(1)}, u32[]{:S(2)}, u32[]{:S(2)}) %collective-permute-start.36) | collective-permute-done | bytes 524320 | tf_op jit(solution)/shard_map/ppermute | solution.py:261
  373.9 1.2 collective-permute-start.37
  375.1 1.4 collective-permute-start.38
  376.5 27.2 %collective-permute-done.44 = bf16[3,112,1216]{2,1,0:T(8,128)(2,1)S(1)} collective-permute-done((bf16[3,112,1216]{2,1,0:T(8,128)(2,1)S(1)}, bf16[3,112,1216]{2,1,0:T(8,128)(2,1)S(1)}, u32[]{:S(2)}, u32[]{:S(2)}) %collective-permute-start.44) | collective-permute-done | bytes 817184 | tf_op jit(solution)/shard_map/ppermute | solution.py:264
  403.7 5.8 %collective-permute-done.46 = bf16[3,112,1216]{2,1,0:T(8,128)(2,1)S(1)} collective-permute-done((bf16[3,112,1216]{2,1,0:T(8,128)(2,1)S(1)}, bf16[3,112,1216]{2,1,0:T(8,128)(2,1)S(1)}, u32[]{:S(2)}, u32[]{:S(2)}) %collective-permute-start.46) | collective-permute-done | bytes 817184 | tf_op jit(solution)/shard_map/ppermute | solution.py:264
  409.9 10.1 %collective-permute-done.38 = bf16[32,2048]{1,0:T(8,128)(2,1)S(1)} collective-permute-done((bf16[32,2048]{1,0:T(8,128)(2,1)S(1)}, bf16[32,2048]{1,0:T(8,128)(2,1)S(1)}, u32[]{:S(2)}, u32[]{:S(2)}) %collective-permute-start.38) | collective-permute-done | bytes 131104 | tf_op jit(solution)/shard_map/ppermute | solution.py:264
  420.0 1.4 collective-permute-start.40
  421.4 1.3 collective-permute-start.41
  423.6 1.2 slice_bitcast_fusion
  424.8 1.3 collective-permute-done.40
  426.0 1.3 collective-permute-done.41
  (166 shorter events, 36.2 us)
Async XLA Ops:
  0.6 24.6 %copy-start.6 = (bf16[512,896]{1,0:T(8,128)(2,1)S(1)}, bf16[512,896]{1,0:T(8,128)(2,1)}, u32[]{:S(2)}) copy-start(bf16[512,896]{1,0:T(8,128)(2,1)} %tokens.1) | copy-start | bytes 2752516
  5.2 35.1 %copy-start.26 = (s32[1,1024]{1,0:T(1,128)S(1)}, s32[1,1024]{1,0:T(1,128)}, u32[]{:S(2)}) copy-start(s32[1,1024]{1,0:T(1,128)} %doc_row.3) | copy-start | bytes 12292
  5.6 37.5 %copy-start.3 = (bf16[128,2048]{1,0:T(8,128)(2,1)}, bf16[128,2048]{1,0:T(8,128)(2,1)S(1)}, u32[]{:S(2)}) copy-start(bf16[128,2048]{1,0:T(8,128)(2,1)S(1)} %concatenate.25.refs_0_) | copy-start | bytes 1572868
  5.7 8.2 %collective-permute-start = (bf16[32,2048]{1,0:T(8,128)(2,1)S(1)}, bf16[32,2048]{1,0:T(8,128)(2,1)S(1)}, u32[]{:S(2)}, u32[]{:S(2)}) collective-permute-start(bf16[32,2048]{1,0:T(8,128)(2,1)S(1)} %constant_dynamic-slice_fusion.4), channel_id=1, source_target_pairs={{0,8},{8,0},{16,24},{24,16},{1,9},{9,1},{17,25},{25,17},{2,10},{10... | collective-permute-start | bytes 393224 | tf_op jit(solution)/shard_map/ppermute | solution.py:264
  8.8 12.9 %collective-permute-start.1 = (bf16[32,2048]{1,0:T(8,128)(2,1)S(1)}, bf16[32,2048]{1,0:T(8,128)(2,1)S(1)}, u32[]{:S(2)}, u32[]{:S(2)}) collective-permute-start(bf16[32,2048]{1,0:T(8,128)(2,1)S(1)} %constant_dynamic-slice_fusion.4), channel_id=1, source_target_pairs={{0,16},{8,24},{16,0},{24,8},{1,17},{9,25},{17,1},{25,9},{2,18},{10... | collective-permute-start | bytes 393224 | tf_op jit(solution)/shard_map/ppermute | solution.py:264
  11.4 10.3 %collective-permute-start.2 = (bf16[32,2048]{1,0:T(8,128)(2,1)S(1)}, bf16[32,2048]{1,0:T(8,128)(2,1)S(1)}, u32[]{:S(2)}, u32[]{:S(2)}) collective-permute-start(bf16[32,2048]{1,0:T(8,128)(2,1)S(1)} %constant_dynamic-slice_fusion.4), channel_id=1, source_target_pairs={{0,24},{8,16},{16,8},{24,0},{1,25},{9,17},{17,9},{25,1},{2,26},{10... | collective-permute-start | bytes 393224 | tf_op jit(solution)/shard_map/ppermute | solution.py:264
  11.4 36.4 %collective-permute-start.6 = (bf16[128,2048]{1,0:T(8,128)(2,1)S(1)}, bf16[128,2048]{1,0:T(8,128)(2,1)}, u32[]{:S(2)}, u32[]{:S(2)}) collective-permute-start(bf16[128,2048]{1,0:T(8,128)(2,1)S(1)} %concatenate.25.refs_0_), channel_id=1, source_target_pairs={{0,4},{4,0},{1,5},{5,1},{2,6},{6,2},{3,7},{7,3},{8,12},{12,8},{9,1... | collective-permute-start | bytes 1572872 | tf_op jit(solution)/shard_map/ppermute | solution.py:258
  21.7 28.4 %copy-start.14 = (bf16[96,2048]{1,0:T(8,128)(2,1)}, bf16[96,2048]{1,0:T(8,128)(2,1)S(1)}, u32[]{:S(2)}) copy-start(bf16[96,2048]{1,0:T(8,128)(2,1)S(1)} %constant_dynamic-update-slice_fusion.refs_1_) | copy-start | bytes 1179652
  21.7 13.0 %collective-permute-start.5 = (bf16[96,2048]{1,0:T(8,128)(2,1)S(1)}, bf16[96,2048]{1,0:T(8,128)(2,1)S(1)}, u32[]{:S(2)}, u32[]{:S(2)}) collective-permute-start(bf16[96,2048]{1,0:T(8,128)(2,1)S(1)} %constant_dynamic-update-slice_fusion.refs_1_), channel_id=1, source_target_pairs={{0,3},{1,2},{2,1},{3,0},{4,7},{5,6},{6,5},{7,4},{8,11},{9,10},{10,... | collective-permute-start | bytes 1179656 | tf_op jit(solution)/shard_map/ppermute | solution.py:261
  24.2 15.5 %collective-permute-start.3 = (bf16[96,2048]{1,0:T(8,128)(2,1)S(1)}, bf16[96,2048]{1,0:T(8,128)(2,1)}, u32[]{:S(2)}, u32[]{:S(2)}) collective-permute-start(bf16[96,2048]{1,0:T(8,128)(2,1)S(1)} %constant_dynamic-update-slice_fusion.refs_1_), channel_id=1, source_target_pairs={{0,1},{1,0},{2,3},{3,2},{4,5},{5,4},{6,7},{7,6},{8,9},{9,8},{10,11... | collective-permute-start | bytes 1179656 | tf_op jit(solution)/shard_map/ppermute | solution.py:261
  24.8 15.0 %collective-permute-start.4 = (bf16[96,2048]{1,0:T(8,128)(2,1)S(1)}, bf16[96,2048]{1,0:T(8,128)(2,1)}, u32[]{:S(2)}, u32[]{:S(2)}) collective-permute-start(bf16[96,2048]{1,0:T(8,128)(2,1)S(1)} %constant_dynamic-update-slice_fusion.refs_1_), channel_id=1, source_target_pairs={{0,2},{1,3},{2,0},{3,1},{4,6},{5,7},{6,4},{7,5},{8,10},{9,11},{10,... | collective-permute-start | bytes 1179656 | tf_op jit(solution)/shard_map/ppermute | solution.py:261
  25.8 37.9 %copy-start.15 = (f32[32,512]{1,0:T(8,128)}, f32[32,512]{1,0:T(8,128)S(1)}, u32[]{:S(2)}) copy-start(f32[32,512]{1,0:T(8,128)S(1)} %get-tuple-element.162.cosine) | copy-start | bytes 196612
  25.9 37.9 %copy-start.16 = (f32[32,512]{1,0:T(8,128)}, f32[32,512]{1,0:T(8,128)S(1)}, u32[]{:S(2)}) copy-start(f32[32,512]{1,0:T(8,128)S(1)} %get-tuple-element.163.sine) | copy-start | bytes 196612
  25.9 17.3 %collective-permute-start.7 = (bf16[96,2048]{1,0:T(8,128)(2,1)S(1)}, bf16[96,2048]{1,0:T(8,128)(2,1)}, u32[]{:S(2)}, u32[]{:S(2)}) collective-permute-start(bf16[96,2048]{1,0:T(8,128)(2,1)S(1)} %constant_dynamic-update-slice_fusion.refs_1_), channel_id=1, source_target_pairs={{0,4},{4,0},{1,5},{5,1},{2,6},{6,2},{3,7},{7,3},{8,12},{12,8},{9,1... | collective-permute-start | bytes 1179656 | tf_op jit(solution)/shard_map/ppermute | solution.py:258
  34.7 15.5 %copy-start.17 = (bf16[96,2048]{1,0:T(8,128)(2,1)}, bf16[96,2048]{1,0:T(8,128)(2,1)S(1)}, u32[]{:S(2)}) copy-start(bf16[96,2048]{1,0:T(8,128)(2,1)S(1)} %collective-permute-done.5.refs_4_) | copy-start | bytes 1179652
  34.7 14.5 %collective-permute-start.10 = (bf16[96,2048]{1,0:T(8,128)(2,1)S(1)}, bf16[96,2048]{1,0:T(8,128)(2,1)}, u32[]{:S(2)}, u32[]{:S(2)}) collective-permute-start(bf16[96,2048]{1,0:T(8,128)(2,1)S(1)} %collective-permute-done.5.refs_4_), channel_id=1, source_target_pairs={{0,4},{4,0},{1,5},{5,1},{2,6},{6,2},{3,7},{7,3},{8,12},{12,8},{9,1... | collective-permute-start | bytes 1179656 | tf_op jit(solution)/shard_map/ppermute | solution.py:258
  39.7 10.4 %collective-permute-start.8 = (bf16[96,2048]{1,0:T(8,128)(2,1)}, bf16[96,2048]{1,0:T(8,128)(2,1)}, u32[]{:S(2)}, u32[]{:S(2)}) collective-permute-start(bf16[96,2048]{1,0:T(8,128)(2,1)} %collective-permute-done.3.refs_2_), channel_id=1, source_target_pairs={{0,4},{4,0},{1,5},{5,1},{2,6},{6,2},{3,7},{7,3},{8,12},{12,8},{9,1... | collective-permute-start | bytes 1179656 | tf_op jit(solution)/shard_map/ppermute | solution.py:258
  39.8 10.4 %collective-permute-start.9 = (bf16[96,2048]{1,0:T(8,128)(2,1)}, bf16[96,2048]{1,0:T(8,128)(2,1)}, u32[]{:S(2)}, u32[]{:S(2)}) collective-permute-start(bf16[96,2048]{1,0:T(8,128)(2,1)} %collective-permute-done.4.refs_3_), channel_id=1, source_target_pairs={{0,4},{4,0},{1,5},{5,1},{2,6},{6,2},{3,7},{7,3},{8,12},{12,8},{9,1... | collective-permute-start | bytes 1179656 | tf_op jit(solution)/shard_map/ppermute | solution.py:258
  40.3 19.4 %copy-start.24 = (f32[512]{0:T(512)}, f32[512]{0:T(512)S(1)}, u32[]{:S(2)}) copy-start(f32[512]{0:T(512)S(1)} %add_rsqrt_fusion.1) | copy-start | bytes 6148
  43.1 85.9 %copy-start.1 = (bf16[336,1216]{1,0:T(8,128)(2,1)}, bf16[336,1216]{1,0:T(8,128)(2,1)S(1)}, u32[]{:S(2)}) copy-start(bf16[336,1216]{1,0:T(8,128)(2,1)S(1)} %pad_maximum_fusion.refs_0_) | copy-start | bytes 2451460
  43.1 16.5 %copy-start.7 = (bf16[512,896]{1,0:T(8,128)(2,1)S(1)}, bf16[512,896]{1,0:T(8,128)(2,1)}, u32[]{:S(2)}) copy-start(bf16[512,896]{1,0:T(8,128)(2,1)} %tokens.1) | copy-start | bytes 2752516
  43.1 42.4 %collective-permute-start.13 = (bf16[336,1216]{1,0:T(8,128)(2,1)S(1)}, bf16[336,1216]{1,0:T(8,128)(2,1)}, u32[]{:S(2)}, u32[]{:S(2)}) collective-permute-start(bf16[336,1216]{1,0:T(8,128)(2,1)S(1)} %pad_maximum_fusion.refs_0_), channel_id=1, source_target_pairs={{0,16},{8,24},{16,0},{24,8},{1,17},{9,25},{17,1},{25,9},{2,18},{10... | collective-permute-start | bytes 2451464 | tf_op jit(solution)/shard_map/ppermute | solution.py:264
  47.7 85.4 %collective-permute-start.22 = (bf16[512,896]{1,0:T(8,128)(2,1)}, bf16[512,896]{1,0:T(8,128)(2,1)}, u32[]{:S(2)}, u32[]{:S(2)}) collective-permute-start(bf16[512,896]{1,0:T(8,128)(2,1)} %g_ref), channel_id=1, source_target_pairs={{0,1},{1,0},{2,3},{3,2},{4,5},{5,4},{6,7},{7,6},{8,9},{9,8},{10,11... | collective-permute-start | bytes 2752520 | tf_op jit(solution)/shard_map/ppermute | solution.py:261
  49.2 84.0 %collective-permute-start.23 = (bf16[512,896]{1,0:T(8,128)(2,1)}, bf16[512,896]{1,0:T(8,128)(2,1)}, u32[]{:S(2)}, u32[]{:S(2)}) collective-permute-start(bf16[512,896]{1,0:T(8,128)(2,1)} %g_ref), channel_id=1, source_target_pairs={{0,2},{1,3},{2,0},{3,1},{4,6},{5,7},{6,4},{7,5},{8,10},{9,11},{10,... | collective-permute-start | bytes 2752520 | tf_op jit(solution)/shard_map/ppermute | solution.py:261
  63.8 23.8 %collective-permute-start.11 = (bf16[256,512]{1,0:T(8,128)(2,1)}, bf16[256,512]{1,0:T(8,128)(2,1)}, u32[]{:S(2)}, u32[]{:S(2)}) collective-permute-start(bf16[256,512]{1,0:T(8,128)(2,1)} %pad_maximum_fusion.2.own), channel_id=1, source_target_pairs={{0,4},{4,0},{1,5},{5,1},{2,6},{6,2},{3,7},{7,3},{8,12},{12,8},{9,1... | collective-permute-start | bytes 786440 | tf_op jit(solution)/shard_map/ppermute | solution.py:258
  85.6 24.1 %collective-permute-start.14 = (bf16[336,1216]{1,0:T(8,128)(2,1)S(1)}, bf16[336,1216]{1,0:T(8,128)(2,1)S(1)}, u32[]{:S(2)}, u32[]{:S(2)}) collective-permute-start(bf16[336,1216]{1,0:T(8,128)(2,1)S(1)} %pad_maximum_fusion.refs_0_), channel_id=1, source_target_pairs={{8,16},{16,8},{9,17},{17,9},{10,18},{18,10},{11,19},{19,11},{12,20... | collective-permute-start | bytes 2451464 | tf_op jit(solution)/shard_map/ppermute | solution.py:289
  86.3 27.0 %collective-permute-start.15 = (bf16[336,1216]{1,0:T(8,128)(2,1)}, bf16[336,1216]{1,0:T(8,128)(2,1)}, u32[]{:S(2)}, u32[]{:S(2)}) collective-permute-start(bf16[336,1216]{1,0:T(8,128)(2,1)} %collective-permute-done.13.refs_2_), channel_id=1, source_target_pairs={{16,24},{8,0},{17,25},{9,1},{18,26},{10,2},{19,27},{11,3},{20,28},... | collective-permute-start | bytes 2451464 | tf_op jit(solution)/shard_map/ppermute | solution.py:290
  108.1 25.5 %collective-permute-start.20 = (bf16[512,896]{1,0:T(8,128)(2,1)}, bf16[512,896]{1,0:T(8,128)(2,1)}, u32[]{:S(2)}, u32[]{:S(2)}) collective-permute-start(bf16[512,896]{1,0:T(8,128)(2,1)} %multiply_convert_fusion.x_ref), channel_id=1, source_target_pairs={{0,1},{1,0},{2,3},{3,2},{4,5},{5,4},{6,7},{7,6},{8,9},{9,8},{10,11... | collective-permute-start | bytes 2752520 | tf_op jit(solution)/shard_map/ppermute | solution.py:261
  109.6 19.4 %collective-permute-start.12 = (bf16[336,1216]{1,0:T(8,128)(2,1)S(1)}, bf16[336,1216]{1,0:T(8,128)(2,1)}, u32[]{:S(2)}, u32[]{:S(2)}) collective-permute-start(bf16[336,1216]{1,0:T(8,128)(2,1)S(1)} %pad_maximum_fusion.refs_0_), channel_id=1, source_target_pairs={{0,8},{8,0},{16,24},{24,16},{1,9},{9,1},{17,25},{25,17},{2,10},{10... | collective-permute-start | bytes 2451464 | tf_op jit(solution)/shard_map/ppermute | solution.py:264
  113.2 20.5 %collective-permute-start.21 = (bf16[512,896]{1,0:T(8,128)(2,1)}, bf16[512,896]{1,0:T(8,128)(2,1)S(1)}, u32[]{:S(2)}, u32[]{:S(2)}) collective-permute-start(bf16[512,896]{1,0:T(8,128)(2,1)} %multiply_convert_fusion.x_ref), channel_id=1, source_target_pairs={{0,2},{1,3},{2,0},{3,1},{4,6},{5,7},{6,4},{7,5},{8,10},{9,11},{10,... | collective-permute-start | bytes 2752520 | tf_op jit(solution)/shard_map/ppermute | solution.py:261
  115.9 23.1 %copy-start.2 = (bf16[336,1216]{1,0:T(8,128)(2,1)}, bf16[336,1216]{1,0:T(8,128)(2,1)S(1)}, u32[]{:S(2)}) copy-start(bf16[336,1216]{1,0:T(8,128)(2,1)S(1)} %broadcast_select_fusion.refs_3_) | copy-start | bytes 2451460
  129.0 6.1 %collective-permute-start.16 = (bf16[336,1216]{1,0:T(8,128)(2,1)S(1)}, bf16[336,1216]{1,0:T(8,128)(2,1)S(1)}, u32[]{:S(2)}, u32[]{:S(2)}) collective-permute-start(bf16[336,1216]{1,0:T(8,128)(2,1)S(1)} %pad_maximum_fusion.refs_0_), channel_id=1, source_target_pairs={{0,4},{4,0},{1,5},{5,1},{2,6},{6,2},{3,7},{7,3},{8,12},{12,8},{9,1... | collective-permute-start | bytes 2451464 | tf_op jit(solution)/shard_map/ppermute | solution.py:258
  133.1 3.6 collective-permute-start.18
  133.2 4.5 %collective-permute-start.17 = (bf16[336,1216]{1,0:T(8,128)(2,1)}, bf16[336,1216]{1,0:T(8,128)(2,1)S(1)}, u32[]{:S(2)}, u32[]{:S(2)}) collective-permute-start(bf16[336,1216]{1,0:T(8,128)(2,1)} %collective-permute-done.12.refs_1_), channel_id=1, source_target_pairs={{0,4},{4,0},{1,5},{5,1},{2,6},{6,2},{3,7},{7,3},{8,12},{12,8},{9,1... | collective-permute-start | bytes 2451464 | tf_op jit(solution)/shard_map/ppermute | solution.py:258
  133.7 5.3 %collective-permute-start.19 = (bf16[336,1216]{1,0:T(8,128)(2,1)S(1)}, bf16[336,1216]{1,0:T(8,128)(2,1)}, u32[]{:S(2)}, u32[]{:S(2)}) collective-permute-start(bf16[336,1216]{1,0:T(8,128)(2,1)S(1)} %broadcast_select_fusion.refs_3_), channel_id=1, source_target_pairs={{0,4},{4,0},{1,5},{5,1},{2,6},{6,2},{3,7},{7,3},{8,12},{12,8},{9,1... | collective-permute-start | bytes 2451464 | tf_op jit(solution)/shard_map/ppermute | solution.py:258
  133.7 56.9 %collective-permute-start.25 = (bf16[512,896]{1,0:T(8,128)(2,1)}, bf16[512,896]{1,0:T(8,128)(2,1)}, u32[]{:S(2)}, u32[]{:S(2)}) collective-permute-start(bf16[512,896]{1,0:T(8,128)(2,1)} %g_ref), channel_id=1, source_target_pairs={{0,3},{1,2},{2,1},{3,0},{4,7},{5,6},{6,5},{7,4},{8,11},{9,10},{10,... | collective-permute-start | bytes 2752520 | tf_op jit(solution)/shard_map/ppermute | solution.py:261
  135.2 55.5 %collective-permute-start.24 = (bf16[512,896]{1,0:T(8,128)(2,1)}, bf16[512,896]{1,0:T(8,128)(2,1)}, u32[]{:S(2)}, u32[]{:S(2)}) collective-permute-start(bf16[512,896]{1,0:T(8,128)(2,1)} %multiply_convert_fusion.x_ref), channel_id=1, source_target_pairs={{0,3},{1,2},{2,1},{3,0},{4,7},{5,6},{6,5},{7,4},{8,11},{9,10},{10,... | collective-permute-start | bytes 2752520 | tf_op jit(solution)/shard_map/ppermute | solution.py:261
  188.7 22.7 %collective-permute-start.27 = (bf16[512,896]{1,0:T(8,128)(2,1)}, bf16[512,896]{1,0:T(8,128)(2,1)}, u32[]{:S(2)}, u32[]{:S(2)}) collective-permute-start(bf16[512,896]{1,0:T(8,128)(2,1)} %get-tuple-element.106), channel_id=1, source_target_pairs={{0,2},{1,3},{2,0},{3,1},{4,6},{5,7},{6,4},{7,5},{8,10},{9,11},{10,... | collective-permute-start | bytes 2752520 | tf_op jit(solution)/shard_map/ppermute | solution.py:261
  190.1 23.0 %collective-permute-start.26 = (bf16[512,896]{1,0:T(8,128)(2,1)}, bf16[512,896]{1,0:T(8,128)(2,1)}, u32[]{:S(2)}, u32[]{:S(2)}) collective-permute-start(bf16[512,896]{1,0:T(8,128)(2,1)} %get-tuple-element.105), channel_id=1, source_target_pairs={{0,1},{1,0},{2,3},{3,2},{4,5},{5,4},{6,7},{7,6},{8,9},{9,8},{10,11... | collective-permute-start | bytes 2752520 | tf_op jit(solution)/shard_map/ppermute | solution.py:261
  190.7 16.0 %copy-start.25 = (f32[512]{0:T(512)S(1)}, f32[512]{0:T(512)}, u32[]{:S(2)}) copy-start(f32[512]{0:T(512)} %copy-done.24) | copy-start | bytes 6148
  190.7 16.9 %copy-start.22 = (f32[8,1,112]{2,1,0:T(1,128)S(1)}, f32[8,1,112]{2,1,0:T(1,128)}, u32[]{:S(2)}) copy-start(f32[8,1,112]{2,1,0:T(1,128)} %get-tuple-element.154) | copy-start | bytes 10756
  190.7 42.2 %copy-start.9 = (bf16[512,896]{1,0:T(8,128)(2,1)S(1)}, bf16[512,896]{1,0:T(8,128)(2,1)}, u32[]{:S(2)}) copy-start(bf16[512,896]{1,0:T(8,128)(2,1)} %get-tuple-element.104) | copy-start | bytes 2752516
  205.1 27.7 %collective-permute-start.28 = (bf16[512,896]{1,0:T(8,128)(2,1)}, bf16[512,896]{1,0:T(8,128)(2,1)}, u32[]{:S(2)}, u32[]{:S(2)}) collective-permute-start(bf16[512,896]{1,0:T(8,128)(2,1)} %get-tuple-element.107), channel_id=1, source_target_pairs={{0,3},{1,2},{2,1},{3,0},{4,7},{5,6},{6,5},{7,4},{8,11},{9,10},{10,... | collective-permute-start | bytes 2752520 | tf_op jit(solution)/shard_map/ppermute | solution.py:261
  260.9 34.3 %collective-permute-start.32 = (f32[256,512]{1,0:T(8,128)}, f32[256,512]{1,0:T(8,128)S(1)}, u32[]{:S(2)}, u32[]{:S(2)}) collective-permute-start(f32[256,512]{1,0:T(8,128)} %get-tuple-element.118), channel_id=1, source_target_pairs={{0,4},{4,0},{1,5},{5,1},{2,6},{6,2},{3,7},{7,3},{8,12},{12,8},{9,1... | collective-permute-start | bytes 1572872 | tf_op jit(solution)/shard_map/ppermute | solution.py:258
  294.6 22.0 %collective-permute-start.43 = (bf16[4,3,112,1216]{3,2,1,0:T(8,128)(2,1)}, bf16[4,3,112,1216]{3,2,1,0:T(8,128)(2,1)}, u32[]{:S(2)}, u32[]{:S(2)}) collective-permute-start(bf16[4,3,112,1216]{3,2,1,0:T(8,128)(2,1)} %get-tuple-element.125), channel_id=1, source_target_pairs={{0,4},{4,0},{1,5},{5,1},{2,6},{6,2},{3,7},{7,3},{8,12},{12,8},{9,1... | collective-permute-start | bytes 9805832 | tf_op jit(solution)/shard_map/ppermute | solution.py:258
  296.0 12.9 %copy-start.27 = (bf16[512,896]{1,0:T(8,128)(2,1)S(1)}, bf16[512,896]{1,0:T(8,128)(2,1)}, u32[]{:S(2)}) copy-start(bf16[512,896]{1,0:T(8,128)(2,1)} %get-tuple-element.114) | copy-start | bytes 2752516
  307.5 4.6 %collective-permute-start.33 = (bf16[4,128,2048]{2,1,0:T(8,128)(2,1)}, bf16[4,128,2048]{2,1,0:T(8,128)(2,1)}, u32[]{:S(2)}, u32[]{:S(2)}) collective-permute-start(bf16[4,128,2048]{2,1,0:T(8,128)(2,1)} %get-tuple-element.121), channel_id=1, source_target_pairs={{0,4},{4,0},{1,5},{5,1},{2,6},{6,2},{3,7},{7,3},{8,12},{12,8},{9,1... | collective-permute-start | bytes 6291464 | tf_op jit(solution)/shard_map/ppermute | solution.py:258
  308.0 23.4 %collective-permute-start.29 = (bf16[512,896]{1,0:T(8,128)(2,1)}, bf16[512,896]{1,0:T(8,128)(2,1)S(1)}, u32[]{:S(2)}, u32[]{:S(2)}) collective-permute-start(bf16[512,896]{1,0:T(8,128)(2,1)} %get-tuple-element.113), channel_id=1, source_target_pairs={{0,1},{1,0},{2,3},{3,2},{4,5},{5,4},{6,7},{7,6},{8,9},{9,8},{10,11... | collective-permute-start | bytes 2752520 | tf_op jit(solution)/shard_map/ppermute | solution.py:261
  308.9 42.7 %collective-permute-start.30 = (bf16[512,896]{1,0:T(8,128)(2,1)S(1)}, bf16[512,896]{1,0:T(8,128)(2,1)S(1)}, u32[]{:S(2)}, u32[]{:S(2)}) collective-permute-start(bf16[512,896]{1,0:T(8,128)(2,1)S(1)} %copy-done.27), channel_id=1, source_target_pairs={{0,2},{1,3},{2,0},{3,1},{4,6},{5,7},{6,4},{7,5},{8,10},{9,11},{10,... | collective-permute-start | bytes 2752520 | tf_op jit(solution)/shard_map/ppermute | solution.py:261
  310.0 43.0 %collective-permute-start.31 = (bf16[512,896]{1,0:T(8,128)(2,1)}, bf16[512,896]{1,0:T(8,128)(2,1)S(1)}, u32[]{:S(2)}, u32[]{:S(2)}) collective-permute-start(bf16[512,896]{1,0:T(8,128)(2,1)} %get-tuple-element.115), channel_id=1, source_target_pairs={{0,3},{1,2},{2,1},{3,0},{4,7},{5,6},{6,5},{7,4},{8,11},{9,10},{10,... | collective-permute-start | bytes 2752520 | tf_op jit(solution)/shard_map/ppermute | solution.py:261
  312.1 4.4 %copy-start = (bf16[4,3,112,1216]{3,2,1,0:T(8,128)(2,1)S(1)}, bf16[4,3,112,1216]{3,2,1,0:T(8,128)(2,1)}, u32[]{:S(2)}) copy-start(bf16[4,3,112,1216]{3,2,1,0:T(8,128)(2,1)} %get-tuple-element.124) | copy-start | bytes 9805828
  315.6 46.8 %collective-permute-start.34 = (bf16[4,32,2048]{2,1,0:T(8,128)(2,1)S(1)}, bf16[4,32,2048]{2,1,0:T(8,128)(2,1)S(1)}, u32[]{:S(2)}, u32[]{:S(2)}) collective-permute-start(bf16[4,32,2048]{2,1,0:T(8,128)(2,1)S(1)} %get-tuple-element.132), channel_id=1, source_target_pairs={{0,1},{1,0},{2,3},{3,2},{4,5},{5,4},{6,7},{7,6},{8,9},{9,8},{10,11... | collective-permute-start | bytes 1572872 | tf_op jit(solution)/shard_map/ppermute | solution.py:261
  319.5 45.5 %collective-permute-start.35 = (bf16[4,32,2048]{2,1,0:T(8,128)(2,1)S(1)}, bf16[4,32,2048]{2,1,0:T(8,128)(2,1)S(1)}, u32[]{:S(2)}, u32[]{:S(2)}) collective-permute-start(bf16[4,32,2048]{2,1,0:T(8,128)(2,1)S(1)} %get-tuple-element.133), channel_id=1, source_target_pairs={{0,2},{1,3},{2,0},{3,1},{4,6},{5,7},{6,4},{7,5},{8,10},{9,11},{10,... | collective-permute-start | bytes 1572872 | tf_op jit(solution)/shard_map/ppermute | solution.py:261
  331.4 32.0 %copy-start.5 = (bf16[512,896]{1,0:T(8,128)(2,1)S(1)}, bf16[512,896]{1,0:T(8,128)(2,1)}, u32[]{:S(2)}) copy-start(bf16[512,896]{1,0:T(8,128)(2,1)} %get-tuple-element.112) | copy-start | bytes 2752516
  331.5 42.1 %collective-permute-start.36 = (bf16[4,32,2048]{2,1,0:T(8,128)(2,1)S(1)}, bf16[4,32,2048]{2,1,0:T(8,128)(2,1)S(1)}, u32[]{:S(2)}, u32[]{:S(2)}) collective-permute-start(bf16[4,32,2048]{2,1,0:T(8,128)(2,1)S(1)} %get-tuple-element.134), channel_id=1, source_target_pairs={{0,3},{1,2},{2,1},{3,0},{4,7},{5,6},{6,5},{7,4},{8,11},{9,10},{10,... | collective-permute-start | bytes 1572872 | tf_op jit(solution)/shard_map/ppermute | solution.py:261
  351.6 52.1 %collective-permute-start.44 = (bf16[3,112,1216]{2,1,0:T(8,128)(2,1)S(1)}, bf16[3,112,1216]{2,1,0:T(8,128)(2,1)S(1)}, u32[]{:S(2)}, u32[]{:S(2)}) collective-permute-start(bf16[3,112,1216]{2,1,0:T(8,128)(2,1)S(1)} %get-tuple-element.135), channel_id=1, source_target_pairs={{0,16},{8,24},{16,0},{24,8},{1,17},{9,25},{17,1},{25,9},{2,18},{10... | collective-permute-start | bytes 2451464 | tf_op jit(solution)/shard_map/ppermute | solution.py:264
  353.0 50.7 %collective-permute-start.45 = (bf16[3,112,1216]{2,1,0:T(8,128)(2,1)S(1)}, bf16[3,112,1216]{2,1,0:T(8,128)(2,1)S(1)}, u32[]{:S(2)}, u32[]{:S(2)}) collective-permute-start(bf16[3,112,1216]{2,1,0:T(8,128)(2,1)S(1)} %get-tuple-element.137), channel_id=1, source_target_pairs={{0,24},{8,16},{16,8},{24,0},{1,25},{9,17},{17,9},{25,1},{2,26},{10... | collective-permute-start | bytes 2451464 | tf_op jit(solution)/shard_map/ppermute | solution.py:264
  362.4 47.1 %collective-permute-start.46 = (bf16[3,112,1216]{2,1,0:T(8,128)(2,1)S(1)}, bf16[3,112,1216]{2,1,0:T(8,128)(2,1)S(1)}, u32[]{:S(2)}, u32[]{:S(2)}) collective-permute-start(bf16[3,112,1216]{2,1,0:T(8,128)(2,1)S(1)} %get-tuple-element.136), channel_id=1, source_target_pairs={{0,8},{8,0},{16,24},{24,16},{1,9},{9,1},{17,25},{25,17},{2,10},{10... | collective-permute-start | bytes 2451464 | tf_op jit(solution)/shard_map/ppermute | solution.py:264
  373.9 36.0 %collective-permute-start.37 = (bf16[32,2048]{1,0:T(8,128)(2,1)S(1)}, bf16[32,2048]{1,0:T(8,128)(2,1)S(1)}, u32[]{:S(2)}, u32[]{:S(2)}) collective-permute-start(bf16[32,2048]{1,0:T(8,128)(2,1)S(1)} %get-tuple-element.145), channel_id=1, source_target_pairs={{0,24},{8,16},{16,8},{24,0},{1,25},{9,17},{17,9},{25,1},{2,26},{10... | collective-permute-start | bytes 393224 | tf_op jit(solution)/shard_map/ppermute | solution.py:264
  375.1 44.8 %collective-permute-start.38 = (bf16[32,2048]{1,0:T(8,128)(2,1)S(1)}, bf16[32,2048]{1,0:T(8,128)(2,1)S(1)}, u32[]{:S(2)}, u32[]{:S(2)}) collective-permute-start(bf16[32,2048]{1,0:T(8,128)(2,1)S(1)} %get-tuple-element.147), channel_id=1, source_target_pairs={{0,16},{8,24},{16,0},{24,8},{1,17},{9,25},{17,1},{25,9},{2,18},{10... | collective-permute-start | bytes 393224 | tf_op jit(solution)/shard_map/ppermute | solution.py:264
  403.7 16.3 %collective-permute-start.39 = (bf16[32,2048]{1,0:T(8,128)(2,1)S(1)}, bf16[32,2048]{1,0:T(8,128)(2,1)S(1)}, u32[]{:S(2)}, u32[]{:S(2)}) collective-permute-start(bf16[32,2048]{1,0:T(8,128)(2,1)S(1)} %get-tuple-element.146), channel_id=1, source_target_pairs={{0,8},{8,0},{16,24},{24,16},{1,9},{9,1},{17,25},{25,17},{2,10},{10... | collective-permute-start | bytes 393224 | tf_op jit(solution)/shard_map/ppermute | solution.py:264
  420.0 6.0 %collective-permute-start.40 = (bf16[32,2048]{1,0:T(8,128)(2,1)S(1)}, bf16[32,2048]{1,0:T(8,128)(2,1)S(1)}, u32[]{:S(2)}, u32[]{:S(2)}) collective-permute-start(bf16[32,2048]{1,0:T(8,128)(2,1)S(1)} %fusion.19), channel_id=1, source_target_pairs={{0,3},{1,2},{2,1},{3,0},{4,7},{5,6},{6,5},{7,4},{8,11},{9,10},{10,... | collective-permute-start | bytes 393224 | tf_op jit(solution)/shard_map/ppermute | solution.py:261
  421.4 5.9 %collective-permute-start.41 = (bf16[32,2048]{1,0:T(8,128)(2,1)S(1)}, bf16[32,2048]{1,0:T(8,128)(2,1)S(1)}, u32[]{:S(2)}, u32[]{:S(2)}) collective-permute-start(bf16[32,2048]{1,0:T(8,128)(2,1)S(1)} %fusion.19), channel_id=1, source_target_pairs={{0,2},{1,3},{2,0},{3,1},{4,6},{5,7},{6,4},{7,5},{8,10},{9,11},{10,... | collective-permute-start | bytes 393224 | tf_op jit(solution)/shard_map/ppermute | solution.py:261
  422.7 5.0 %collective-permute-start.42 = (bf16[32,2048]{1,0:T(8,128)(2,1)S(1)}, bf16[32,2048]{1,0:T(8,128)(2,1)S(1)}, u32[]{:S(2)}, u32[]{:S(2)}) collective-permute-start(bf16[32,2048]{1,0:T(8,128)(2,1)S(1)} %fusion.19), channel_id=1, source_target_pairs={{0,1},{1,0},{2,3},{3,2},{4,5},{5,4},{6,7},{7,6},{8,9},{9,8},{10,11... | collective-permute-start | bytes 393224 | tf_op jit(solution)/shard_map/ppermute | solution.py:261
  (12 other events, 25.0 us)
